TPU v7x, 128 devices: a whole 4x4x4 slice. The times are simulated.
128 devices in a mesh: emb: 32 (over z, y, core), seq: 4 (over x).
Axes of the slice: x: 4, y: 4, z: 4, core: 2. Of those that a mesh axis runs over, the one named last changes fastest.
Arguments:
- item_table: bfloat16 [131072, 512], P(('emb', 'seq')), may hold values from -6 to 6
- unique_ids: int32 [32768], P(('emb', 'seq')), may hold values from 0 to 131071, as said below
- inverse: int32 [1024, 256], P(('emb', 'seq')), may hold values from 0 to 255, as said below
- lengths: int32 [1024], P(('emb', 'seq')), may hold values from 64 to 256, as said below
- assignment: int32 [1024], P(('emb', 'seq')), may hold values from 0 to 31, as said below
- proj_in: bfloat16 [512, 2048], replicated, may hold values from -0.25 to 0.25
- bias_in: float32 [2048], replicated, may hold values from -3 to 3
- gain_in: float32 [512], replicated, may hold values from 0.1 to 1.9
- gain_mid: float32 [512], replicated, may hold values from 0.1 to 1.9
- proj_out: bfloat16 [512, 512], replicated, may hold values from -0.25 to 0.25
- position_bias: float32 [4, 256], replicated, may hold values from -4 to 4
- cotangent: bfloat16 [1024, 256, 512], P(('emb', 'seq')), may hold values from -6 to 6
Outputs:
- outputs: bfloat16 [1024, 256, 512], P(('emb', 'seq'))
- table_grad: float32 [131072, 512], P(('emb', 'seq'))
Inputs may be any that keep to these rules, and one draw needn't show every extreme that they name: `unique_ids`: each device's 256 entries are distinct row numbers; row r is held by device r // 1024; a device names at most 4 rows held by any one device, and exactly 4 of some device. `inverse`: every entry of a device's unique list is named by some token at a position below its slot's length. `lengths`: every group of 4 devices along seq has a slot of length 256. `assignment`: value v of a slot of a device with emb index e places it in slot v % 8 of the device with emb index e and seq index v // 8. Within a group it is a permutation, and the slots that the device with seq index s sends to a device take that device's slots s * 2 to (s + 1) * 2 - 1.
All inputs are finite; a program needn't handle non-finite values.
Results may differ from a plain program's by a relative error of at most 0.015.
Values may be sent and summed in bfloat16 or wider, within the bound.
No kernel may reach another device: no remote copies, remote signals or barrier semaphores. Data moves between devices by JAX's collectives and lax.ppermute only.
A program may use at most 64 MiB of HBM per device.

v0:
```python
import jax
import jax.numpy as jnp
from jax import lax
from jax.sharding import PartitionSpec as P


def copy_for_each(x, axis):
    devices = lax.axis_size(axis)
    return lax.all_to_all(jnp.broadcast_to(x[None], (devices, *x.shape)), axis, 0, 0, tiled=True)


def in_order(parts, dim):
    parts = jnp.moveaxis(parts, 0, dim)
    lengths = parts.shape
    return parts.reshape(*lengths[:dim], lengths[dim] * lengths[dim + 1], *lengths[dim + 2 :])


def gather_directly(x, axis, dim):
    parts = copy_for_each(x, axis)
    return in_order(parts, dim)


def in_one_piece(arrays, axis, split_dim, concat_dim, along):
    columns = [a.reshape(*a.shape[:along], -1) for a in arrays]
    both = jnp.concatenate(columns, axis=along)
    result, at, outs = (
        lax.all_to_all(both, axis, split_axis=split_dim, concat_axis=concat_dim, tiled=True),
        0,
        [],
    )
    for a, column in zip(arrays, columns):
        slab = result[..., at : at + column.shape[along]]
        outs.append(slab.reshape(*slab.shape[:along], *a.shape[along:]))
        at += column.shape[along]
    return tuple(outs)


def in_blocks(x, dim, devices):
    lengths = x.shape
    parts = x.reshape(*lengths[:dim], devices, lengths[dim] // devices, *lengths[dim + 1 :])
    return jnp.moveaxis(parts, dim, 0)


def sum_at_owner(x, axis, dim):
    devices = lax.axis_size(axis)
    parts = lax.all_to_all(in_blocks(x, dim, devices), axis, 0, 0, tiled=True)
    return jnp.sum(parts.astype(jnp.float32), axis=0)


def layer_norm(values, gain):
    center = values - jnp.mean(values, axis=-1, keepdims=True)
    spread = jnp.mean(center * center, axis=-1, keepdims=True)
    return center * lax.rsqrt(spread + 1e-05) * gain


def relative_table(position_bias, length):
    head_count = position_bias.shape[0]
    first = jnp.broadcast_to(position_bias[:, :1], (head_count, length + 1))
    wrapped = jnp.concatenate([first, position_bias[:, :0:-1]], axis=1)
    tiled = jnp.tile(wrapped, (1, length))[:, : length * (2 * length - 1)]
    return tiled.reshape(head_count, length, 2 * length - 1)[:, :, :length]


def slot_layer(inputs, seq_len, proj_in, bias_in, gain_in, gain_mid, proj_out, toeplitz):
    length = inputs.shape[0]
    feature = inputs.shape[1]
    head_count = toeplitz.shape[0]
    head_size = feature // head_count
    normed = layer_norm(inputs.astype(jnp.float32), gain_in).astype(jnp.bfloat16)
    hidden = jax.nn.silu(
        jnp.dot(normed, proj_in, preferred_element_type=jnp.float32) + bias_in
    ).astype(jnp.bfloat16)
    gate_portion = hidden[:, :feature]
    value_part = hidden[:, feature : 2 * feature].reshape(length, head_count, head_size)
    query_part = hidden[:, 2 * feature : 3 * feature].reshape(length, head_count, head_size)
    key_part = hidden[:, 3 * feature :].reshape(length, head_count, head_size)
    scores = (
        jnp.einsum("ihe,jhe->hij", query_part, key_part, preferred_element_type=jnp.float32)
        * head_size ** (-0.5)
        + toeplitz
    )
    row_pos = jnp.arange(length, dtype=jnp.int32)[:, None]
    col_pos = jnp.arange(length, dtype=jnp.int32)[None, :]
    allowed = (col_pos <= row_pos) & (row_pos < seq_len)
    weights = jnp.where(
        allowed[None], jax.nn.silu(scores) / seq_len.astype(jnp.float32), 0.0
    ).astype(jnp.bfloat16)
    mixed_heads = jnp.einsum(
        "hij,jhe->ihe", weights, value_part, preferred_element_type=jnp.float32
    ).reshape(length, feature)
    gated_out = (layer_norm(mixed_heads, gain_mid) * gate_portion.astype(jnp.float32)).astype(
        jnp.bfloat16
    )
    result = inputs.astype(jnp.float32) + jnp.dot(
        gated_out, proj_out, preferred_element_type=jnp.float32
    )
    return jnp.where(row_pos < seq_len, result, 0.0).astype(jnp.bfloat16)


def slot_step(slot_in, seq_len, grad_out, proj_in, bias_in, gain_in, gain_mid, proj_out, toeplitz):
    result, pullback = jax.vjp(
        lambda inputs: slot_layer(
            inputs, seq_len, proj_in, bias_in, gain_in, gain_mid, proj_out, toeplitz
        ),
        slot_in,
    )
    return (result, pullback(grad_out)[0])


def selector(ids, in_range, width):
    columns = jnp.arange(width, dtype=jnp.int32)
    return ((ids[:, :, None] == columns[None, None, :]) & in_range[:, :, None]).astype(jnp.bfloat16)


def shards(
    item_table,
    unique_ids,
    inverse,
    lengths,
    assignment,
    proj_in,
    bias_in,
    gain_in,
    gain_mid,
    proj_out,
    position_bias,
    cotangent,
):
    emb_count = lax.axis_size("emb")
    seq_count = lax.axis_size("seq")
    devices = emb_count * seq_count
    rows_dev = item_table.shape[0]
    feature = item_table.shape[1]
    unique_count = unique_ids.shape[0]
    slot_cap = 2 * unique_count // devices
    owners = unique_ids // rows_dev
    local_row = unique_ids % rows_dev
    matches = (owners[:, None] == jnp.arange(devices, dtype=jnp.int32)[None, :]).astype(jnp.int32)
    running = jnp.cumsum(matches, axis=0)
    slot_rank = jnp.sum(running * matches, axis=1) - 1
    request = (
        jnp.full((devices, slot_cap), rows_dev, jnp.int32).at[owners, slot_rank].set(local_row)
    )
    asked = lax.all_to_all(request, ("emb", "seq"), split_axis=0, concat_axis=0, tiled=True)
    answer = lax.all_to_all(
        item_table[jnp.minimum(asked, rows_dev - 1)],
        ("emb", "seq"),
        split_axis=0,
        concat_axis=0,
        tiled=True,
    )
    distinct_item_rows = answer[owners, slot_rank]
    slot_count = lengths.shape[0]
    per_partner = slot_count // seq_count
    max_len = inverse.shape[1]
    bucket = assignment // slot_count * per_partner + assignment % per_partner
    chosen = (
        jnp.zeros((slot_count,), jnp.int32).at[bucket].set(jnp.arange(slot_count, dtype=jnp.int32))
    )
    sent_ids = inverse[chosen]
    sent_len = lengths[chosen]
    position = jnp.arange(max_len, dtype=jnp.int32)
    toeplitz = relative_table(position_bias, max_len)
    shared = gather_directly(distinct_item_rows, "seq", 0)
    got_ids, count_totals = in_one_piece(
        (
            sent_ids.reshape(seq_count, per_partner, max_len),
            sent_len.reshape(seq_count, per_partner),
        ),
        "seq",
        0,
        0,
        2,
    )
    count_totals = count_totals.reshape(slot_count)
    source = jnp.arange(slot_count, dtype=jnp.int32) // per_partner
    shared_ids = got_ids.reshape(slot_count, max_len) + (source * unique_count)[:, None]
    in_range = position[None, :] < count_totals[:, None]
    row_chooser = selector(shared_ids, in_range, seq_count * unique_count)
    balanced = jnp.einsum(
        "gmq,qp->gmp", row_chooser, shared, preferred_element_type=jnp.float32
    ).astype(jnp.bfloat16)
    outputs, token_grads = lax.map(
        lambda packed: slot_step(
            packed[0], packed[1], packed[2], proj_in, bias_in, gain_in, gain_mid, proj_out, toeplitz
        ),
        (balanced, count_totals, cotangent),
    )
    partial_sums = jnp.einsum(
        "ehm,ehr->mr", row_chooser, token_grads, preferred_element_type=jnp.float32
    )
    row_gradient_list = sum_at_owner(partial_sums.astype(jnp.bfloat16), "seq", 0)
    outgoing_grads = (
        jnp.zeros((devices, slot_cap, feature), jnp.float32)
        .at[owners, slot_rank]
        .set(row_gradient_list)
    )
    landed = lax.all_to_all(
        outgoing_grads.astype(jnp.bfloat16), ("emb", "seq"), split_axis=0, concat_axis=0, tiled=True
    ).astype(outgoing_grads.dtype)
    table_grad = (
        jnp.zeros((rows_dev, feature), jnp.float32)
        .at[asked.reshape(-1)]
        .add(landed.reshape(-1, feature), mode="drop")
    )
    return (outputs, table_grad)


def solution(mesh):
    in_specs = (
        P(("emb", "seq"), None),
        P(("emb", "seq")),
        P(("emb", "seq"), None),
        P(("emb", "seq")),
        P(("emb", "seq")),
        P(),
        P(),
        P(),
        P(),
        P(),
        P(),
        P(("emb", "seq"), None, None),
    )
    out_specs = (P(("emb", "seq"), None, None), P(("emb", "seq"), None))
    return jax.shard_map(shards, mesh=mesh, in_specs=in_specs, out_specs=out_specs, check_vma=False)
```

profile of v0, /device:TPU:1, one launch (start us, length us, event | category | flops | bytes accessed | tf_op | source)
XLA Modules:
  0.0 405.1 jit_solution(12954335621760301109)
XLA Ops:
  2.1 11.1 %scatter_fusion = s32[128,4]{0,1:T(4,128)S(1)} fusion(s32[128,4]{0,1:T(4,128)S(1)} %broadcast.310, s32[256]{0:T(256)S(1)} %bitcast.202, s32[256]{0:T(256)S(1)} %get-tuple-element.115), kind=kCustom, calls=%fused_computation.5 | custom fusion | bytes 5120 | tf_op jit(solution)/shard_map/scatter | solution.py:142
  13.9 11.5 %all-to-all-start.1 = ((s32[128,1,4]{2,1,0:T(1,128)}), s32[128,1,4]{2,1,0:T(1,128)S(1)}, u32[]{:S(2)}, u32[]{:S(2)}) async-start(s32[128,1,4]{2,1,0:T(1,128)} %copy.62), calls=%async_computation.1 | async-start | bytes 131072 | tf_op jit(solution)/shard_map/all_to_all | solution.py:144
  26.0 9.0 %all-to-all-done.1 = s32[128,1,4]{2,1,0:T(1,128)S(1)} async-done(((s32[128,1,4]{2,1,0:T(1,128)}), s32[128,1,4]{2,1,0:T(1,128)S(1)}, u32[]{:S(2)}, u32[]{:S(2)}) %all-to-all-start.1) | async-done | bytes 2080 | tf_op jit(solution)/shard_map/all_to_all | solution.py:144
  39.5 4.3 %all-to-all-start.2 = ((bf16[128,4,512]{2,1,0:T(4,128)(2,1)}), bf16[128,4,512]{2,1,0:T(4,128)(2,1)S(1)}, u32[]{:S(2)}, u32[]{:S(2)}) async-start(bf16[128,4,512]{2,1,0:T(4,128)(2,1)} %reshape.320), calls=%async_computation.2 | async-start | bytes 1048576 | tf_op jit(solution)/shard_map/all_to_all | solution.py:145
  46.2 11.5 %all-to-all-done.2 = bf16[128,4,512]{2,1,0:T(4,128)(2,1)S(1)} async-done(((bf16[128,4,512]{2,1,0:T(4,128)(2,1)}), bf16[128,4,512]{2,1,0:T(4,128)(2,1)S(1)}, u32[]{:S(2)}, u32[]{:S(2)}) %all-to-all-start.2) | async-done | bytes 524320 | tf_op jit(solution)/shard_map/all_to_all | solution.py:145
  57.7 3.3 all-to-all-start
  61.1 2.1 gather_fusion.3
  66.1 4.4 %all-to-all-start.3 = ((bf16[4,256,512]{2,1,0:T(8,128)(2,1)}), bf16[4,256,512]{2,1,0:T(8,128)(2,1)}, u32[]{:S(2)}, u32[]{:S(2)}) async-start(bf16[4,256,512]{2,1,0:T(8,128)(2,1)} %broadcast_in_dim.76), calls=%async_computation.3 | async-start | bytes 2097152 | tf_op jit(solution)/shard_map/all_to_all | solution.py:9
  72.4 3.7 reshape.295
  76.0 2.3 slice.64
  78.7 5.4 %all-to-all-done.3 = bf16[4,256,512]{2,1,0:T(8,128)(2,1)} async-done(((bf16[4,256,512]{2,1,0:T(8,128)(2,1)}), bf16[4,256,512]{2,1,0:T(8,128)(2,1)}, u32[]{:S(2)}, u32[]{:S(2)}) %all-to-all-start.3) | async-done | bytes 1048608 | tf_op jit(solution)/shard_map/all_to_all | solution.py:9
  84.1 5.1 %fusion.88 = bf16[8,256,512]{2,1,0:T(8,128)(2,1)} fusion(bf16[1024,512,1]{1,0,2:T(8,128)(2,1)} %bitcast.28, s32[8,256]{1,0:T(8,128)S(1)} %broadcast_add_fusion.2, pred[8,256]{1,0:T(8,128)(4,1)S(1)} %iota_compare_fusion.4), kind=kOutput, calls=%fused_computation.127 | convolution fusion | flops 2152726528 | bytes 3155968 | tf_op jit(solution)/shard_map/gmq,qp->gmp/dot_general | solution.py:180
  89.2 257.3 %while.12 = (s32[]{:T(128)}, bf16[8,256,512]{2,1,0:T(8,128)(2,1)}, bf16[8,256,512]{2,1,0:T(8,128)(2,1)}, s32[8]{0:T(128)S(1)}, bf16[8,256,512]{2,1,0:T(8,128)(2,...) while((s32[]{:T(128)}, bf16[8,256,512]{2,1,0:T(8,128)(2,1)}, ...), condition=%wide.region_14.15_spmd, body=%wide.region_5.14_spmd.sunk | while | flops 1773407488 | bytes 45682792 | solution.py:183
  91.7 3.9 multiply_convert_fusion.3
  99.1 2.8 select_convert_fusion.2
  112.5 3.6 fusion.184
  117.4 2.0 fusion.186
  119.5 2.1 fusion.178
  123.9 3.9 multiply_convert_fusion.3
  131.3 2.8 select_convert_fusion.2
  138.6 2.0 fusion.181
  144.6 3.6 fusion.184
  149.6 2.0 fusion.186
  151.6 2.1 fusion.178
  156.0 3.9 multiply_convert_fusion.3
  163.4 2.8 select_convert_fusion.2
  170.7 2.0 fusion.181
  176.8 3.6 fusion.184
  181.7 2.0 fusion.186
  183.7 2.1 fusion.178
  188.1 3.9 multiply_convert_fusion.3
  195.5 2.8 select_convert_fusion.2
  208.9 3.6 fusion.184
  213.8 2.0 fusion.186
  215.9 2.1 fusion.178
  220.3 3.9 multiply_convert_fusion.3
  227.7 2.8 select_convert_fusion.2
  235.0 2.0 fusion.181
  241.0 3.6 fusion.184
  246.0 2.0 fusion.186
  248.0 2.1 fusion.178
  252.4 3.9 multiply_convert_fusion.3
  259.8 2.8 select_convert_fusion.2
  267.1 2.0 fusion.181
  273.2 3.6 fusion.184
  278.1 2.0 fusion.186
  280.1 2.1 fusion.178
  284.5 3.9 multiply_convert_fusion.3
  291.9 2.8 select_convert_fusion.2
  299.3 2.0 fusion.181
  305.3 3.6 fusion.184
  310.2 2.0 fusion.186
  312.3 2.1 fusion.178
  316.7 3.9 multiply_convert_fusion.3
  324.1 2.8 select_convert_fusion.2
  337.4 3.6 fusion.184
  342.4 2.0 fusion.186
  344.4 2.1 fusion.178
  346.5 3.9 bitcast_convert_fusion
  350.5 15.2 %all_to_all.34 = bf16[4,256,512]{2,1,0:T(8,128)(2,1)S(1)} all-to-all(bf16[4,256,512]{2,1,0:T(8,128)(2,1)S(1)} %bitcast.215), channel_id=1, replica_groups=mesh['emb'=32,'seq'=4] {'seq'}, dimensions={0} | all-to-all | bytes 2097152 | tf_op jit(solution)/shard_map/all_to_all | solution.py:46
  366.0 12.3 %scatter_fusion.1 = f32[128,4,512]{2,1,0:T(4,128)S(1)} fusion(f32[128,4,512]{2,1,0:T(4,128)S(1)} %broadcast_in_dim.107, s32[256]{0:T(256)S(1)} %bitcast.203, f32[256,512]{1,0:T(8,128)S(1)} %convert_reduce_fusion.1), kind=kCustom, calls=%fused_computation.6 | custom fusion | bytes 1574912 | tf_op jit(solution)/shard_map/scatter | solution.py:196
  379.3 6.7 %all-to-all-start.5 = ((bf16[128,4,512]{2,1,0:T(4,128)(2,1)}), bf16[128,4,512]{2,1,0:T(4,128)(2,1)S(1)}, u32[]{:S(2)}, u32[]{:S(2)}) async-start(bf16[128,4,512]{2,1,0:T(4,128)(2,1)} %convert_element_type.105), calls=%async_computation.5 | async-start | bytes 1048576 | tf_op jit(solution)/shard_map/all_to_all | solution.py:198
  386.1 13.9 %all-to-all-done.5 = bf16[128,4,512]{2,1,0:T(4,128)(2,1)S(1)} async-done(((bf16[128,4,512]{2,1,0:T(4,128)(2,1)}), bf16[128,4,512]{2,1,0:T(4,128)(2,1)S(1)}, u32[]{:S(2)}, u32[]{:S(2)}) %all-to-all-start.5) | async-done | bytes 524320 | tf_op jit(solution)/shard_map/all_to_all | solution.py:198
  400.1 5.0 %scatter_custom_fusion.3 = f32[1024,512]{1,0:T(8,128)} fusion(s32[512]{0:T(512)S(1)} %bitcast.225, f32[512,512]{1,0:T(8,128)S(1)} %reshape.357, f32[]{:T(128)} %constant.132.clone.1), kind=kCustom, calls=%fused_computation.128 | custom fusion | flops 262144 | bytes 2097156 | tf_op jit(solution)/shard_map/scatter-add | solution.py:204
  (552 shorter events, 140.7 us)
Async XLA Ops:
  0.6 35.9 %copy-start = (bf16[1024,512]{1,0:T(8,128)(2,1)S(1)}, bf16[1024,512]{1,0:T(8,128)(2,1)}, u32[]{:S(2)}) copy-start(bf16[1024,512]{1,0:T(8,128)(2,1)} %param.14) | copy-start | bytes 3145732
  0.6 24.7 %copy-start.24 = (s32[8]{0:T(128)S(1)}, s32[8]{0:T(128)}, u32[]{:S(2)}) copy-start(s32[8]{0:T(128)} %param.18) | copy-start | bytes 100
  13.9 21.1 %all-to-all-start.1 = ((s32[128,1,4]{2,1,0:T(1,128)}), s32[128,1,4]{2,1,0:T(1,128)S(1)}, u32[]{:S(2)}, u32[]{:S(2)}) async-start(s32[128,1,4]{2,1,0:T(1,128)} %copy.62), calls=%async_computation.1 | async-start | bytes 131072 | tf_op jit(solution)/shard_map/all_to_all | solution.py:144
  38.5 5.2 %copy-start.6 = (s32[8,256]{1,0:T(8,128)S(1)}, s32[8,256]{1,0:T(8,128)}, u32[]{:S(2)}) copy-start(s32[8,256]{1,0:T(8,128)} %param.16) | copy-start | bytes 24580
  38.5 5.8 %copy-start.1 = (s32[8]{0:T(128)S(1)}, s32[8]{0:T(128)}, u32[]{:S(2)}) copy-start(s32[8]{0:T(128)} %param.17) | copy-start | bytes 100
  38.5 6.6 %copy-start.15 = (f32[4,256]{1,0:T(4,128)S(1)}, f32[4,256]{1,0:T(4,128)}, u32[]{:S(2)}) copy-start(f32[4,256]{1,0:T(4,128)} %param.24) | copy-start | bytes 12292
  39.5 18.2 %all-to-all-start.2 = ((bf16[128,4,512]{2,1,0:T(4,128)(2,1)}), bf16[128,4,512]{2,1,0:T(4,128)(2,1)S(1)}, u32[]{:S(2)}, u32[]{:S(2)}) async-start(bf16[128,4,512]{2,1,0:T(4,128)(2,1)} %reshape.320), calls=%async_computation.2 | async-start | bytes 1048576 | tf_op jit(solution)/shard_map/all_to_all | solution.py:145
  57.7 7.4 %all-to-all-start = ((s32[4,2,257]{2,1,0:T(2,128)}), s32[4,2,257]{2,1,0:T(2,128)S(1)}, u32[]{:S(2)}, u32[]{:S(2)}) async-start(s32[4,2,257]{2,1,0:T(2,128)} %pad_add_fusion), calls=%async_computation | async-start | bytes 24576 | tf_op jit(solution)/shard_map/all_to_all | solution.py:27
  66.1 18.0 %all-to-all-start.3 = ((bf16[4,256,512]{2,1,0:T(8,128)(2,1)}), bf16[4,256,512]{2,1,0:T(8,128)(2,1)}, u32[]{:S(2)}, u32[]{:S(2)}) async-start(bf16[4,256,512]{2,1,0:T(8,128)(2,1)} %broadcast_in_dim.76), calls=%async_computation.3 | async-start | bytes 2097152 | tf_op jit(solution)/shard_map/all_to_all | solution.py:9
  78.7 10.5 %copy-start.19 = (pred[8,256]{1,0:T(8,128)(4,1)}, pred[8,256]{1,0:T(8,128)(4,1)S(1)}, u32[]{:S(2)}) copy-start(pred[8,256]{1,0:T(8,128)(4,1)S(1)} %iota_compare_fusion.4) | copy-start | bytes 6148
  78.7 10.5 %copy-start.16 = (s32[8,256]{1,0:T(8,128)}, s32[8,256]{1,0:T(8,128)S(1)}, u32[]{:S(2)}) copy-start(s32[8,256]{1,0:T(8,128)S(1)} %broadcast_add_fusion.2) | copy-start | bytes 24580
  84.1 5.1 %copy-start.9 = (f32[512]{0:T(512)S(1)}, f32[512]{0:T(512)}, u32[]{:S(2)}) copy-start(f32[512]{0:T(512)} %param.22) | copy-start | bytes 6148
  84.1 5.1 %copy-start.20 = (f32[2048]{0:T(1024)S(1)}, f32[2048]{0:T(1024)}, u32[]{:S(2)}) copy-start(f32[2048]{0:T(1024)} %param.20) | copy-start | bytes 24580
  84.1 5.1 %copy-start.22 = (f32[512]{0:T(512)S(1)}, f32[512]{0:T(512)}, u32[]{:S(2)}) copy-start(f32[512]{0:T(512)} %param.21) | copy-start | bytes 6148
  89.5 7.5 %copy-start.17 = (s32[8]{0:T(128)}, s32[8]{0:T(128)S(1)}, u32[]{:S(2)}) copy-start(s32[8]{0:T(128)S(1)} %get-tuple-element.256) | copy-start | bytes 100 | tf_op jit(solution)/shard_map/while
  96.7 5.2 %copy-start.3 = (bf16[32,4,8,128]{3,2,1,0:T(8,128)(2,1)}, bf16[32,4,8,128]{3,2,1,0:T(8,128)(2,1)S(1)}, u32[]{:S(2)}) copy-start(bf16[32,4,8,128]{3,2,1,0:T(8,128)(2,1)S(1)} %get-tuple-element.213) | copy-start | bytes 786436 | tf_op jit(solution)/shard_map/while
  112.5 4.9 %copy-start.12 = (pred[256]{0:T(512)(128)(4,1)S(1)}, pred[256]{0:T(512)(128)(4,1)}, u32[]{:S(2)}) copy-start(pred[256]{0:T(512)(128)(4,1)} %copy-done.11) | copy-start | bytes 772 | tf_op jit(solution)/shard_map/while
  116.1 5.5 %copy-start.18 = (s32[8]{0:T(128)S(1)}, s32[8]{0:T(128)}, u32[]{:S(2)}) copy-start(s32[8]{0:T(128)} %copy-done.17) | copy-start | bytes 100 | tf_op jit(solution)/shard_map/while
  116.1 5.5 %copy-start.21 = (f32[2048]{0:T(1024)S(1)}, f32[2048]{0:T(1024)}, u32[]{:S(2)}) copy-start(f32[2048]{0:T(1024)} %get-tuple-element.298) | copy-start | bytes 24580 | tf_op jit(solution)/shard_map/while
  116.1 5.5 %copy-start.23 = (f32[512]{0:T(512)S(1)}, f32[512]{0:T(512)}, u32[]{:S(2)}) copy-start(f32[512]{0:T(512)} %get-tuple-element.314) | copy-start | bytes 6148 | tf_op jit(solution)/shard_map/while
  121.6 7.5 %copy-start.17 = (s32[8]{0:T(128)}, s32[8]{0:T(128)S(1)}, u32[]{:S(2)}) copy-start(s32[8]{0:T(128)S(1)} %get-tuple-element.256) | copy-start | bytes 100 | tf_op jit(solution)/shard_map/while
  128.8 5.2 %copy-start.3 = (bf16[32,4,8,128]{3,2,1,0:T(8,128)(2,1)}, bf16[32,4,8,128]{3,2,1,0:T(8,128)(2,1)S(1)}, u32[]{:S(2)}) copy-start(bf16[32,4,8,128]{3,2,1,0:T(8,128)(2,1)S(1)} %get-tuple-element.213) | copy-start | bytes 786436 | tf_op jit(solution)/shard_map/while
  144.6 4.9 %copy-start.12 = (pred[256]{0:T(512)(128)(4,1)S(1)}, pred[256]{0:T(512)(128)(4,1)}, u32[]{:S(2)}) copy-start(pred[256]{0:T(512)(128)(4,1)} %copy-done.11) | copy-start | bytes 772 | tf_op jit(solution)/shard_map/while
  148.2 5.5 %copy-start.18 = (s32[8]{0:T(128)S(1)}, s32[8]{0:T(128)}, u32[]{:S(2)}) copy-start(s32[8]{0:T(128)} %copy-done.17) | copy-start | bytes 100 | tf_op jit(solution)/shard_map/while
  148.2 5.5 %copy-start.21 = (f32[2048]{0:T(1024)S(1)}, f32[2048]{0:T(1024)}, u32[]{:S(2)}) copy-start(f32[2048]{0:T(1024)} %get-tuple-element.298) | copy-start | bytes 24580 | tf_op jit(solution)/shard_map/while
  148.3 5.5 %copy-start.23 = (f32[512]{0:T(512)S(1)}, f32[512]{0:T(512)}, u32[]{:S(2)}) copy-start(f32[512]{0:T(512)} %get-tuple-element.314) | copy-start | bytes 6148 | tf_op jit(solution)/shard_map/while
  153.7 7.5 %copy-start.17 = (s32[8]{0:T(128)}, s32[8]{0:T(128)S(1)}, u32[]{:S(2)}) copy-start(s32[8]{0:T(128)S(1)} %get-tuple-element.256) | copy-start | bytes 100 | tf_op jit(solution)/shard_map/while
  160.9 5.2 %copy-start.3 = (bf16[32,4,8,128]{3,2,1,0:T(8,128)(2,1)}, bf16[32,4,8,128]{3,2,1,0:T(8,128)(2,1)S(1)}, u32[]{:S(2)}) copy-start(bf16[32,4,8,128]{3,2,1,0:T(8,128)(2,1)S(1)} %get-tuple-element.213) | copy-start | bytes 786436 | tf_op jit(solution)/shard_map/while
  176.8 4.9 %copy-start.12 = (pred[256]{0:T(512)(128)(4,1)S(1)}, pred[256]{0:T(512)(128)(4,1)}, u32[]{:S(2)}) copy-start(pred[256]{0:T(512)(128)(4,1)} %copy-done.11) | copy-start | bytes 772 | tf_op jit(solution)/shard_map/while
  180.4 5.5 %copy-start.18 = (s32[8]{0:T(128)S(1)}, s32[8]{0:T(128)}, u32[]{:S(2)}) copy-start(s32[8]{0:T(128)} %copy-done.17) | copy-start | bytes 100 | tf_op jit(solution)/shard_map/while
  180.4 5.5 %copy-start.21 = (f32[2048]{0:T(1024)S(1)}, f32[2048]{0:T(1024)}, u32[]{:S(2)}) copy-start(f32[2048]{0:T(1024)} %get-tuple-element.298) | copy-start | bytes 24580 | tf_op jit(solution)/shard_map/while
  180.4 5.5 %copy-start.23 = (f32[512]{0:T(512)S(1)}, f32[512]{0:T(512)}, u32[]{:S(2)}) copy-start(f32[512]{0:T(512)} %get-tuple-element.314) | copy-start | bytes 6148 | tf_op jit(solution)/shard_map/while
  185.9 7.5 %copy-start.17 = (s32[8]{0:T(128)}, s32[8]{0:T(128)S(1)}, u32[]{:S(2)}) copy-start(s32[8]{0:T(128)S(1)} %get-tuple-element.256) | copy-start | bytes 100 | tf_op jit(solution)/shard_map/while
  193.1 5.2 %copy-start.3 = (bf16[32,4,8,128]{3,2,1,0:T(8,128)(2,1)}, bf16[32,4,8,128]{3,2,1,0:T(8,128)(2,1)S(1)}, u32[]{:S(2)}) copy-start(bf16[32,4,8,128]{3,2,1,0:T(8,128)(2,1)S(1)} %get-tuple-element.213) | copy-start | bytes 786436 | tf_op jit(solution)/shard_map/while
  208.9 4.9 %copy-start.12 = (pred[256]{0:T(512)(128)(4,1)S(1)}, pred[256]{0:T(512)(128)(4,1)}, u32[]{:S(2)}) copy-start(pred[256]{0:T(512)(128)(4,1)} %copy-done.11) | copy-start | bytes 772 | tf_op jit(solution)/shard_map/while
  212.5 5.5 %copy-start.18 = (s32[8]{0:T(128)S(1)}, s32[8]{0:T(128)}, u32[]{:S(2)}) copy-start(s32[8]{0:T(128)} %copy-done.17) | copy-start | bytes 100 | tf_op jit(solution)/shard_map/while
  212.5 5.5 %copy-start.21 = (f32[2048]{0:T(1024)S(1)}, f32[2048]{0:T(1024)}, u32[]{:S(2)}) copy-start(f32[2048]{0:T(1024)} %get-tuple-element.298) | copy-start | bytes 24580 | tf_op jit(solution)/shard_map/while
  212.5 5.5 %copy-start.23 = (f32[512]{0:T(512)S(1)}, f32[512]{0:T(512)}, u32[]{:S(2)}) copy-start(f32[512]{0:T(512)} %get-tuple-element.314) | copy-start | bytes 6148 | tf_op jit(solution)/shard_map/while
  218.0 7.5 %copy-start.17 = (s32[8]{0:T(128)}, s32[8]{0:T(128)S(1)}, u32[]{:S(2)}) copy-start(s32[8]{0:T(128)S(1)} %get-tuple-element.256) | copy-start | bytes 100 | tf_op jit(solution)/shard_map/while
  225.2 5.2 %copy-start.3 = (bf16[32,4,8,128]{3,2,1,0:T(8,128)(2,1)}, bf16[32,4,8,128]{3,2,1,0:T(8,128)(2,1)S(1)}, u32[]{:S(2)}) copy-start(bf16[32,4,8,128]{3,2,1,0:T(8,128)(2,1)S(1)} %get-tuple-element.213) | copy-start | bytes 786436 | tf_op jit(solution)/shard_map/while
  226.9 4.3 %copy-start.11 = (pred[256]{0:T(512)(128)(4,1)}, pred[256]{0:T(512)(128)(4,1)S(1)}, u32[]{:S(2)}) copy-start(pred[256]{0:T(512)(128)(4,1)S(1)} %iota_compare_fusion.6) | copy-start | bytes 772 | tf_op jit(solution)/shard_map/while
  241.0 4.9 %copy-start.12 = (pred[256]{0:T(512)(128)(4,1)S(1)}, pred[256]{0:T(512)(128)(4,1)}, u32[]{:S(2)}) copy-start(pred[256]{0:T(512)(128)(4,1)} %copy-done.11) | copy-start | bytes 772 | tf_op jit(solution)/shard_map/while
  244.6 5.5 %copy-start.18 = (s32[8]{0:T(128)S(1)}, s32[8]{0:T(128)}, u32[]{:S(2)}) copy-start(s32[8]{0:T(128)} %copy-done.17) | copy-start | bytes 100 | tf_op jit(solution)/shard_map/while
  244.7 5.5 %copy-start.21 = (f32[2048]{0:T(1024)S(1)}, f32[2048]{0:T(1024)}, u32[]{:S(2)}) copy-start(f32[2048]{0:T(1024)} %get-tuple-element.298) | copy-start | bytes 24580 | tf_op jit(solution)/shard_map/while
  244.7 5.5 %copy-start.23 = (f32[512]{0:T(512)S(1)}, f32[512]{0:T(512)}, u32[]{:S(2)}) copy-start(f32[512]{0:T(512)} %get-tuple-element.314) | copy-start | bytes 6148 | tf_op jit(solution)/shard_map/while
  250.1 7.5 %copy-start.17 = (s32[8]{0:T(128)}, s32[8]{0:T(128)S(1)}, u32[]{:S(2)}) copy-start(s32[8]{0:T(128)S(1)} %get-tuple-element.256) | copy-start | bytes 100 | tf_op jit(solution)/shard_map/while
  257.4 5.2 %copy-start.3 = (bf16[32,4,8,128]{3,2,1,0:T(8,128)(2,1)}, bf16[32,4,8,128]{3,2,1,0:T(8,128)(2,1)S(1)}, u32[]{:S(2)}) copy-start(bf16[32,4,8,128]{3,2,1,0:T(8,128)(2,1)S(1)} %get-tuple-element.213) | copy-start | bytes 786436 | tf_op jit(solution)/shard_map/while
  273.2 4.9 %copy-start.12 = (pred[256]{0:T(512)(128)(4,1)S(1)}, pred[256]{0:T(512)(128)(4,1)}, u32[]{:S(2)}) copy-start(pred[256]{0:T(512)(128)(4,1)} %copy-done.11) | copy-start | bytes 772 | tf_op jit(solution)/shard_map/while
  276.8 5.5 %copy-start.18 = (s32[8]{0:T(128)S(1)}, s32[8]{0:T(128)}, u32[]{:S(2)}) copy-start(s32[8]{0:T(128)} %copy-done.17) | copy-start | bytes 100 | tf_op jit(solution)/shard_map/while
  276.8 5.5 %copy-start.21 = (f32[2048]{0:T(1024)S(1)}, f32[2048]{0:T(1024)}, u32[]{:S(2)}) copy-start(f32[2048]{0:T(1024)} %get-tuple-element.298) | copy-start | bytes 24580 | tf_op jit(solution)/shard_map/while
  276.8 5.5 %copy-start.23 = (f32[512]{0:T(512)S(1)}, f32[512]{0:T(512)}, u32[]{:S(2)}) copy-start(f32[512]{0:T(512)} %get-tuple-element.314) | copy-start | bytes 6148 | tf_op jit(solution)/shard_map/while
  282.3 7.5 %copy-start.17 = (s32[8]{0:T(128)}, s32[8]{0:T(128)S(1)}, u32[]{:S(2)}) copy-start(s32[8]{0:T(128)S(1)} %get-tuple-element.256) | copy-start | bytes 100 | tf_op jit(solution)/shard_map/while
  289.5 5.2 %copy-start.3 = (bf16[32,4,8,128]{3,2,1,0:T(8,128)(2,1)}, bf16[32,4,8,128]{3,2,1,0:T(8,128)(2,1)S(1)}, u32[]{:S(2)}) copy-start(bf16[32,4,8,128]{3,2,1,0:T(8,128)(2,1)S(1)} %get-tuple-element.213) | copy-start | bytes 786436 | tf_op jit(solution)/shard_map/while
  305.3 4.9 %copy-start.12 = (pred[256]{0:T(512)(128)(4,1)S(1)}, pred[256]{0:T(512)(128)(4,1)}, u32[]{:S(2)}) copy-start(pred[256]{0:T(512)(128)(4,1)} %copy-done.11) | copy-start | bytes 772 | tf_op jit(solution)/shard_map/while
  308.9 5.5 %copy-start.18 = (s32[8]{0:T(128)S(1)}, s32[8]{0:T(128)}, u32[]{:S(2)}) copy-start(s32[8]{0:T(128)} %copy-done.17) | copy-start | bytes 100 | tf_op jit(solution)/shard_map/while
  308.9 5.5 %copy-start.21 = (f32[2048]{0:T(1024)S(1)}, f32[2048]{0:T(1024)}, u32[]{:S(2)}) copy-start(f32[2048]{0:T(1024)} %get-tuple-element.298) | copy-start | bytes 24580 | tf_op jit(solution)/shard_map/while
  308.9 5.5 %copy-start.23 = (f32[512]{0:T(512)S(1)}, f32[512]{0:T(512)}, u32[]{:S(2)}) copy-start(f32[512]{0:T(512)} %get-tuple-element.314) | copy-start | bytes 6148 | tf_op jit(solution)/shard_map/while
  314.4 7.5 %copy-start.17 = (s32[8]{0:T(128)}, s32[8]{0:T(128)S(1)}, u32[]{:S(2)}) copy-start(s32[8]{0:T(128)S(1)} %get-tuple-element.256) | copy-start | bytes 100 | tf_op jit(solution)/shard_map/while
  321.6 5.2 %copy-start.3 = (bf16[32,4,8,128]{3,2,1,0:T(8,128)(2,1)}, bf16[32,4,8,128]{3,2,1,0:T(8,128)(2,1)S(1)}, u32[]{:S(2)}) copy-start(bf16[32,4,8,128]{3,2,1,0:T(8,128)(2,1)S(1)} %get-tuple-element.213) | copy-start | bytes 786436 | tf_op jit(solution)/shard_map/while
  337.4 4.9 %copy-start.12 = (pred[256]{0:T(512)(128)(4,1)S(1)}, pred[256]{0:T(512)(128)(4,1)}, u32[]{:S(2)}) copy-start(pred[256]{0:T(512)(128)(4,1)} %copy-done.11) | copy-start | bytes 772 | tf_op jit(solution)/shard_map/while
  341.0 5.5 %copy-start.18 = (s32[8]{0:T(128)S(1)}, s32[8]{0:T(128)}, u32[]{:S(2)}) copy-start(s32[8]{0:T(128)} %copy-done.17) | copy-start | bytes 100 | tf_op jit(solution)/shard_map/while
  341.1 5.5 %copy-start.21 = (f32[2048]{0:T(1024)S(1)}, f32[2048]{0:T(1024)}, u32[]{:S(2)}) copy-start(f32[2048]{0:T(1024)} %get-tuple-element.298) | copy-start | bytes 24580 | tf_op jit(solution)/shard_map/while
  341.1 5.5 %copy-start.23 = (f32[512]{0:T(512)S(1)}, f32[512]{0:T(512)}, u32[]{:S(2)}) copy-start(f32[512]{0:T(512)} %get-tuple-element.314) | copy-start | bytes 6148 | tf_op jit(solution)/shard_map/while
  379.3 20.7 %all-to-all-start.5 = ((bf16[128,4,512]{2,1,0:T(4,128)(2,1)}), bf16[128,4,512]{2,1,0:T(4,128)(2,1)S(1)}, u32[]{:S(2)}, u32[]{:S(2)}) async-start(bf16[128,4,512]{2,1,0:T(4,128)(2,1)} %convert_element_type.105), calls=%async_computation.5 | async-start | bytes 1048576 | tf_op jit(solution)/shard_map/all_to_all | solution.py:198
  (71 other events, 204.6 us)
where the time goes:
time: 409 us; the launch traced here: 405 us
  matrix products  151 us (37%)
  local copies, waits for them, and re-layouts  80.6 us (20%)
  other arithmetic  77 us (19%)
  waiting for transfers between devices  41.7 us (10%)
  starting transfers between devices  30.1 us (7%)
  blocking collectives  15.2 us (4%)
  loops' own time  8.14 us (2%)
    dot_general x16, matrix products, slot_layer(): jnp.dot(normed, proj_in, preferred_element_type=jnp.float32) + bias_in  59.3 us
    reduce_sum x24, other arithmetic, layer_norm(): center = values - jnp.mean(values, axis=-1, keepdims=True)  34.1 us
    dot_general x24, matrix products, slot_layer(): jnp.einsum('ihe,jhe->hij', query_part, key_part, preferred_element_type=j...  32.3 us
    dot_general x16, matrix products, slot_layer(): jnp.dot(gated_out, proj_out, preferred_element_type=jnp.float32)  30.1 us
    dot_general x24, matrix products, slot_layer(): jnp.einsum('hij,jhe->ihe', weights, value_part, preferred_element_type=jn...  20.6 us
    dynamic_update_slice x8, other arithmetic, shards(): lax.map(lambda packed: slot_step(packed[0], packed[1], packed[2], proj_in...  16.1 us
    reshape x16, local copies, waits for them, and re-layouts, slot_layer(): key_part = hidden[:, 3 * feature:].reshape(length, head_count, head_size)  15.4 us
    all_to_all x1, blocking collectives, sum_at_owner(): parts = lax.all_to_all(in_blocks(x, dim, devices), axis, 0, 0, tiled=True)  15.2 us
  transfers between devices with their start and end apart: 5, of which 5 were waited for; matrix products, arithmetic and copies ran while one was open for 3% of the time, Pallas kernels for 0%

commit v1 on v0

v1 whole, which is shorter than its diff:
```python
import functools

import jax
import jax.numpy as jnp
from jax import lax
from jax.experimental import pallas as pl
from jax.experimental.pallas import tpu as pltpu
from jax.sharding import PartitionSpec as P

D = 512
HEADS = 4
HEAD = 128
MAXLEN = 256
UNIQ = 256
ROWS_DEV = 1024
DEVICES = 128
SCALE = HEAD**-0.5
EPS = 1e-05
MASKED = -1e30
BF = jnp.bfloat16
F32 = jnp.float32
I32 = jnp.int32


def nn(a, b):
    return lax.dot_general(a, b, (((1,), (0,)), ((), ())), preferred_element_type=F32)


def nt(a, b):
    return lax.dot_general(a, b, (((1,), (1,)), ((), ())), preferred_element_type=F32)


def tn(a, b):
    return lax.dot_general(a, b, (((0,), (0,)), ((), ())), preferred_element_type=F32)


def iota(shape, dim):
    return lax.broadcasted_iota(I32, shape, dim)


def onehot(mask):
    return jnp.where(mask, 1.0, 0.0).astype(BF)


def params(**kw):
    return pltpu.CompilerParams(vmem_limit_bytes=48 << 20, **kw)


def pack_kernel(assign_ref, len_ref, seq_ref, ids_ref, inv_ref, req_ref, pos_ref, *msg_refs):
    ids = ids_ref[...]
    owner = ids >> 10
    local = (ids & (ROWS_DEV - 1)).astype(F32)
    held = iota((DEVICES, UNIQ), 0) == owner
    earlier = onehot(iota((UNIQ, UNIQ), 0) < iota((UNIQ, UNIQ), 1))
    before = nn(onehot(held), earlier)
    rank = jnp.sum(jnp.where(held, before, 0.0), axis=0, keepdims=True)
    pos_ref[...] = owner * 8 + rank.astype(I32)
    lane = iota((DEVICES, 4), 1)
    req = jnp.zeros((DEVICES, 4), F32)
    for r in range(4):
        chosen = held & (before == float(r))
        col = jnp.sum(jnp.where(chosen, ROWS_DEV - local, 0.0), axis=1, keepdims=True)
        req = jnp.where(lane == r, ROWS_DEV - col, req)
    req_ref[...] = req.astype(I32)
    seq = seq_ref[0]
    for j in range(8):
        place = assign_ref[j]
        delta = (place // 8 - seq + 4) % 4
        half = place % 2
        row = jnp.concatenate(
            [inv_ref[j : j + 1, :], jnp.full((1, 128), len_ref[j], I32)], axis=1
        )
        for d in range(4):
            for b in range(2):

                @pl.when((delta == d) & (half == b))
                def _():
                    msg_refs[d][b : b + 1, :] = row


def pack(assignment, lengths, seq, ids, inverse):
    smem = pl.BlockSpec(memory_space=pltpu.SMEM)
    vmem = pl.BlockSpec(memory_space=pltpu.VMEM)
    return pl.pallas_call(
        pack_kernel,
        in_specs=[smem, smem, smem, vmem, vmem],
        out_specs=[vmem] * 6,
        out_shape=[
            jax.ShapeDtypeStruct((DEVICES, 4), I32),
            jax.ShapeDtypeStruct((1, UNIQ), I32),
        ]
        + [jax.ShapeDtypeStruct((2, MAXLEN + 128), I32)] * 4,
        compiler_params=params(),
        name="pack",
    )(assignment, lengths, seq, ids.reshape(1, UNIQ), inverse)


def tables_kernel(flipped_ref, pos_ref, bias_ref, pos_rows_ref):
    i = iota((MAXLEN, MAXLEN), 0)
    j = iota((MAXLEN, MAXLEN), 1)
    for h in range(HEADS):
        line = jnp.broadcast_to(flipped_ref[h : h + 1, :], (MAXLEN, MAXLEN))
        spread = pltpu.roll(line, 1, 1, stride=1, stride_axis=0)
        full = jnp.where(j <= i, 0.5 * spread, MASKED)
        bias_ref[h] = full[:, :128]
    pos = jnp.broadcast_to(pos_ref[...], (UNIQ, UNIQ)).astype(F32)
    col = jnp.sum(jnp.where(i == j, pos, 0.0), axis=1, keepdims=True)
    pos_rows_ref[...] = jnp.broadcast_to(col.astype(I32), (UNIQ, 128))


def tables(position_bias, pos):
    return pl.pallas_call(
        tables_kernel,
        out_shape=[
            jax.ShapeDtypeStruct((HEADS, MAXLEN, 128), F32),
            jax.ShapeDtypeStruct((UNIQ, 128), I32),
        ],
        compiler_params=params(),
        name="tables",
    )(position_bias[:, ::-1], pos)


def asked_parts(asked_ref):
    asked = asked_ref[...]
    return (asked >> 5).astype(BF), (asked & 31).astype(BF)


def answer_kernel(asked_ref, table_ref, out_ref):
    high, low = asked_parts(asked_ref)
    count = 256
    for c in range(8 * DEVICES // count):
        row = iota((count, DEVICES), 0) + c * count
        spread = onehot((row >> 3) == iota((count, DEVICES), 1))
        value = nn(spread, high) * 32.0 + nn(spread, low)
        rank = (iota((count, 4), 0)) & 3
        col = jnp.sum(jnp.where(iota((count, 4), 1) == rank, value, 0.0), axis=1, keepdims=True)
        pick = onehot(iota((count, ROWS_DEV), 1) == col.astype(I32))
        both = nn(pick, table_ref[...])
        upper = (iota((count, D // 2), 0) & 7) < 4
        out_ref[pl.ds(c * count, count), :] = jnp.where(
            upper, both[:, : D // 2], both[:, D // 2 :]
        ).astype(BF)


def answer_rows(asked, table):
    return pl.pallas_call(
        answer_kernel,
        out_shape=jax.ShapeDtypeStruct((8 * DEVICES, D // 2), BF),
        compiler_params=params(),
        name="answer",
    )(asked, table)


def compact_kernel(pos_ref, got_ref, out_ref):
    pos = pos_ref[:, :1]
    lane = iota((UNIQ, 8 * DEVICES), 1)
    for half in range(2):
        pick = onehot(lane == pos + 4 * half)
        out_ref[:, pl.ds(half * 256, 256)] = nn(pick, got_ref[...]).astype(BF)


def compact(pos_rows, got):
    return pl.pallas_call(
        compact_kernel,
        out_shape=jax.ShapeDtypeStruct((UNIQ, D), BF),
        compiler_params=params(),
        name="compact",
    )(pos_rows, got)


def row_mean(x):
    return jnp.sum(x, axis=-1, keepdims=True) * (1.0 / D)


def norm_parts(x):
    center = x - row_mean(x)
    spread = row_mean(center * center)
    inv = lax.rsqrt(spread + EPS)
    return center * inv, inv


def norm_grad(g, unit, inv):
    return inv * (g - row_mean(g) - unit * row_mean(g * unit))


def slot_body(size, count, ids, rows, cot, out_ref, acc_ref, fresh, refs):
    (win_ref, bin_ref, gin_ref, gmid_ref, wout_ref, bias_ref, hid, slope, wts, wslope, dpre, mix) = refs
    rowpos = iota((size, 1), 0)
    valid = rowpos < count
    ids_rows = jnp.broadcast_to(ids[:, :size], (8, size)).astype(F32)
    ids_cols = ids_rows.T[:, :1].astype(I32)
    pick = onehot((iota((size, UNIQ), 1) == ids_cols) & valid)
    x = nn(pick, rows)
    unit_in, inv_in = norm_parts(x)
    normed = (unit_in * gin_ref[...]).astype(BF)
    for c in range(4):
        cols = pl.ds(c * D, D)
        half = 0.5 * (nn(normed, win_ref[:, cols]) + bin_ref[:, cols])
        up = 1.0 + jnp.tanh(half)
        act = half * up
        hid[:size, cols] = act.astype(BF)
        slope[:size, cols] = 0.5 * (up + act * (2.0 - up))
    per = jnp.where(valid, 1.0, 0.0) / count.astype(F32)
    blocks = size // 128
    for h in range(HEADS):
        vcol, qcol, kcol = (pl.ds(D * g + h * HEAD, HEAD) for g in (1, 2, 3))
        for bi in range(blocks):
            rs = pl.ds(bi * 128, 128)
            width = (bi + 1) * 128
            if bi == 0:
                bias = bias_ref[h, :128, :]
            else:
                bias = jnp.concatenate([bias_ref[h, 128:, :], bias_ref[h, :128, :]], axis=1)
            half = nt(hid[rs, qcol], hid[:width, kcol]) * (0.5 * SCALE) + bias
            up = 1.0 + jnp.tanh(half)
            act = half * up
            scale = per[bi * 128 : (bi + 1) * 128]
            w = (act * scale).astype(BF)
            wts[h, rs, :width] = w
            wslope[h, rs, :width] = (up + act * (2.0 - up)) * (scale * (0.5 * SCALE))
            mix[rs, pl.ds(h * HEAD, HEAD)] = nn(w, hid[:width, vcol])
    unit_mid, inv_mid = norm_parts(mix[:size, :])
    scaled = unit_mid * gmid_ref[...]
    gate = hid[:size, :D].astype(F32)
    gated = (scaled * gate).astype(BF)
    result = x + nn(gated, wout_ref[...])
    out_ref[0, :size, :] = jnp.where(valid, result, 0.0).astype(BF)
    if size < MAXLEN:
        out_ref[0, size:, :] = jnp.zeros((MAXLEN - size, D), BF)
    grad = jnp.where(valid, cot.astype(F32), 0.0)
    dgated = nt(grad.astype(BF), wout_ref[...]).astype(BF).astype(F32)
    dgate = (dgated * scaled).astype(BF).astype(F32)
    dpre[:size, :D] = (dgate * slope[:size, :D]).astype(BF)
    dmix = norm_grad(dgated * gate * gmid_ref[...], unit_mid, inv_mid).astype(BF)
    for h in range(HEADS):
        vcol, qcol, kcol = (pl.ds(D * g + h * HEAD, HEAD) for g in (1, 2, 3))
        dv = [None] * blocks
        dk = [None] * blocks
        for bi in range(blocks):
            rs = pl.ds(bi * 128, 128)
            width = (bi + 1) * 128
            dm = dmix[bi * 128 : (bi + 1) * 128, h * HEAD : (h + 1) * HEAD]
            dw = nt(dm, hid[:width, vcol])
            ds = (dw * wslope[h, rs, :width]).astype(BF)
            dq = nn(ds, hid[:width, kcol]).astype(BF).astype(F32)
            dpre[rs, qcol] = (dq * slope[rs, qcol]).astype(BF)
            dvs = tn(wts[h, rs, :width], dm)
            dks = tn(ds, hid[rs, qcol])
            for bj in range(bi + 1):
                part = slice(bj * 128, (bj + 1) * 128)
                dv[bj] = dvs[part] if dv[bj] is None else dv[bj] + dvs[part]
                dk[bj] = dks[part] if dk[bj] is None else dk[bj] + dks[part]
        for bj in range(blocks):
            rs = pl.ds(bj * 128, 128)
            dpre[rs, vcol] = (dv[bj].astype(BF).astype(F32) * slope[rs, vcol]).astype(BF)
            dpre[rs, kcol] = (dk[bj].astype(BF).astype(F32) * slope[rs, kcol]).astype(BF)
    dnormed = nt(dpre[:size, :], win_ref[...]).astype(BF).astype(F32)
    dx = norm_grad(dnormed * gin_ref[...], unit_in, inv_in)
    token = (dx + grad).astype(BF)
    back = onehot((iota((UNIQ, size), 0) == ids[:, :size]) & (iota((UNIQ, size), 1) < count))
    sums = nn(back, token)
    acc_ref[...] = jnp.where(fresh, sums, sums + acc_ref[...])


def layer_kernel(plan, aliased, *refs):
    deltas, each = plan
    n_src = len(deltas)
    refs = list(refs)
    seq_ref = refs.pop(0)
    smsg = [refs.pop(0) for _ in range(n_src)]
    vmsg = [refs.pop(0) for _ in range(n_src)]
    rows_refs = [refs.pop(0) for _ in range(n_src)]
    cot_ref = refs.pop(0)
    win_ref, bin_ref, gin_ref, gmid_ref, wout_ref, bias_ref = (refs.pop(0) for _ in range(6))
    if aliased:
        refs.pop(0)
    out_ref = refs.pop(0)
    part_refs = [refs.pop(0) for _ in range(n_src)]
    rows, ids_sc, acc = (refs.pop(0) for _ in range(3))
    scratch = refs
    step = pl.program_id(0)
    src = step // len(each)
    turn = step % len(each)
    count = jnp.int32(0)
    for d in range(n_src):
        for t, b in enumerate(each):
            here = (src == d) & (turn == t)
            count = jnp.where(here, smsg[d][b, MAXLEN], count)

            @pl.when(here)
            def _():
                ids_sc[...] = vmsg[d][b : b + 1, :MAXLEN]
                if t == 0:
                    rows[...] = rows_refs[d][...]

    weights = (win_ref, bin_ref, gin_ref, gmid_ref, wout_ref, bias_ref, *scratch)
    for size in (128, 256):

        @pl.when((count <= 128) == (size == 128))
        def _():
            slot_body(
                size,
                count,
                ids_sc[...],
                rows[...],
                cot_ref[0, :size, :],
                out_ref,
                acc,
                turn == 0,
                weights,
            )

    for d in range(n_src):

        @pl.when((src == d) & (turn == len(each) - 1))
        def _():
            part_refs[d][...] = acc[...].astype(BF)


def layer(plan, seq, msgs, rows, cot, weights, prior):
    deltas, each = plan
    n_src = len(deltas)
    n_each = len(each)

    def slot(i, seq_ref):
        src = i // n_each
        delta = deltas[0]
        for d in range(1, n_src):
            delta = jnp.where(src == d, deltas[d], delta)
        turn = i % n_each
        b = each[0]
        for t in range(1, n_each):
            b = jnp.where(turn == t, each[t], b)
        return ((seq_ref[0] - delta + 4) % 4) * 2 + b, 0, 0

    whole = lambda a: pl.BlockSpec(a.shape, lambda i, s, n=a.ndim: (0,) * n, pipeline_mode=pl.Buffered(1))
    smem = pl.BlockSpec(memory_space=pltpu.SMEM)
    in_specs = [smem] * n_src + [whole(m) for m in msgs] + [whole(r) for r in rows]
    in_specs += [pl.BlockSpec((1, MAXLEN, D), slot)] + [whole(w) for w in weights]
    args = [*msgs, *msgs, *rows, cot, *weights]
    alias = {}
    if prior is not None:
        in_specs.append(pl.BlockSpec(memory_space=pl.ANY))
        args.append(prior)
        alias = {len(args): 0}
    part = jax.ShapeDtypeStruct((UNIQ, D), BF)
    return pl.pallas_call(
        functools.partial(layer_kernel, plan, prior is not None),
        grid_spec=pltpu.PrefetchScalarGridSpec(
            num_scalar_prefetch=1,
            grid=(n_src * n_each,),
            in_specs=in_specs,
            out_specs=[pl.BlockSpec((1, MAXLEN, D), slot)]
            + [pl.BlockSpec((UNIQ, D), lambda i, s: (0, 0))] * n_src,
            scratch_shapes=[
                pltpu.VMEM((UNIQ, D), BF),
                pltpu.VMEM((1, MAXLEN), I32),
                pltpu.VMEM((UNIQ, D), F32),
                pltpu.VMEM((MAXLEN, 4 * D), BF),
                pltpu.VMEM((MAXLEN, 4 * D), F32),
                pltpu.VMEM((HEADS, MAXLEN, MAXLEN), BF),
                pltpu.VMEM((HEADS, MAXLEN, MAXLEN), F32),
                pltpu.VMEM((MAXLEN, 4 * D), BF),
                pltpu.VMEM((MAXLEN, D), F32),
            ],
        ),
        out_shape=[jax.ShapeDtypeStruct(cot.shape, BF)] + [part] * n_src,
        input_output_aliases=alias,
        compiler_params=params(dimension_semantics=("arbitrary",)),
        name="layer",
    )(seq, *args)


def expand_kernel(pos_ref, *refs):
    out_ref = refs[-1]
    total = refs[0][...].astype(F32)
    for r in refs[1:-1]:
        total = total + r[...].astype(F32)
    total = total.astype(BF)
    row = iota((8 * DEVICES, UNIQ), 0)
    pos = pos_ref[...]
    upper = nn(onehot(row == pos), total[:, : D // 2])
    lower = nn(onehot(row == pos + 4), total[:, D // 2 :])
    out_ref[...] = (upper + lower).astype(BF)


def expand(pos, parts):
    return pl.pallas_call(
        expand_kernel,
        out_shape=jax.ShapeDtypeStruct((8 * DEVICES, D // 2), BF),
        compiler_params=params(),
        name="expand",
    )(pos, *parts)


def asked_line_kernel(asked_ref, out_ref):
    parts = []
    spread = onehot(iota((DEVICES, 8 * DEVICES), 0) == (iota((DEVICES, 8 * DEVICES), 1) >> 3))
    for part in asked_parts(asked_ref):
        square = jnp.concatenate([part.astype(F32), jnp.zeros((DEVICES, 124), F32)], axis=1)
        parts.append(nn(square.T[:8].astype(BF), spread))
    value = parts[0] * 32.0 + parts[1]
    mine = iota((8, 8 * DEVICES), 0) == (iota((8, 8 * DEVICES), 1) & 3)
    out_ref[...] = jnp.sum(jnp.where(mine, value, 0.0), axis=0, keepdims=True).astype(I32)


def asked_line(asked):
    return pl.pallas_call(
        asked_line_kernel,
        out_shape=jax.ShapeDtypeStruct((1, 8 * DEVICES), I32),
        compiler_params=params(),
        name="asked_line",
    )(asked)


def scatter_kernel(line_ref, landed_ref, out_ref):
    size = out_ref.shape[0]
    row = iota((size, 8 * DEVICES), 0) + pl.program_id(0) * size
    upper = (iota((1, 8 * DEVICES), 1) & 7) < 4
    line = line_ref[...]
    for half in range(2):
        wanted = jnp.where(upper == (half == 0), line, -1)
        out_ref[:, pl.ds(half * 256, 256)] = nn(onehot(row == wanted), landed_ref[...])


def scatter(line, landed):
    size = 256
    whole = lambda a: pl.BlockSpec(a.shape, lambda i: (0, 0), pipeline_mode=pl.Buffered(1))
    return pl.pallas_call(
        scatter_kernel,
        grid=(ROWS_DEV // size,),
        in_specs=[whole(line), whole(landed)],
        out_specs=pl.BlockSpec((size, D), lambda i: (i, 0)),
        out_shape=jax.ShapeDtypeStruct((ROWS_DEV, D), F32),
        compiler_params=params(dimension_semantics=("arbitrary",)),
        name="scatter",
    )(line, landed)


def ring(delta):
    return [(i, (i + delta) % 4) for i in range(4)]


def exchange(x, shape):
    got = lax.all_to_all(x.reshape(shape), ("emb", "seq"), split_axis=0, concat_axis=0, tiled=True)
    return got.reshape(x.shape)


PLANS = (((0, 1, 3, 2), (0, 1)),)


def shards(
    item_table,
    unique_ids,
    inverse,
    lengths,
    assignment,
    proj_in,
    bias_in,
    gain_in,
    gain_mid,
    proj_out,
    position_bias,
    cotangent,
):
    seq = lax.axis_index("seq").astype(I32).reshape(1)
    req, pos, *sent = pack(assignment, lengths, seq, unique_ids, inverse)
    asked = exchange(req, (DEVICES, 1, 4))
    msgs = [sent[0]] + [lax.ppermute(sent[d], "seq", ring(d)) for d in (1, 2, 3)]
    bias, pos_rows = tables(position_bias, pos)
    answer = answer_rows(asked, item_table)
    got = exchange(answer, (DEVICES, 8, D // 2))
    line = asked_line(asked)
    own = compact(pos_rows, got)
    rows = [own] + [lax.ppermute(own, "seq", ring(d)) for d in (1, 2, 3)]
    weights = (
        proj_in,
        bias_in.reshape(1, 4 * D),
        gain_in.reshape(1, D),
        gain_mid.reshape(1, D),
        proj_out,
        bias,
    )
    outputs = None
    sums = []
    for plan in PLANS:
        outputs, *parts = layer(
            plan,
            seq,
            [msgs[d] for d in plan[0]],
            [rows[d] for d in plan[0]],
            cotangent,
            weights,
            outputs,
        )
        for d, part in zip(plan[0], parts):
            sums.append(part if d == 0 else lax.ppermute(part, "seq", ring(-d)))
    landed = exchange(expand(pos, sums), (DEVICES, 8, D // 2))
    return (outputs, scatter(line, landed))


def solution(mesh):
    both = ("emb", "seq")
    in_specs = (
        P(both, None),
        P(both),
        P(both, None),
        P(both),
        P(both),
        P(),
        P(),
        P(),
        P(),
        P(),
        P(),
        P(both, None, None),
    )
    out_specs = (P(both, None, None), P(both, None))
    return jax.shard_map(shards, mesh=mesh, in_specs=in_specs, out_specs=out_specs, check_vma=False)
```

time: 409 us -> 146 us (0.36)
  matrix products: 151 us -> 0 us
  other arithmetic: 77 us -> 0 us
  local copies, waits for them, and re-layouts: 80.6 us -> 6.1 us
  Pallas kernels: 0 us -> 48.4 us
  starting transfers between devices: 30.1 us -> 19.8 us
  waiting for transfers between devices: 41.7 us -> 49.9 us
  loops' own time: 8.14 us -> 0 us
  blocking collectives: 15.2 us -> 21 us
    dot_general x82 -> x0, matrix products: 151 us -> none  [the longest x16 59.3 us: slot_layer(): jnp.dot(normed, proj_in, preferred_element_type=jnp.float32) + bias_in]
    pallas_call x0 -> x8, Pallas kernels: none -> 48.4 us  [the longest x1 38.7 us: layer(): pl.pallas_call(functools.partial(layer_kernel, plan, prior is not None),...]
    reduce_sum x42 -> x0, other arithmetic: 44.6 us -> none  [the longest x24 34.1 us: layer_norm(): center = values - jnp.mean(values, axis=-1, keepdims=True)]
    reshape x61 -> x0, local copies, waits for them, and re-layouts: 25.2 us -> none  [the longest x16 15.4 us: slot_layer(): key_part = hidden[:, 3 * feature:].reshape(length, head_count, head_size)]
    scatter x3 -> x0, local copies, waits for them, and re-layouts: 24 us -> none  [the longest x1 12.3 us: shards(): outgoing_grads = jnp.zeros((devices, slot_cap, feature), jnp.float32).at[...]
    ppermute x0 -> x9, waiting for transfers between devices: none -> 23.6 us  [the longest x3 13.5 us: shards(): lax.ppermute(sent[d], 'seq', ring(d))]
    all_to_all x5 -> x2, starting transfers between devices: 30.1 us -> 11.9 us  [exchange(): lax.all_to_all(x.reshape(shape), ('emb', 'seq'), split_axis=0, concat_axi...]
    dynamic_update_slice x8 -> x0, other arithmetic: 16.1 us -> none  [shards(): lax.map(lambda packed: slot_step(packed[0], packed[1], packed[2], proj_in...]
  transfers between devices with their start and end apart: 5 -> 11, of which waited for: 5 -> 7; matrix products, arithmetic and copies ran while one was open for 3% -> 0% of each run, Pallas kernels for 0% -> 0%
where the time goes in v1:
time: 146 us
  waiting for transfers between devices  49.9 us (34%)
  Pallas kernels  48.4 us (33%)
  blocking collectives  21 us (14%)
  starting transfers between devices  19.8 us (14%)
  local copies, waits for them, and re-layouts  6.1 us (4%)
    pallas_call x1, Pallas kernels, layer(): pl.pallas_call(functools.partial(layer_kernel, plan, prior is not None),...  38.7 us
    all_to_all x2, waiting for transfers between devices, exchange(): lax.all_to_all(x.reshape(shape), ('emb', 'seq'), split_axis=0, concat_axi...  26.3 us
    all_to_all x1, blocking collectives, exchange(): lax.all_to_all(x.reshape(shape), ('emb', 'seq'), split_axis=0, concat_axi...  21 us
    ppermute x3, waiting for transfers between devices, shards(): lax.ppermute(sent[d], 'seq', ring(d))  13.5 us
    all_to_all x2, starting transfers between devices, exchange(): lax.all_to_all(x.reshape(shape), ('emb', 'seq'), split_axis=0, concat_axi...  11.9 us
    ppermute x3, waiting for transfers between devices, shards(): sums.append(part if d == 0 else lax.ppermute(part, 'seq', ring(-d)))  10.1 us
    unnamed x26, local copies, waits for them, and re-layouts  5.9 us
    ppermute x3, starting transfers between devices, shards(): lax.ppermute(sent[d], 'seq', ring(d))  3.17 us
  transfers between devices with their start and end apart: 11, of which 7 were waited for; matrix products, arithmetic and copies ran while one was open for 0% of the time, Pallas kernels for 0%

profile of v1, /device:TPU:1, one launch (start us, length us, event | category | flops | bytes accessed | tf_op | source)
XLA Modules:
  0.0 145.9 jit_solution(14351836337682602364)
XLA Ops:
  0.6 0.0 copy-start
  0.6 0.0 copy-start.6
  0.7 0.8 copy-done.6
  1.5 0.0 copy-start.9
  1.5 0.7 copy-done.9
  2.2 0.0 copy-start.10
  2.2 0.7 copy-done.10
  2.8 0.0 copy-start.11
  2.8 0.7 copy-done.11
  3.5 1.3 pack.1
  4.8 21.0 %all_to_all.15 = s32[128,1,4]{2,1,0:T(1,128)S(1)} all-to-all(s32[128,1,4]{2,1,0:T(1,128)S(1)} %bitcast.17), channel_id=1, replica_groups=mesh['emb'=32,'seq'=4] {'emb','seq'}, dimensions={0} | all-to-all | bytes 4096 | tf_op jit(solution)/shard_map/all_to_all | solution.py:445
  25.8 0.0 copy-start.1
  25.8 1.2 copy-done.1
  27.0 0.0 copy-start.12
  27.0 0.0 copy-start.2
  27.0 0.0 copy-start.5
  27.0 0.0 copy-start.7
  27.0 0.0 copy-start.8
  27.0 3.1 %answer.1 = bf16[1024,256]{1,0:T(8,128)(2,1)} custom-call(s32[128,4]{1,0:T(8,128)S(1)} %bitcast.15, bf16[1024,512]{1,0:T(8,128)(2,1)S(1)} %copy-done.1), custom_call_target="tpu_custom_call" | custom-call | tf_op jit(solution)/shard_map/answer/pallas_call | solution.py:146
  30.2 4.2 %all-to-all-start.1 = ((bf16[128,8,256]{2,1,0:T(8,128)(2,1)}), bf16[128,8,256]{2,1,0:T(8,128)(2,1)S(1)}, u32[]{:S(2)}, u32[]{:S(2)}) async-start(bf16[128,8,256]{2,1,0:T(8,128)(2,1)} %bitcast.5), calls=%async_computation.1 | async-start | bytes 1048576 | tf_op jit(solution)/shard_map/all_to_all | solution.py:445
  34.4 0.0 copy-done.12
  34.4 0.2 rev.3.flipped_ref
  34.6 0.3 tables.1
  34.9 0.0 copy-start.3
  34.9 0.8 copy-done.3
  35.7 12.6 %all-to-all-done.1 = bf16[128,8,256]{2,1,0:T(8,128)(2,1)S(1)} async-done(((bf16[128,8,256]{2,1,0:T(8,128)(2,1)}), bf16[128,8,256]{2,1,0:T(8,128)(2,1)S(1)}, u32[]{:S(2)}, u32[]{:S(2)}) %all-to-all-start.1) | async-done | bytes 524320 | tf_op jit(solution)/shard_map/all_to_all | solution.py:445
  48.3 0.5 compact.1.refs_9_
  48.8 0.6 collective-permute-start.5
  49.4 2.2 %collective-permute-start.4 = (bf16[256,512]{1,0:T(8,128)(2,1)S(1)}, bf16[256,512]{1,0:T(8,128)(2,1)S(1)}, u32[]{:S(2)}, u32[]{:S(2)}) collective-permute-start(bf16[256,512]{1,0:T(8,128)(2,1)S(1)} %compact.1.refs_9_), channel_id=1, source_target_pairs={{0,3},{1,0},{2,1},{3,2},{4,7},{5,4},{6,5},{7,6},{8,11},{9,8},{10,9... | collective-permute-start | bytes 786440 | tf_op jit(solution)/shard_map/ppermute | solution.py:475
  51.6 0.0 collective-permute-start.3
  51.6 0.3 collective-permute-start
  51.9 2.4 %collective-permute-start.1 = (s32[2,384]{1,0:T(2,128)S(1)}, s32[2,384]{1,0:T(2,128)S(1)}, u32[]{:S(2)}, u32[]{:S(2)}) collective-permute-start(s32[2,384]{1,0:T(2,128)S(1)} %get-tuple-element.17), channel_id=1, source_target_pairs={{0,3},{1,0},{2,1},{3,2},{4,7},{5,4},{6,5},{7,6},{8,11},{9,8},{10,9... | collective-permute-start | bytes 9224 | tf_op jit(solution)/shard_map/ppermute | solution.py:469
  54.3 10.0 %collective-permute-done.refs_2_.refs_6_ = s32[2,384]{1,0:T(2,128)S(1)} collective-permute-done((s32[2,384]{1,0:T(2,128)S(1)}, s32[2,384]{1,0:T(2,128)S(1)}, u32[]{:S(2)}, u32[]{:S(2)}) %collective-permute-start) | collective-permute-done | bytes 3104 | tf_op jit(solution)/shard_map/ppermute | solution.py:469
  64.3 0.5 collective-permute-start.2
  64.8 0.0 collective-permute-done.1.refs_3_.refs_7_
  64.8 3.5 %collective-permute-done.2.refs_4_.refs_8_ = s32[2,384]{1,0:T(2,128)S(1)} collective-permute-done((s32[2,384]{1,0:T(2,128)S(1)}, s32[2,384]{1,0:T(2,128)S(1)}, u32[]{:S(2)}, u32[]{:S(2)}) %collective-permute-start.2) | collective-permute-done | bytes 3104 | tf_op jit(solution)/shard_map/ppermute | solution.py:469
  68.3 0.0 collective-permute-done.5.refs_12_
  68.3 0.0 collective-permute-done.4.refs_11_
  68.3 0.0 collective-permute-done.3.refs_10_
  68.3 0.0 copy-done
  68.3 0.0 copy-done.2
  68.3 0.0 copy-done.5
  68.3 0.0 copy-done.7
  68.3 0.0 copy-done.8
  68.3 0.0 copy-start.4
  68.3 1.0 copy-done.4
  69.4 38.7 %layer.1 = (bf16[8,256,512]{2,1,0:T(8,128)(2,1)}, bf16[256,512]{1,0:T(8,128)(2,1)S(1)}, bf16[256,512]{1,0:T(8,128)(2,1)S(1)}, bf16[256,512]{1,0:T(8,128)(2,1)S(1)}, bf16[256,512]{1,0:T(8,128)(2,1)S(1)}) custom-call(s32[1]{0:T(128)} %bitcast.seq_ref.refs_0_, s32[2,384]{1,0:T(2,128)S(1)} %get-tuple-element.15.refs_1_.refs_5_, ...), custom_call_target="tpu_custom_call" | custom-call | tf_op jit(solution)/shard_map/layer/pallas_call | solution.py:347
  108.1 0.0 collective-permute-start.6
  108.1 1.5 %collective-permute-start.7 = (bf16[256,512]{1,0:T(8,128)(2,1)S(1)}, bf16[256,512]{1,0:T(8,128)(2,1)S(1)}, u32[]{:S(2)}, u32[]{:S(2)}) collective-permute-start(bf16[256,512]{1,0:T(8,128)(2,1)S(1)} %get-tuple-element.26), channel_id=1, source_target_pairs={{0,1},{1,2},{2,3},{3,0},{4,5},{5,6},{6,7},{7,4},{8,9},{9,10},{10,1... | collective-permute-start | bytes 786440 | tf_op jit(solution)/shard_map/ppermute | solution.py:497
  109.6 0.5 collective-permute-start.8
  110.0 4.3 %collective-permute-done.6.refs_1_ = bf16[256,512]{1,0:T(8,128)(2,1)S(1)} collective-permute-done((bf16[256,512]{1,0:T(8,128)(2,1)S(1)}, bf16[256,512]{1,0:T(8,128)(2,1)S(1)}, u32[]{:S(2)}, u32[]{:S(2)}) %collective-permute-start.6) | collective-permute-done | bytes 262176 | tf_op jit(solution)/shard_map/ppermute | solution.py:497
  114.4 1.3 collective-permute-done.7.refs_2_
  115.6 4.5 %collective-permute-done.8.refs_3_ = bf16[256,512]{1,0:T(8,128)(2,1)S(1)} collective-permute-done((bf16[256,512]{1,0:T(8,128)(2,1)S(1)}, bf16[256,512]{1,0:T(8,128)(2,1)S(1)}, u32[]{:S(2)}, u32[]{:S(2)}) %collective-permute-start.8) | collective-permute-done | bytes 262176 | tf_op jit(solution)/shard_map/ppermute | solution.py:497
  120.1 1.3 expand.1
  121.4 7.7 %all-to-all-start.2 = ((bf16[128,8,256]{2,1,0:T(8,128)(2,1)}), bf16[128,8,256]{2,1,0:T(8,128)(2,1)S(1)}, u32[]{:S(2)}, u32[]{:S(2)}) async-start(bf16[128,8,256]{2,1,0:T(8,128)(2,1)} %bitcast.10), calls=%async_computation.2 | async-start | bytes 1048576 | tf_op jit(solution)/shard_map/all_to_all | solution.py:445
  129.1 0.3 asked_line.1.line_ref
  129.4 13.6 %all-to-all-done.2 = bf16[128,8,256]{2,1,0:T(8,128)(2,1)S(1)} async-done(((bf16[128,8,256]{2,1,0:T(8,128)(2,1)}), bf16[128,8,256]{2,1,0:T(8,128)(2,1)S(1)}, u32[]{:S(2)}, u32[]{:S(2)}) %all-to-all-start.2) | async-done | bytes 524320 | tf_op jit(solution)/shard_map/all_to_all | solution.py:445
  143.0 2.9 %scatter.1 = f32[1024,512]{1,0:T(8,128)} custom-call(s32[1,1024]{1,0:T(1,128)S(1)} %asked_line.1.line_ref, bf16[1024,256]{1,0:T(8,128)(2,1)S(1)} %bitcast.13), custom_call_target="tpu_custom_call" | custom-call | tf_op jit(solution)/shard_map/scatter/pallas_call | solution.py:429
Async XLA Ops:
  0.6 67.7 %copy-start = (bf16[8,256,512]{2,1,0:T(8,128)(2,1)S(1)}, bf16[8,256,512]{2,1,0:T(8,128)(2,1)}, u32[]{:S(2)}) copy-start(bf16[8,256,512]{2,1,0:T(8,128)(2,1)} %refs_13_.1) | copy-start | bytes 6291460
  0.6 0.8 copy-start.6
  1.5 0.7 copy-start.9
  2.2 0.7 copy-start.10
  2.8 0.7 copy-start.11
  25.8 1.2 copy-start.1
  27.0 7.4 %copy-start.12 = (f32[4,256]{1,0:T(4,128)S(1)}, f32[4,256]{1,0:T(4,128)}, u32[]{:S(2)}) copy-start(f32[4,256]{1,0:T(4,128)} %param.22) | copy-start | bytes 12292
  27.0 41.3 %copy-start.2 = (bf16[512,512]{1,0:T(8,128)(2,1)S(1)}, bf16[512,512]{1,0:T(8,128)(2,1)}, u32[]{:S(2)}) copy-start(bf16[512,512]{1,0:T(8,128)(2,1)} %refs_18_.1) | copy-start | bytes 1572868
  27.0 41.3 %copy-start.5 = (f32[2048]{0:T(1024)S(1)}, f32[2048]{0:T(1024)}, u32[]{:S(2)}) copy-start(f32[2048]{0:T(1024)} %param.18) | copy-start | bytes 24580
  27.0 41.3 %copy-start.7 = (f32[512]{0:T(512)S(1)}, f32[512]{0:T(512)}, u32[]{:S(2)}) copy-start(f32[512]{0:T(512)} %param.19) | copy-start | bytes 6148
  27.0 41.3 %copy-start.8 = (f32[512]{0:T(512)S(1)}, f32[512]{0:T(512)}, u32[]{:S(2)}) copy-start(f32[512]{0:T(512)} %param.20) | copy-start | bytes 6148
  30.2 18.2 %all-to-all-start.1 = ((bf16[128,8,256]{2,1,0:T(8,128)(2,1)}), bf16[128,8,256]{2,1,0:T(8,128)(2,1)S(1)}, u32[]{:S(2)}, u32[]{:S(2)}) async-start(bf16[128,8,256]{2,1,0:T(8,128)(2,1)} %bitcast.5), calls=%async_computation.1 | async-start | bytes 1048576 | tf_op jit(solution)/shard_map/all_to_all | solution.py:445
  34.9 0.8 copy-start.3
  48.8 19.4 %collective-permute-start.5 = (bf16[256,512]{1,0:T(8,128)(2,1)S(1)}, bf16[256,512]{1,0:T(8,128)(2,1)S(1)}, u32[]{:S(2)}, u32[]{:S(2)}) collective-permute-start(bf16[256,512]{1,0:T(8,128)(2,1)S(1)} %compact.1.refs_9_), channel_id=1, source_target_pairs={{0,2},{1,3},{2,0},{3,1},{4,6},{5,7},{6,4},{7,5},{8,10},{9,11},{10,... | collective-permute-start | bytes 786440 | tf_op jit(solution)/shard_map/ppermute | solution.py:475
  49.4 18.9 %collective-permute-start.4 = (bf16[256,512]{1,0:T(8,128)(2,1)S(1)}, bf16[256,512]{1,0:T(8,128)(2,1)S(1)}, u32[]{:S(2)}, u32[]{:S(2)}) collective-permute-start(bf16[256,512]{1,0:T(8,128)(2,1)S(1)} %compact.1.refs_9_), channel_id=1, source_target_pairs={{0,3},{1,0},{2,1},{3,2},{4,7},{5,4},{6,5},{7,6},{8,11},{9,8},{10,9... | collective-permute-start | bytes 786440 | tf_op jit(solution)/shard_map/ppermute | solution.py:475
  51.6 16.7 %collective-permute-start.3 = (bf16[256,512]{1,0:T(8,128)(2,1)S(1)}, bf16[256,512]{1,0:T(8,128)(2,1)S(1)}, u32[]{:S(2)}, u32[]{:S(2)}) collective-permute-start(bf16[256,512]{1,0:T(8,128)(2,1)S(1)} %compact.1.refs_9_), channel_id=1, source_target_pairs={{0,1},{1,2},{2,3},{3,0},{4,5},{5,6},{6,7},{7,4},{8,9},{9,10},{10,1... | collective-permute-start | bytes 786440 | tf_op jit(solution)/shard_map/ppermute | solution.py:475
  51.6 12.7 %collective-permute-start = (s32[2,384]{1,0:T(2,128)S(1)}, s32[2,384]{1,0:T(2,128)S(1)}, u32[]{:S(2)}, u32[]{:S(2)}) collective-permute-start(s32[2,384]{1,0:T(2,128)S(1)} %get-tuple-element.16), channel_id=1, source_target_pairs={{0,1},{1,2},{2,3},{3,0},{4,5},{5,6},{6,7},{7,4},{8,9},{9,10},{10,1... | collective-permute-start | bytes 9224 | tf_op jit(solution)/shard_map/ppermute | solution.py:469
  51.9 12.9 %collective-permute-start.1 = (s32[2,384]{1,0:T(2,128)S(1)}, s32[2,384]{1,0:T(2,128)S(1)}, u32[]{:S(2)}, u32[]{:S(2)}) collective-permute-start(s32[2,384]{1,0:T(2,128)S(1)} %get-tuple-element.17), channel_id=1, source_target_pairs={{0,3},{1,0},{2,1},{3,2},{4,7},{5,4},{6,5},{7,6},{8,11},{9,8},{10,9... | collective-permute-start | bytes 9224 | tf_op jit(solution)/shard_map/ppermute | solution.py:469
  64.3 4.0 %collective-permute-start.2 = (s32[2,384]{1,0:T(2,128)S(1)}, s32[2,384]{1,0:T(2,128)S(1)}, u32[]{:S(2)}, u32[]{:S(2)}) collective-permute-start(s32[2,384]{1,0:T(2,128)S(1)} %get-tuple-element.18), channel_id=1, source_target_pairs={{0,2},{1,3},{2,0},{3,1},{4,6},{5,7},{6,4},{7,5},{8,10},{9,11},{10,... | collective-permute-start | bytes 9224 | tf_op jit(solution)/shard_map/ppermute | solution.py:469
  68.3 1.0 copy-start.4
  108.1 6.2 %collective-permute-start.6 = (bf16[256,512]{1,0:T(8,128)(2,1)S(1)}, bf16[256,512]{1,0:T(8,128)(2,1)S(1)}, u32[]{:S(2)}, u32[]{:S(2)}) collective-permute-start(bf16[256,512]{1,0:T(8,128)(2,1)S(1)} %get-tuple-element.25), channel_id=1, source_target_pairs={{0,3},{1,0},{2,1},{3,2},{4,7},{5,4},{6,5},{7,6},{8,11},{9,8},{10,9... | collective-permute-start | bytes 786440 | tf_op jit(solution)/shard_map/ppermute | solution.py:497
  108.1 7.5 %collective-permute-start.7 = (bf16[256,512]{1,0:T(8,128)(2,1)S(1)}, bf16[256,512]{1,0:T(8,128)(2,1)S(1)}, u32[]{:S(2)}, u32[]{:S(2)}) collective-permute-start(bf16[256,512]{1,0:T(8,128)(2,1)S(1)} %get-tuple-element.26), channel_id=1, source_target_pairs={{0,1},{1,2},{2,3},{3,0},{4,5},{5,6},{6,7},{7,4},{8,9},{9,10},{10,1... | collective-permute-start | bytes 786440 | tf_op jit(solution)/shard_map/ppermute | solution.py:497
  109.6 10.5 %collective-permute-start.8 = (bf16[256,512]{1,0:T(8,128)(2,1)S(1)}, bf16[256,512]{1,0:T(8,128)(2,1)S(1)}, u32[]{:S(2)}, u32[]{:S(2)}) collective-permute-start(bf16[256,512]{1,0:T(8,128)(2,1)S(1)} %get-tuple-element.27), channel_id=1, source_target_pairs={{0,2},{1,3},{2,0},{3,1},{4,6},{5,7},{6,4},{7,5},{8,10},{9,11},{10,... | collective-permute-start | bytes 786440 | tf_op jit(solution)/shard_map/ppermute | solution.py:497
  121.4 21.6 %all-to-all-start.2 = ((bf16[128,8,256]{2,1,0:T(8,128)(2,1)}), bf16[128,8,256]{2,1,0:T(8,128)(2,1)S(1)}, u32[]{:S(2)}, u32[]{:S(2)}) async-start(bf16[128,8,256]{2,1,0:T(8,128)(2,1)} %bitcast.10), calls=%async_computation.2 | async-start | bytes 1048576 | tf_op jit(solution)/shard_map/all_to_all | solution.py:445

commit v2 on v1

--- a/solution.py
+++ b/solution.py
@@ -43,7 +43,7 @@
 
 
 def params(**kw):
-    return pltpu.CompilerParams(vmem_limit_bytes=48 << 20, **kw)
+    return pltpu.CompilerParams(vmem_limit_bytes=24 << 20, **kw)
 
 
 def pack_kernel(assign_ref, len_ref, seq_ref, ids_ref, inv_ref, req_ref, pos_ref, *msg_refs):
@@ -446,10 +446,10 @@
     return got.reshape(x.shape)
 
 
-PLANS = (((0, 1, 3, 2), (0, 1)),)
-
-
-def shards(
+PLANS = (((0,), (0,)), ((1, 3, 2), (0, 1)), ((0,), (1,)))
+
+
+def program(
     item_table,
     unique_ids,
     inverse,
@@ -470,6 +470,7 @@
     bias, pos_rows = tables(position_bias, pos)
     answer = answer_rows(asked, item_table)
     got = exchange(answer, (DEVICES, 8, D // 2))
+    got, *msgs = lax.optimization_barrier((got, *msgs))
     line = asked_line(asked)
     own = compact(pos_rows, got)
     rows = [own] + [lax.ppermute(own, "seq", ring(d)) for d in (1, 2, 3)]
@@ -516,4 +517,4 @@
         P(both, None, None),
     )
     out_specs = (P(both, None, None), P(both, None))
-    return jax.shard_map(shards, mesh=mesh, in_specs=in_specs, out_specs=out_specs, check_vma=False)
+    return jax.shard_map(program, mesh=mesh, in_specs=in_specs, out_specs=out_specs, check_vma=False)

time: 146 us -> 134 us (0.918)
  waiting for transfers between devices: 49.9 us -> 35.1 us
  Pallas kernels: 48.4 us -> 51 us
    ppermute x9, waiting for transfers between devices: 23.6 us -> 15.9 us  [the longest x3 7.49 us: program(): sums.append(part if d == 0 else lax.ppermute(part, 'seq', ring(-d)))]
    all_to_all x2, waiting for transfers between devices: 26.3 us -> 19.2 us  [exchange(): lax.all_to_all(x.reshape(shape), ('emb', 'seq'), split_axis=0, concat_axi...]
    ppermute x9, starting transfers between devices: 7.86 us -> 9.95 us  [the longest x3 5.03 us: program(): lax.ppermute(sent[d], 'seq', ring(d))]
    all_to_all x2, starting transfers between devices: 11.9 us -> 10.2 us  [exchange(): lax.all_to_all(x.reshape(shape), ('emb', 'seq'), split_axis=0, concat_axi...]
    pallas_call x1 -> x3, Pallas kernels: 38.7 us -> 40.2 us  [layer(): pl.pallas_call(functools.partial(layer_kernel, plan, prior is not None),...]
    unnamed x26 -> x24, local copies, waits for them, and re-layouts: 5.9 us -> 5.66 us
  transfers between devices with their start and end apart: 11 -> 11, of which waited for: 7 -> 7; matrix products, arithmetic and copies ran while one was open for 0% -> 0% of each run, Pallas kernels for 0% -> 8%
where the time goes in v2:
time: 134 us
  Pallas kernels  51 us (38%)
  waiting for transfers between devices  35.1 us (26%)
  blocking collectives  21 us (16%)
  starting transfers between devices  20.1 us (15%)
  local copies, waits for them, and re-layouts  5.84 us (4%)
    pallas_call x3, Pallas kernels, layer(): pl.pallas_call(functools.partial(layer_kernel, plan, prior is not None),...  40.2 us
    all_to_all x1, blocking collectives, exchange(): lax.all_to_all(x.reshape(shape), ('emb', 'seq'), split_axis=0, concat_axi...  21 us
    all_to_all x2, waiting for transfers between devices, exchange(): lax.all_to_all(x.reshape(shape), ('emb', 'seq'), split_axis=0, concat_axi...  19.2 us
    all_to_all x2, starting transfers between devices, exchange(): lax.all_to_all(x.reshape(shape), ('emb', 'seq'), split_axis=0, concat_axi...  10.2 us
    ppermute x3, waiting for transfers between devices, program(): sums.append(part if d == 0 else lax.ppermute(part, 'seq', ring(-d)))  7.49 us
    unnamed x24, local copies, waits for them, and re-layouts  5.66 us
    ppermute x3, waiting for transfers between devices, program(): rows = [own] + [lax.ppermute(own, 'seq', ring(d)) for d in (1, 2, 3)]  5.58 us
    ppermute x3, starting transfers between devices, program(): lax.ppermute(sent[d], 'seq', ring(d))  5.03 us
  transfers between devices with their start and end apart: 11, of which 7 were waited for; matrix products, arithmetic and copies ran while one was open for 0% of the time, Pallas kernels for 8%

profile of v2, /device:TPU:1, one launch (start us, length us, event | category | flops | bytes accessed | tf_op | source)
XLA Modules:
  0.0 133.9 jit_solution(5281811282441943680)
XLA Ops:
  0.6 0.0 copy-start
  0.6 0.0 copy-start.2
  0.7 0.0 copy-start.7
  0.7 0.8 copy-done.7
  1.5 0.0 copy-start.8
  1.5 0.7 copy-done.8
  2.2 0.0 copy-start.9
  2.2 0.7 copy-done.9
  2.8 0.0 copy-start.10
  2.8 0.7 copy-done.10
  3.5 1.3 pack.1
  4.8 21.0 %all_to_all.15 = s32[128,1,4]{2,1,0:T(1,128)S(1)} all-to-all(s32[128,1,4]{2,1,0:T(1,128)S(1)} %bitcast.19), channel_id=1, replica_groups=mesh['emb'=32,'seq'=4] {'emb','seq'}, dimensions={0} | all-to-all | bytes 4096 | tf_op jit(solution)/shard_map/all_to_all | solution.py:445
  25.8 0.0 copy-start.3
  25.8 1.2 copy-done.3
  27.0 0.0 copy-start.11
  27.0 0.0 copy-start.4
  27.0 0.0 copy-start.5
  27.0 0.0 copy-start.6
  27.0 3.1 %answer.1 = bf16[1024,256]{1,0:T(8,128)(2,1)} custom-call(s32[128,4]{1,0:T(8,128)S(1)} %bitcast.14, bf16[1024,512]{1,0:T(8,128)(2,1)S(1)} %copy-done.3), custom_call_target="tpu_custom_call" | custom-call | tf_op jit(solution)/shard_map/answer/pallas_call | solution.py:146
  30.2 5.2 %all-to-all-start.1 = ((bf16[128,8,256]{2,1,0:T(8,128)(2,1)}), bf16[128,8,256]{2,1,0:T(8,128)(2,1)}, u32[]{:S(2)}, u32[]{:S(2)}) async-start(bf16[128,8,256]{2,1,0:T(8,128)(2,1)} %bitcast.5), calls=%async_computation.1 | async-start | bytes 1048576 | tf_op jit(solution)/shard_map/all_to_all | solution.py:445
  35.3 1.4 %collective-permute-start = (s32[2,384]{1,0:T(2,128)S(1)}, s32[2,384]{1,0:T(2,128)S(1)}, u32[]{:S(2)}, u32[]{:S(2)}) collective-permute-start(s32[2,384]{1,0:T(2,128)S(1)} %get-tuple-element.25), channel_id=1, source_target_pairs={{0,1},{1,2},{2,3},{3,0},{4,5},{5,6},{6,7},{7,4},{8,9},{9,10},{10,1... | collective-permute-start | bytes 9224 | tf_op jit(solution)/shard_map/ppermute | solution.py:469
  36.8 2.4 %collective-permute-start.1 = (s32[2,384]{1,0:T(2,128)S(1)}, s32[2,384]{1,0:T(2,128)S(1)}, u32[]{:S(2)}, u32[]{:S(2)}) collective-permute-start(s32[2,384]{1,0:T(2,128)S(1)} %get-tuple-element.26), channel_id=1, source_target_pairs={{0,2},{1,3},{2,0},{3,1},{4,6},{5,7},{6,4},{7,5},{8,10},{9,11},{10,... | collective-permute-start | bytes 9224 | tf_op jit(solution)/shard_map/ppermute | solution.py:469
  39.2 1.2 collective-permute-start.2
  40.4 0.0 copy-done.11
  40.4 0.2 rev.3.flipped_ref
  40.5 0.3 tables.1
  40.8 1.8 %collective-permute-done.refs_1_.refs_4_ = s32[2,384]{1,0:T(2,128)S(1)} collective-permute-done((s32[2,384]{1,0:T(2,128)S(1)}, s32[2,384]{1,0:T(2,128)S(1)}, u32[]{:S(2)}, u32[]{:S(2)}) %collective-permute-start) | collective-permute-done | bytes 3104 | tf_op jit(solution)/shard_map/ppermute | solution.py:469
  42.7 1.0 collective-permute-done.1.refs_3_.refs_6_
  43.6 0.0 collective-permute-done.2.refs_2_.refs_5_
  43.6 5.5 %all-to-all-done.1 = bf16[128,8,256]{2,1,0:T(8,128)(2,1)} async-done(((bf16[128,8,256]{2,1,0:T(8,128)(2,1)}), bf16[128,8,256]{2,1,0:T(8,128)(2,1)}, u32[]{:S(2)}, u32[]{:S(2)}) %all-to-all-start.1) | async-done | bytes 524320 | tf_op jit(solution)/shard_map/all_to_all | solution.py:445
  49.1 1.5 %compact.1.refs_3_ = bf16[256,512]{1,0:T(8,128)(2,1)S(1)} custom-call(s32[256,128]{1,0:T(8,128)S(1)} %get-tuple-element.30.pos_ref, bf16[1024,256]{1,0:T(8,128)(2,1)} %bitcast.6.got_ref), custom_call_target="tpu_custom_call" | custom-call | tf_op jit(solution)/shard_map/compact/pallas_call | solution.py:163
  50.6 0.5 collective-permute-start.5
  51.2 2.2 %collective-permute-start.4 = (bf16[256,512]{1,0:T(8,128)(2,1)S(1)}, bf16[256,512]{1,0:T(8,128)(2,1)S(1)}, u32[]{:S(2)}, u32[]{:S(2)}) collective-permute-start(bf16[256,512]{1,0:T(8,128)(2,1)S(1)} %compact.1.refs_3_), channel_id=1, source_target_pairs={{0,3},{1,0},{2,1},{3,2},{4,7},{5,4},{6,5},{7,6},{8,11},{9,8},{10,9... | collective-permute-start | bytes 786440 | tf_op jit(solution)/shard_map/ppermute | solution.py:476
  53.4 0.0 collective-permute-start.3
  53.4 0.0 copy-done
  53.4 0.0 copy-done.2
  53.4 0.0 copy-done.4
  53.4 0.0 copy-done.5
  53.4 0.0 copy-done.6
  53.4 0.0 copy-start.1
  53.4 1.6 %copy-done.1 = bf16[512,2048]{1,0:T(8,128)(2,1)S(1)} copy-done((bf16[512,2048]{1,0:T(8,128)(2,1)S(1)}, bf16[512,2048]{1,0:T(8,128)(2,1)}, u32[]{:S(2)}) %copy-start.1) | copy-done | bytes 2097176
  55.0 5.4 %layer.3 = (bf16[8,256,512]{2,1,0:T(8,128)(2,1)}, bf16[256,512]{1,0:T(8,128)(2,1)S(1)}) custom-call(s32[1]{0:T(128)} %bitcast.seq_ref.refs_0_, s32[2,384]{1,0:T(2,128)S(1)} %get-tuple-element.28.refs_1_.refs_2_, s32[2,384]{1,0:T(2,128)S(1)} %get-tuple-element.28.refs_1_.refs_2_, bf16[256,512]{1,0:T(8,128)(2,1)S(1)} %compact.1.refs_3_, ...), custom_call_target="tpu_custom_call" | custom-call | tf_op jit(solution)/shard_map/layer/pallas_call | solution.py:347
  60.5 0.0 collective-permute-done.5.refs_9_
  60.5 3.2 %collective-permute-done.4.refs_8_ = bf16[256,512]{1,0:T(8,128)(2,1)S(1)} collective-permute-done((bf16[256,512]{1,0:T(8,128)(2,1)S(1)}, bf16[256,512]{1,0:T(8,128)(2,1)S(1)}, u32[]{:S(2)}, u32[]{:S(2)}) %collective-permute-start.4) | collective-permute-done | bytes 262176 | tf_op jit(solution)/shard_map/ppermute | solution.py:476
  63.7 2.4 %collective-permute-done.3.refs_7_ = bf16[256,512]{1,0:T(8,128)(2,1)S(1)} collective-permute-done((bf16[256,512]{1,0:T(8,128)(2,1)S(1)}, bf16[256,512]{1,0:T(8,128)(2,1)S(1)}, u32[]{:S(2)}, u32[]{:S(2)}) %collective-permute-start.3) | collective-permute-done | bytes 262176 | tf_op jit(solution)/shard_map/ppermute | solution.py:476
  66.0 29.5 %layer.4 = (bf16[8,256,512]{2,1,0:T(8,128)(2,1)}, bf16[256,512]{1,0:T(8,128)(2,1)S(1)}, bf16[256,512]{1,0:T(8,128)(2,1)S(1)}, bf16[256,512]{1,0:T(8,128)(2,1)S(1)}) custom-call(s32[1]{0:T(128)} %bitcast.seq_ref.refs_0_, s32[2,384]{1,0:T(2,128)S(1)} %collective-permute-done.refs_1_.refs_4_, ...), custom_call_target="tpu_custom_call", output_to_operand_aliasing={{0}: (17, {})} | custom-call | tf_op jit(solution)/shard_map/layer/pallas_call | solution.py:347
  95.6 1.0 collective-permute-start.6
  96.5 0.5 collective-permute-start.7
  97.0 0.7 collective-permute-start.8
  97.7 5.3 %layer.5 = (bf16[8,256,512]{2,1,0:T(8,128)(2,1)}, bf16[256,512]{1,0:T(8,128)(2,1)S(1)}) custom-call(s32[1]{0:T(128)} %bitcast.seq_ref.refs_0_, s32[2,384]{1,0:T(2,128)S(1)} %get-tuple-element.28.refs_1_.refs_2_, s32[2,384]{1,0:T(2,128)S(1)} %get-tuple-element.28.refs_1_.refs_2_, ...), custom_call_target="tpu_custom_call", output_to_operand_aliasing={{0}: (11, {})} | custom-call | tf_op jit(solution)/shard_map/layer/pallas_call | solution.py:347
  103.0 0.0 collective-permute-done.6.refs_1_
  103.0 7.5 %collective-permute-done.7.refs_2_ = bf16[256,512]{1,0:T(8,128)(2,1)S(1)} collective-permute-done((bf16[256,512]{1,0:T(8,128)(2,1)S(1)}, bf16[256,512]{1,0:T(8,128)(2,1)S(1)}, u32[]{:S(2)}, u32[]{:S(2)}) %collective-permute-start.7) | collective-permute-done | bytes 262176 | tf_op jit(solution)/shard_map/ppermute | solution.py:498
  110.5 0.0 collective-permute-done.8.refs_3_
  110.5 1.4 %expand.1 = bf16[1024,256]{1,0:T(8,128)(2,1)} custom-call(s32[1,256]{1,0:T(1,128)S(1)} %get-tuple-element.29.pos_ref, bf16[256,512]{1,0:T(8,128)(2,1)S(1)} %get-tuple-element.39.refs_0_, bf16[256,512]{1,0:T(8,128)(2,1)S(1)} %collective-permute-done.6.refs_1_, bf16[256,512]{1,0:T(8,128)(2,1)S(1)} %collective-permute-done.7.refs_2_, ...), custom_call_target="tpu_custom_call" | custom-call | tf_op jit(solution)/shard_map/expand/pallas_call | solution.py:388
  111.8 5.0 %all-to-all-start.2 = ((bf16[128,8,256]{2,1,0:T(8,128)(2,1)}), bf16[128,8,256]{2,1,0:T(8,128)(2,1)S(1)}, u32[]{:S(2)}, u32[]{:S(2)}) async-start(bf16[128,8,256]{2,1,0:T(8,128)(2,1)} %bitcast.10), calls=%async_computation.2 | async-start | bytes 1048576 | tf_op jit(solution)/shard_map/all_to_all | solution.py:445
  116.9 0.3 asked_line.1.line_ref
  117.1 13.8 %all-to-all-done.2 = bf16[128,8,256]{2,1,0:T(8,128)(2,1)S(1)} async-done(((bf16[128,8,256]{2,1,0:T(8,128)(2,1)}), bf16[128,8,256]{2,1,0:T(8,128)(2,1)S(1)}, u32[]{:S(2)}, u32[]{:S(2)}) %all-to-all-start.2) | async-done | bytes 524320 | tf_op jit(solution)/shard_map/all_to_all | solution.py:445
  130.9 2.9 %scatter.1 = f32[1024,512]{1,0:T(8,128)} custom-call(s32[1,1024]{1,0:T(1,128)S(1)} %asked_line.1.line_ref, bf16[1024,256]{1,0:T(8,128)(2,1)S(1)} %bitcast.13), custom_call_target="tpu_custom_call" | custom-call | tf_op jit(solution)/shard_map/scatter/pallas_call | solution.py:429
Async XLA Ops:
  0.6 52.8 %copy-start = (bf16[8,256,512]{2,1,0:T(8,128)(2,1)S(1)}, bf16[8,256,512]{2,1,0:T(8,128)(2,1)}, u32[]{:S(2)}) copy-start(bf16[8,256,512]{2,1,0:T(8,128)(2,1)} %refs_4_.3) | copy-start | bytes 6291460
  0.6 52.8 %copy-start.2 = (bf16[512,512]{1,0:T(8,128)(2,1)S(1)}, bf16[512,512]{1,0:T(8,128)(2,1)}, u32[]{:S(2)}) copy-start(bf16[512,512]{1,0:T(8,128)(2,1)} %refs_9_.3) | copy-start | bytes 1572868
  0.7 0.8 copy-start.7
  1.5 0.7 copy-start.8
  2.2 0.7 copy-start.9
  2.8 0.7 copy-start.10
  25.8 1.2 copy-start.3
  27.0 13.3 %copy-start.11 = (f32[4,256]{1,0:T(4,128)S(1)}, f32[4,256]{1,0:T(4,128)}, u32[]{:S(2)}) copy-start(f32[4,256]{1,0:T(4,128)} %param.22) | copy-start | bytes 12292
  27.0 26.4 %copy-start.4 = (f32[2048]{0:T(1024)S(1)}, f32[2048]{0:T(1024)}, u32[]{:S(2)}) copy-start(f32[2048]{0:T(1024)} %param.18) | copy-start | bytes 24580
  27.0 26.4 %copy-start.5 = (f32[512]{0:T(512)S(1)}, f32[512]{0:T(512)}, u32[]{:S(2)}) copy-start(f32[512]{0:T(512)} %param.19) | copy-start | bytes 6148
  27.0 26.4 %copy-start.6 = (f32[512]{0:T(512)S(1)}, f32[512]{0:T(512)}, u32[]{:S(2)}) copy-start(f32[512]{0:T(512)} %param.20) | copy-start | bytes 6148
  30.2 18.9 %all-to-all-start.1 = ((bf16[128,8,256]{2,1,0:T(8,128)(2,1)}), bf16[128,8,256]{2,1,0:T(8,128)(2,1)}, u32[]{:S(2)}, u32[]{:S(2)}) async-start(bf16[128,8,256]{2,1,0:T(8,128)(2,1)} %bitcast.5), calls=%async_computation.1 | async-start | bytes 1048576 | tf_op jit(solution)/shard_map/all_to_all | solution.py:445
  35.3 7.3 %collective-permute-start = (s32[2,384]{1,0:T(2,128)S(1)}, s32[2,384]{1,0:T(2,128)S(1)}, u32[]{:S(2)}, u32[]{:S(2)}) collective-permute-start(s32[2,384]{1,0:T(2,128)S(1)} %get-tuple-element.25), channel_id=1, source_target_pairs={{0,1},{1,2},{2,3},{3,0},{4,5},{5,6},{6,7},{7,4},{8,9},{9,10},{10,1... | collective-permute-start | bytes 9224 | tf_op jit(solution)/shard_map/ppermute | solution.py:469
  36.8 6.9 %collective-permute-start.1 = (s32[2,384]{1,0:T(2,128)S(1)}, s32[2,384]{1,0:T(2,128)S(1)}, u32[]{:S(2)}, u32[]{:S(2)}) collective-permute-start(s32[2,384]{1,0:T(2,128)S(1)} %get-tuple-element.26), channel_id=1, source_target_pairs={{0,2},{1,3},{2,0},{3,1},{4,6},{5,7},{6,4},{7,5},{8,10},{9,11},{10,... | collective-permute-start | bytes 9224 | tf_op jit(solution)/shard_map/ppermute | solution.py:469
  39.2 4.4 %collective-permute-start.2 = (s32[2,384]{1,0:T(2,128)S(1)}, s32[2,384]{1,0:T(2,128)S(1)}, u32[]{:S(2)}, u32[]{:S(2)}) collective-permute-start(s32[2,384]{1,0:T(2,128)S(1)} %get-tuple-element.27), channel_id=1, source_target_pairs={{0,3},{1,0},{2,1},{3,2},{4,7},{5,4},{6,5},{7,6},{8,11},{9,8},{10,9... | collective-permute-start | bytes 9224 | tf_op jit(solution)/shard_map/ppermute | solution.py:469
  50.6 9.8 %collective-permute-start.5 = (bf16[256,512]{1,0:T(8,128)(2,1)S(1)}, bf16[256,512]{1,0:T(8,128)(2,1)S(1)}, u32[]{:S(2)}, u32[]{:S(2)}) collective-permute-start(bf16[256,512]{1,0:T(8,128)(2,1)S(1)} %compact.1.refs_3_), channel_id=1, source_target_pairs={{0,2},{1,3},{2,0},{3,1},{4,6},{5,7},{6,4},{7,5},{8,10},{9,11},{10,... | collective-permute-start | bytes 786440 | tf_op jit(solution)/shard_map/ppermute | solution.py:476
  51.2 12.5 %collective-permute-start.4 = (bf16[256,512]{1,0:T(8,128)(2,1)S(1)}, bf16[256,512]{1,0:T(8,128)(2,1)S(1)}, u32[]{:S(2)}, u32[]{:S(2)}) collective-permute-start(bf16[256,512]{1,0:T(8,128)(2,1)S(1)} %compact.1.refs_3_), channel_id=1, source_target_pairs={{0,3},{1,0},{2,1},{3,2},{4,7},{5,4},{6,5},{7,6},{8,11},{9,8},{10,9... | collective-permute-start | bytes 786440 | tf_op jit(solution)/shard_map/ppermute | solution.py:476
  53.4 12.7 %collective-permute-start.3 = (bf16[256,512]{1,0:T(8,128)(2,1)S(1)}, bf16[256,512]{1,0:T(8,128)(2,1)S(1)}, u32[]{:S(2)}, u32[]{:S(2)}) collective-permute-start(bf16[256,512]{1,0:T(8,128)(2,1)S(1)} %compact.1.refs_3_), channel_id=1, source_target_pairs={{0,1},{1,2},{2,3},{3,0},{4,5},{5,6},{6,7},{7,4},{8,9},{9,10},{10,1... | collective-permute-start | bytes 786440 | tf_op jit(solution)/shard_map/ppermute | solution.py:476
  53.4 1.6 %copy-start.1 = (bf16[512,2048]{1,0:T(8,128)(2,1)S(1)}, bf16[512,2048]{1,0:T(8,128)(2,1)}, u32[]{:S(2)}) copy-start(bf16[512,2048]{1,0:T(8,128)(2,1)} %refs_5_.3) | copy-start | bytes 6291460
  95.6 7.4 %collective-permute-start.6 = (bf16[256,512]{1,0:T(8,128)(2,1)S(1)}, bf16[256,512]{1,0:T(8,128)(2,1)S(1)}, u32[]{:S(2)}, u32[]{:S(2)}) collective-permute-start(bf16[256,512]{1,0:T(8,128)(2,1)S(1)} %get-tuple-element.40), channel_id=1, source_target_pairs={{0,3},{1,0},{2,1},{3,2},{4,7},{5,4},{6,5},{7,6},{8,11},{9,8},{10,9... | collective-permute-start | bytes 786440 | tf_op jit(solution)/shard_map/ppermute | solution.py:498
  96.5 13.9 %collective-permute-start.7 = (bf16[256,512]{1,0:T(8,128)(2,1)S(1)}, bf16[256,512]{1,0:T(8,128)(2,1)S(1)}, u32[]{:S(2)}, u32[]{:S(2)}) collective-permute-start(bf16[256,512]{1,0:T(8,128)(2,1)S(1)} %get-tuple-element.41), channel_id=1, source_target_pairs={{0,1},{1,2},{2,3},{3,0},{4,5},{5,6},{6,7},{7,4},{8,9},{9,10},{10,1... | collective-permute-start | bytes 786440 | tf_op jit(solution)/shard_map/ppermute | solution.py:498
  97.0 13.4 %collective-permute-start.8 = (bf16[256,512]{1,0:T(8,128)(2,1)S(1)}, bf16[256,512]{1,0:T(8,128)(2,1)S(1)}, u32[]{:S(2)}, u32[]{:S(2)}) collective-permute-start(bf16[256,512]{1,0:T(8,128)(2,1)S(1)} %get-tuple-element.42), channel_id=1, source_target_pairs={{0,2},{1,3},{2,0},{3,1},{4,6},{5,7},{6,4},{7,5},{8,10},{9,11},{10,... | collective-permute-start | bytes 786440 | tf_op jit(solution)/shard_map/ppermute | solution.py:498
  111.8 19.1 %all-to-all-start.2 = ((bf16[128,8,256]{2,1,0:T(8,128)(2,1)}), bf16[128,8,256]{2,1,0:T(8,128)(2,1)S(1)}, u32[]{:S(2)}, u32[]{:S(2)}) async-start(bf16[128,8,256]{2,1,0:T(8,128)(2,1)} %bitcast.10), calls=%async_computation.2 | async-start | bytes 1048576 | tf_op jit(solution)/shard_map/all_to_all | solution.py:445

commit v3 on v2

--- a/solution.py
+++ b/solution.py
@@ -95,7 +95,7 @@
     )(assignment, lengths, seq, ids.reshape(1, UNIQ), inverse)
 
 
-def tables_kernel(flipped_ref, pos_ref, bias_ref, pos_rows_ref):
+def tables_kernel(flipped_ref, pos_ref, win_ref, wout_ref, bias_ref, pos_rows_ref, winb_ref, woutb_ref):
     i = iota((MAXLEN, MAXLEN), 0)
     j = iota((MAXLEN, MAXLEN), 1)
     for h in range(HEADS):
@@ -106,18 +106,24 @@
     pos = jnp.broadcast_to(pos_ref[...], (UNIQ, UNIQ)).astype(F32)
     col = jnp.sum(jnp.where(i == j, pos, 0.0), axis=1, keepdims=True)
     pos_rows_ref[...] = jnp.broadcast_to(col.astype(I32), (UNIQ, 128))
-
-
-def tables(position_bias, pos):
+    for c in range(16):
+        winb_ref[c] = win_ref[:, pl.ds(c * 128, 128)]
+    for c in range(4):
+        woutb_ref[c] = wout_ref[:, pl.ds(c * 128, 128)]
+
+
+def tables(position_bias, pos, proj_in, proj_out):
     return pl.pallas_call(
         tables_kernel,
         out_shape=[
             jax.ShapeDtypeStruct((HEADS, MAXLEN, 128), F32),
             jax.ShapeDtypeStruct((UNIQ, 128), I32),
+            jax.ShapeDtypeStruct((16, D, 128), BF),
+            jax.ShapeDtypeStruct((4, D, 128), BF),
         ],
         compiler_params=params(),
         name="tables",
-    )(position_bias[:, ::-1], pos)
+    )(position_bias[:, ::-1], pos, proj_in, proj_out)
 
 
 def asked_parts(asked_ref):
@@ -183,136 +189,184 @@
     return inv * (g - row_mean(g) - unit * row_mean(g * unit))
 
 
-def slot_body(size, count, ids, rows, cot, out_ref, acc_ref, fresh, refs):
-    (win_ref, bin_ref, gin_ref, gmid_ref, wout_ref, bias_ref, hid, slope, wts, wslope, dpre, mix) = refs
-    rowpos = iota((size, 1), 0)
-    valid = rowpos < count
-    ids_rows = jnp.broadcast_to(ids[:, :size], (8, size)).astype(F32)
-    ids_cols = ids_rows.T[:, :1].astype(I32)
-    pick = onehot((iota((size, UNIQ), 1) == ids_cols) & valid)
-    x = nn(pick, rows)
-    unit_in, inv_in = norm_parts(x)
-    normed = (unit_in * gin_ref[...]).astype(BF)
-    for c in range(4):
-        cols = pl.ds(c * D, D)
-        half = 0.5 * (nn(normed, win_ref[:, cols]) + bin_ref[:, cols])
-        up = 1.0 + jnp.tanh(half)
-        act = half * up
-        hid[:size, cols] = act.astype(BF)
-        slope[:size, cols] = 0.5 * (up + act * (2.0 - up))
-    per = jnp.where(valid, 1.0, 0.0) / count.astype(F32)
-    blocks = size // 128
-    for h in range(HEADS):
-        vcol, qcol, kcol = (pl.ds(D * g + h * HEAD, HEAD) for g in (1, 2, 3))
-        for bi in range(blocks):
-            rs = pl.ds(bi * 128, 128)
-            width = (bi + 1) * 128
-            if bi == 0:
-                bias = bias_ref[h, :128, :]
-            else:
-                bias = jnp.concatenate([bias_ref[h, 128:, :], bias_ref[h, :128, :]], axis=1)
-            half = nt(hid[rs, qcol], hid[:width, kcol]) * (0.5 * SCALE) + bias
+def chunks(size, step=64):
+    return [slice(r, r + step) for r in range(0, size, step)]
+
+
+def side(ref, first, count, rs=slice(None)):
+    return jnp.concatenate([ref[c, rs] for c in range(first, first + count)], axis=1)
+
+
+def lay(ref, rs, value):
+    for c in range(value.shape[1] // 128):
+        ref[c, rs] = value[:, c * 128 : (c + 1) * 128].astype(BF)
+
+
+def rows_body(segments, ids_of, rows, cot_ref, out_ref, acc_ref, fresh, refs):
+    (win_ref, bin_ref, gin_ref, gmid_ref, wout_ref, bias_ref) = refs[:6]
+    (hid, slope, wts, wslope, dpre, xs, unit_in, unit_mid, invs, narrow, wide) = refs[6:]
+    size = sum(seg[1] for seg in segments)
+    every = slice(0, size)
+    gin_half = 0.5 * gin_ref[...]
+    lines = []
+    for first, length, count, place in segments:
+        line = ids_of(place)[:, :length]
+        lines.append(jnp.where(iota((1, length), 1) < count, line, -1))
+    line = lines[0] if len(lines) == 1 else jnp.concatenate(lines, axis=1)
+    cols = jnp.broadcast_to(line, (8, size)).astype(F32).T[:, :1].astype(I32)
+    xs[:size] = nn(onehot(iota((size, UNIQ), 1) == cols), rows)
+    for rs in chunks(size):
+        unit, inv = norm_parts(xs[rs])
+        unit_in[rs] = unit
+        invs[rs] = jnp.broadcast_to(inv, (rs.stop - rs.start, 128))
+        lay(narrow, rs, unit * gin_half)
+    for c in (6, 7, 4, 5, 2, 3, 0, 1):
+        pre = nn(side(narrow, 0, 4, every), side(win_ref, 2 * c, 2))
+        for k in range(2):
+            blk = 2 * c + k
+            half = pre[:, k * 128 : (k + 1) * 128] + 0.5 * bin_ref[:, pl.ds(blk * 128, 128)]
             up = 1.0 + jnp.tanh(half)
             act = half * up
-            scale = per[bi * 128 : (bi + 1) * 128]
-            w = (act * scale).astype(BF)
-            wts[h, rs, :width] = w
-            wslope[h, rs, :width] = (up + act * (2.0 - up)) * (scale * (0.5 * SCALE))
-            mix[rs, pl.ds(h * HEAD, HEAD)] = nn(w, hid[:width, vcol])
-    unit_mid, inv_mid = norm_parts(mix[:size, :])
-    scaled = unit_mid * gmid_ref[...]
-    gate = hid[:size, :D].astype(F32)
-    gated = (scaled * gate).astype(BF)
-    result = x + nn(gated, wout_ref[...])
-    out_ref[0, :size, :] = jnp.where(valid, result, 0.0).astype(BF)
-    if size < MAXLEN:
-        out_ref[0, size:, :] = jnp.zeros((MAXLEN - size, D), BF)
-    grad = jnp.where(valid, cot.astype(F32), 0.0)
-    dgated = nt(grad.astype(BF), wout_ref[...]).astype(BF).astype(F32)
-    dgate = (dgated * scaled).astype(BF).astype(F32)
-    dpre[:size, :D] = (dgate * slope[:size, :D]).astype(BF)
-    dmix = norm_grad(dgated * gate * gmid_ref[...], unit_mid, inv_mid).astype(BF)
+            hid[blk, every] = act.astype(BF)
+            slope[blk, every] = (up + act * (2.0 - up)).astype(BF)
+    units = []
     for h in range(HEADS):
-        vcol, qcol, kcol = (pl.ds(D * g + h * HEAD, HEAD) for g in (1, 2, 3))
-        dv = [None] * blocks
-        dk = [None] * blocks
-        for bi in range(blocks):
-            rs = pl.ds(bi * 128, 128)
-            width = (bi + 1) * 128
-            dm = dmix[bi * 128 : (bi + 1) * 128, h * HEAD : (h + 1) * HEAD]
-            dw = nt(dm, hid[:width, vcol])
-            ds = (dw * wslope[h, rs, :width]).astype(BF)
-            dq = nn(ds, hid[:width, kcol]).astype(BF).astype(F32)
-            dpre[rs, qcol] = (dq * slope[rs, qcol]).astype(BF)
-            dvs = tn(wts[h, rs, :width], dm)
-            dks = tn(ds, hid[rs, qcol])
-            for bj in range(bi + 1):
-                part = slice(bj * 128, (bj + 1) * 128)
-                dv[bj] = dvs[part] if dv[bj] is None else dv[bj] + dvs[part]
-                dk[bj] = dks[part] if dk[bj] is None else dk[bj] + dks[part]
-        for bj in range(blocks):
-            rs = pl.ds(bj * 128, 128)
-            dpre[rs, vcol] = (dv[bj].astype(BF).astype(F32) * slope[rs, vcol]).astype(BF)
-            dpre[rs, kcol] = (dk[bj].astype(BF).astype(F32) * slope[rs, kcol]).astype(BF)
-    dnormed = nt(dpre[:size, :], win_ref[...]).astype(BF).astype(F32)
-    dx = norm_grad(dnormed * gin_ref[...], unit_in, inv_in)
-    token = (dx + grad).astype(BF)
-    back = onehot((iota((UNIQ, size), 0) == ids[:, :size]) & (iota((UNIQ, size), 1) < count))
-    sums = nn(back, token)
+        for first, length, count, place in segments:
+            for bi in range(length // 128):
+                units.append((h, first, bi, count))
+    for h, first, bi, count in units:
+        rs = slice(first + bi * 128, first + bi * 128 + 128)
+        per = jnp.where(
+            iota((128, 1), 0) + bi * 128 < count,
+            1.0 / jnp.full((1, 1), count, I32).astype(F32),
+            0.0,
+        )
+        for bj in range(bi + 1):
+            ks = slice(first + bj * 128, first + bj * 128 + 128)
+            bias = bias_ref[h, (bi - bj) * 128 : (bi - bj) * 128 + 128, :]
+            half = nt(hid[8 + h, rs], hid[12 + h, ks]) * (0.5 * SCALE) + bias
+            up = 1.0 + jnp.tanh(half)
+            act = half * up
+            wts[h, bj, rs] = (act * per).astype(BF)
+            wslope[h, bj, rs] = ((up + act * (2.0 - up)) * (per * (0.5 * SCALE))).astype(BF)
+    for h, first, bi, count in units:
+        rs = slice(first + bi * 128, first + bi * 128 + 128)
+        ks = slice(first, first + (bi + 1) * 128)
+        wide[rs, pl.ds(h * HEAD, HEAD)] = nn(side(wts.at[h], 0, bi + 1, rs), hid[4 + h, ks])
+    for rs in chunks(size):
+        unit, inv = norm_parts(wide[rs])
+        unit_mid[rs] = unit
+        lay(narrow, rs, unit * gmid_ref[...] * side(hid, 0, 4, rs).astype(F32))
+        wide[rs, :128] = jnp.broadcast_to(inv, (rs.stop - rs.start, 128))
+    result = nn(side(narrow, 0, 4, every), side(wout_ref, 0, 4))
+    for first, length, count, place in segments:
+        valid = iota((length, 1), 0) < count
+        rs = slice(first, first + length)
+        out_ref[place, :length, :] = jnp.where(valid, xs[rs] + result[rs], 0.0).astype(BF)
+        if length < MAXLEN:
+            out_ref[place, length:, :] = jnp.zeros((MAXLEN - length, D), BF)
+        lay(narrow, rs, jnp.where(valid, cot_ref[place, :length, :], jnp.zeros((), BF)))
+    xs[:size] = nt(side(narrow, 0, 4, every), side(wout_ref, 0, 4))
+    for rs in chunks(size):
+        unit = unit_mid[rs]
+        inv = wide[rs, :1]
+        grown = xs[rs] * gmid_ref[...]
+        scaled = grown * unit
+        for c in range(4):
+            dpre[c, rs] = scaled[:, c * 128 : (c + 1) * 128].astype(BF) * slope[c, rs]
+        lay(hid, rs, norm_grad(grown * side(hid, 0, 4, rs).astype(F32), unit, inv))
+    for h, first, bi, count in units:
+        rs = slice(first + bi * 128, first + bi * 128 + 128)
+        for bj in range(bi + 1):
+            ks = slice(first + bj * 128, first + bj * 128 + 128)
+            wslope[h, bj, rs] = nt(hid[h, rs], hid[4 + h, ks]).astype(BF) * wslope[h, bj, rs]
+    for h, first, bi, count in units:
+        rs = slice(first + bi * 128, first + bi * 128 + 128)
+        ks = slice(first, first + (bi + 1) * 128)
+        dq = nn(side(wslope.at[h], 0, bi + 1, rs), hid[12 + h, ks])
+        dpre[8 + h, rs] = dq.astype(BF) * slope[8 + h, rs]
+    for h in range(HEADS):
+        for first, length, count, place in segments:
+            for bj in range(length // 128):
+                ks = slice(first + bj * 128, first + bj * 128 + 128)
+                qs = slice(first + bj * 128, first + length)
+                dv = tn(wts[h, bj, qs], hid[h, qs])
+                dpre[4 + h, ks] = dv.astype(BF) * slope[4 + h, ks]
+                dk = tn(wslope[h, bj, qs], hid[8 + h, qs])
+                dpre[12 + h, ks] = dk.astype(BF) * slope[12 + h, ks]
+    wide[:size] = nt(side(dpre, 0, 16, every), side(win_ref, 0, 16))
+    for rs in chunks(size):
+        dx = norm_grad(wide[rs] * gin_half, unit_in[rs], invs[rs, :1])
+        lay(narrow, rs, dx + side(narrow, 0, 4, rs).astype(F32))
+    sums = nn(onehot(iota((UNIQ, size), 0) == line), side(narrow, 0, 4, every))
     acc_ref[...] = jnp.where(fresh, sums, sums + acc_ref[...])
 
 
 def layer_kernel(plan, aliased, *refs):
     deltas, each = plan
     n_src = len(deltas)
+    n_each = len(each)
     refs = list(refs)
-    seq_ref = refs.pop(0)
+    refs.pop(0)
     smsg = [refs.pop(0) for _ in range(n_src)]
     vmsg = [refs.pop(0) for _ in range(n_src)]
     rows_refs = [refs.pop(0) for _ in range(n_src)]
     cot_ref = refs.pop(0)
-    win_ref, bin_ref, gin_ref, gmid_ref, wout_ref, bias_ref = (refs.pop(0) for _ in range(6))
+    weights = [refs.pop(0) for _ in range(6)]
     if aliased:
         refs.pop(0)
     out_ref = refs.pop(0)
     part_refs = [refs.pop(0) for _ in range(n_src)]
     rows, ids_sc, acc = (refs.pop(0) for _ in range(3))
-    scratch = refs
-    step = pl.program_id(0)
-    src = step // len(each)
-    turn = step % len(each)
-    count = jnp.int32(0)
+    work = (*weights, *refs)
+    src = pl.program_id(0)
+    counts = []
+    for b in each:
+        count = smsg[0][b, MAXLEN]
+        for d in range(1, n_src):
+            count = jnp.where(src == d, smsg[d][b, MAXLEN], count)
+        counts.append(count)
     for d in range(n_src):
-        for t, b in enumerate(each):
-            here = (src == d) & (turn == t)
-            count = jnp.where(here, smsg[d][b, MAXLEN], count)
-
-            @pl.when(here)
+
+        @pl.when(src == d)
+        def _():
+            for t, b in enumerate(each):
+                ids_sc[t : t + 1, :] = vmsg[d][b : b + 1, :MAXLEN]
+            rows[...] = rows_refs[d][...]
+
+    def ids_of(place):
+        return ids_sc[pl.ds(place, 1), :]
+
+    def run(segments, fresh):
+        rows_body(segments, ids_of, rows[...], cot_ref, out_ref, acc, fresh, work)
+
+    def alone(place, count, fresh):
+        for size in (128, 256):
+
+            @pl.when((count <= 128) == (size == 128))
             def _():
-                ids_sc[...] = vmsg[d][b : b + 1, :MAXLEN]
-                if t == 0:
-                    rows[...] = rows_refs[d][...]
-
-    weights = (win_ref, bin_ref, gin_ref, gmid_ref, wout_ref, bias_ref, *scratch)
-    for size in (128, 256):
-
-        @pl.when((count <= 128) == (size == 128))
+                run([(0, size, count, place)], fresh)
+
+    if n_each == 1:
+        alone(0, counts[0], True)
+    else:
+        short = (counts[0] <= 128) & (counts[1] <= 128)
+
+        @pl.when(short)
         def _():
-            slot_body(
-                size,
-                count,
-                ids_sc[...],
-                rows[...],
-                cot_ref[0, :size, :],
-                out_ref,
-                acc,
-                turn == 0,
-                weights,
-            )
+            run([(0, 128, counts[0], 0), (128, 128, counts[1], 1)], True)
+
+        @pl.when(jnp.logical_not(short))
+        def _():
+            def one(t, carry):
+                alone(t, jnp.where(t == 0, counts[0], counts[1]), t == 0)
+                return carry
+
+            lax.fori_loop(0, 2, one, 0)
 
     for d in range(n_src):
 
-        @pl.when((src == d) & (turn == len(each) - 1))
+        @pl.when(src == d)
         def _():
             part_refs[d][...] = acc[...].astype(BF)
 
@@ -323,20 +377,16 @@
     n_each = len(each)
 
     def slot(i, seq_ref):
-        src = i // n_each
         delta = deltas[0]
         for d in range(1, n_src):
-            delta = jnp.where(src == d, deltas[d], delta)
-        turn = i % n_each
-        b = each[0]
-        for t in range(1, n_each):
-            b = jnp.where(turn == t, each[t], b)
-        return ((seq_ref[0] - delta + 4) % 4) * 2 + b, 0, 0
+            delta = jnp.where(i == d, deltas[d], delta)
+        source = (seq_ref[0] - delta + 4) % 4
+        return (source if n_each == 2 else source * 2 + each[0]), 0, 0
 
     whole = lambda a: pl.BlockSpec(a.shape, lambda i, s, n=a.ndim: (0,) * n, pipeline_mode=pl.Buffered(1))
     smem = pl.BlockSpec(memory_space=pltpu.SMEM)
     in_specs = [smem] * n_src + [whole(m) for m in msgs] + [whole(r) for r in rows]
-    in_specs += [pl.BlockSpec((1, MAXLEN, D), slot)] + [whole(w) for w in weights]
+    in_specs += [pl.BlockSpec((n_each, MAXLEN, D), slot)] + [whole(w) for w in weights]
     args = [*msgs, *msgs, *rows, cot, *weights]
     alias = {}
     if prior is not None:
@@ -348,19 +398,24 @@
         functools.partial(layer_kernel, plan, prior is not None),
         grid_spec=pltpu.PrefetchScalarGridSpec(
             num_scalar_prefetch=1,
-            grid=(n_src * n_each,),
+            grid=(n_src,),
             in_specs=in_specs,
-            out_specs=[pl.BlockSpec((1, MAXLEN, D), slot)]
+            out_specs=[pl.BlockSpec((n_each, MAXLEN, D), slot)]
             + [pl.BlockSpec((UNIQ, D), lambda i, s: (0, 0))] * n_src,
             scratch_shapes=[
                 pltpu.VMEM((UNIQ, D), BF),
-                pltpu.VMEM((1, MAXLEN), I32),
+                pltpu.VMEM((8, MAXLEN), I32),
                 pltpu.VMEM((UNIQ, D), F32),
-                pltpu.VMEM((MAXLEN, 4 * D), BF),
-                pltpu.VMEM((MAXLEN, 4 * D), F32),
-                pltpu.VMEM((HEADS, MAXLEN, MAXLEN), BF),
-                pltpu.VMEM((HEADS, MAXLEN, MAXLEN), F32),
-                pltpu.VMEM((MAXLEN, 4 * D), BF),
+                pltpu.VMEM((16, MAXLEN, 128), BF),
+                pltpu.VMEM((16, MAXLEN, 128), BF),
+                pltpu.VMEM((HEADS, 2, MAXLEN, 128), BF),
+                pltpu.VMEM((HEADS, 2, MAXLEN, 128), BF),
+                pltpu.VMEM((16, MAXLEN, 128), BF),
+                pltpu.VMEM((MAXLEN, D), F32),
+                pltpu.VMEM((MAXLEN, D), F32),
+                pltpu.VMEM((MAXLEN, D), F32),
+                pltpu.VMEM((MAXLEN, 128), F32),
+                pltpu.VMEM((4, MAXLEN, 128), BF),
                 pltpu.VMEM((MAXLEN, D), F32),
             ],
         ),
@@ -467,7 +522,7 @@
     req, pos, *sent = pack(assignment, lengths, seq, unique_ids, inverse)
     asked = exchange(req, (DEVICES, 1, 4))
     msgs = [sent[0]] + [lax.ppermute(sent[d], "seq", ring(d)) for d in (1, 2, 3)]
-    bias, pos_rows = tables(position_bias, pos)
+    bias, pos_rows, win, wout = tables(position_bias, pos, proj_in, proj_out)
     answer = answer_rows(asked, item_table)
     got = exchange(answer, (DEVICES, 8, D // 2))
     got, *msgs = lax.optimization_barrier((got, *msgs))
@@ -475,11 +530,11 @@
     own = compact(pos_rows, got)
     rows = [own] + [lax.ppermute(own, "seq", ring(d)) for d in (1, 2, 3)]
     weights = (
-        proj_in,
+        win,
         bias_in.reshape(1, 4 * D),
         gain_in.reshape(1, D),
         gain_mid.reshape(1, D),
-        proj_out,
+        wout,
         bias,
     )
     outputs = None

time: 134 us -> 124 us (0.925)
  Pallas kernels: 51 us -> 39.6 us
  local copies, waits for them, and re-layouts: 5.84 us -> 9.64 us
  waiting for transfers between devices: 35.1 us -> 32.1 us
    pallas_call x3, Pallas kernels: 40.2 us -> 28.4 us  [layer(): pl.pallas_call(functools.partial(layer_kernel, plan, prior is not None),...]
    unnamed x24 -> x30, local copies, waits for them, and re-layouts: 5.66 us -> 9.46 us
    ppermute x3, waiting for transfers between devices: 2.82 us -> 0.01 us  [program(): lax.ppermute(sent[d], 'seq', ring(d))]
    all_to_all x2, waiting for transfers between devices: 19.2 us -> 17.7 us  [exchange(): lax.all_to_all(x.reshape(shape), ('emb', 'seq'), split_axis=0, concat_axi...]
where the time goes in v3:
time: 124 us; the launch traced here: 123 us
  Pallas kernels  39.6 us (32%)
  waiting for transfers between devices  32.1 us (26%)
  blocking collectives  21 us (17%)
  starting transfers between devices  20.3 us (16%)
  local copies, waits for them, and re-layouts  9.64 us (8%)
    pallas_call x3, Pallas kernels, layer(): pl.pallas_call(functools.partial(layer_kernel, plan, prior is not None),...  28.4 us
    all_to_all x1, blocking collectives, exchange(): lax.all_to_all(x.reshape(shape), ('emb', 'seq'), split_axis=0, concat_axi...  21 us
    all_to_all x2, waiting for transfers between devices, exchange(): lax.all_to_all(x.reshape(shape), ('emb', 'seq'), split_axis=0, concat_axi...  17.7 us
    all_to_all x2, starting transfers between devices, exchange(): lax.all_to_all(x.reshape(shape), ('emb', 'seq'), split_axis=0, concat_axi...  10.3 us
    unnamed x30, local copies, waits for them, and re-layouts  9.46 us
    ppermute x3, waiting for transfers between devices, program(): sums.append(part if d == 0 else lax.ppermute(part, 'seq', ring(-d)))  8.06 us
    ppermute x3, waiting for transfers between devices, program(): rows = [own] + [lax.ppermute(own, 'seq', ring(d)) for d in (1, 2, 3)]  6.34 us
    ppermute x3, starting transfers between devices, program(): lax.ppermute(sent[d], 'seq', ring(d))  5.03 us
  transfers between devices with their start and end apart: 11, of which 7 were waited for; matrix products, arithmetic and copies ran while one was open for 0% of the time, Pallas kernels for 8%

profile of v3, /device:TPU:1, one launch (start us, length us, event | category | flops | bytes accessed | tf_op | source)
XLA Modules:
  0.0 123.4 jit_solution(5077528256057592103)
XLA Ops:
  0.6 0.0 copy-start.14
  0.6 0.0 copy-start.10
  0.7 0.7 copy-done.10
  1.3 0.0 copy-start.11
  1.3 0.7 copy-done.11
  2.0 0.0 copy-start.12
  2.0 0.7 copy-done.12
  2.7 0.0 copy-start.13
  2.7 0.7 copy-done.13
  3.3 1.3 %pack.1 = (s32[128,4]{1,0:T(8,128)S(1)}, s32[1,256]{1,0:T(1,128)S(1)}, s32[2,384]{1,0:T(2,128)S(1)}, s32[2,384]{1,0:T(2,128)S(1)}, s32[2,384]{1,0:T(2,128)S(1)}, /*index=5*/s32[2,384]{1,0:T(2,128)S(1)}) custom-call(s32[8]{0:T(128)S(1)} %copy-done.12, s32[8]{0:T(128)S(1)} %copy-done.13, s32[1]{0:T(128)} %bitcast.seq_ref.refs_0_, s32[1,256]{1,0:T(1,128)S(1)} %bitcast.26, ...), custom_call_target="tpu_custom_call" | custom-call | tf_op jit(solution)/shard_map/pack/pallas_call | solution.py:84
  4.6 21.0 %all_to_all.15 = s32[128,1,4]{2,1,0:T(1,128)S(1)} all-to-all(s32[128,1,4]{2,1,0:T(1,128)S(1)} %bitcast.19), channel_id=1, replica_groups=mesh['emb'=32,'seq'=4] {'emb','seq'}, dimensions={0} | all-to-all | bytes 4096 | tf_op jit(solution)/shard_map/all_to_all | solution.py:500
  25.6 0.0 copy-start.5
  25.6 1.2 copy-done.5
  26.9 0.0 copy-start.7
  26.9 0.0 copy-start.8
  26.9 0.0 copy-start.9
  26.9 3.1 %answer.1 = bf16[1024,256]{1,0:T(8,128)(2,1)} custom-call(s32[128,4]{1,0:T(8,128)S(1)} %bitcast.14, bf16[1024,512]{1,0:T(8,128)(2,1)S(1)} %copy-done.5), custom_call_target="tpu_custom_call" | custom-call | tf_op jit(solution)/shard_map/answer/pallas_call | solution.py:152
  30.0 0.0 copy-start
  30.0 5.3 %all-to-all-start.1 = ((bf16[128,8,256]{2,1,0:T(8,128)(2,1)}), bf16[128,8,256]{2,1,0:T(8,128)(2,1)}, u32[]{:S(2)}, u32[]{:S(2)}) async-start(bf16[128,8,256]{2,1,0:T(8,128)(2,1)} %bitcast.5), calls=%async_computation.1 | async-start | bytes 1048576 | tf_op jit(solution)/shard_map/all_to_all | solution.py:500
  35.3 1.4 %collective-permute-start = (s32[2,384]{1,0:T(2,128)S(1)}, s32[2,384]{1,0:T(2,128)S(1)}, u32[]{:S(2)}, u32[]{:S(2)}) collective-permute-start(s32[2,384]{1,0:T(2,128)S(1)} %get-tuple-element.27), channel_id=1, source_target_pairs={{0,1},{1,2},{2,3},{3,0},{4,5},{5,6},{6,7},{7,4},{8,9},{9,10},{10,1... | collective-permute-start | bytes 9224 | tf_op jit(solution)/shard_map/ppermute | solution.py:524
  36.7 2.4 %collective-permute-start.1 = (s32[2,384]{1,0:T(2,128)S(1)}, s32[2,384]{1,0:T(2,128)S(1)}, u32[]{:S(2)}, u32[]{:S(2)}) collective-permute-start(s32[2,384]{1,0:T(2,128)S(1)} %get-tuple-element.28), channel_id=1, source_target_pairs={{0,2},{1,3},{2,0},{3,1},{4,6},{5,7},{6,4},{7,5},{8,10},{9,11},{10,... | collective-permute-start | bytes 9224 | tf_op jit(solution)/shard_map/ppermute | solution.py:524
  39.2 1.2 collective-permute-start.2
  40.3 0.0 copy-done.14
  40.3 0.2 rev.3.flipped_ref
  40.5 0.0 copy-start.4
  40.5 1.6 %copy-done.4 = bf16[512,2048]{1,0:T(8,128)(2,1)S(1)} copy-done((bf16[512,2048]{1,0:T(8,128)(2,1)S(1)}, bf16[512,2048]{1,0:T(8,128)(2,1)}, u32[]{:S(2)}) %copy-start.4) | copy-done | bytes 2097176
  42.1 0.0 copy-start.6
  42.1 1.0 copy-done.6
  43.1 0.6 tables.1
  43.8 0.0 copy-start.1
  43.8 1.3 %copy-done.1 = bf16[16,512,128]{2,1,0:T(8,128)(2,1)} copy-done((bf16[16,512,128]{2,1,0:T(8,128)(2,1)}, bf16[16,512,128]{2,1,0:T(8,128)(2,1)S(1)}, u32[]{:S(2)}) %copy-start.1) | copy-done | bytes 2097176
  45.1 0.0 collective-permute-done.refs_1_.refs_4_
  45.1 0.0 collective-permute-done.1.refs_3_.refs_6_
  45.1 0.0 collective-permute-done.2.refs_2_.refs_5_
  45.1 3.9 %all-to-all-done.1 = bf16[128,8,256]{2,1,0:T(8,128)(2,1)} async-done(((bf16[128,8,256]{2,1,0:T(8,128)(2,1)}), bf16[128,8,256]{2,1,0:T(8,128)(2,1)}, u32[]{:S(2)}, u32[]{:S(2)}) %all-to-all-start.1) | async-done | bytes 524320 | tf_op jit(solution)/shard_map/all_to_all | solution.py:500
  49.0 1.5 %compact.1.refs_3_ = bf16[256,512]{1,0:T(8,128)(2,1)S(1)} custom-call(s32[256,128]{1,0:T(8,128)S(1)} %get-tuple-element.32.pos_ref, bf16[1024,256]{1,0:T(8,128)(2,1)} %bitcast.6.got_ref), custom_call_target="tpu_custom_call" | custom-call | tf_op jit(solution)/shard_map/compact/pallas_call | solution.py:169
  50.6 0.5 collective-permute-start.5
  51.1 2.2 %collective-permute-start.4 = (bf16[256,512]{1,0:T(8,128)(2,1)S(1)}, bf16[256,512]{1,0:T(8,128)(2,1)S(1)}, u32[]{:S(2)}, u32[]{:S(2)}) collective-permute-start(bf16[256,512]{1,0:T(8,128)(2,1)S(1)} %compact.1.refs_3_), channel_id=1, source_target_pairs={{0,3},{1,0},{2,1},{3,2},{4,7},{5,4},{6,5},{7,6},{8,11},{9,8},{10,9... | collective-permute-start | bytes 786440 | tf_op jit(solution)/shard_map/ppermute | solution.py:531
  53.3 0.0 collective-permute-start.3
  53.3 0.0 copy-done.7
  53.3 0.0 copy-done.8
  53.3 0.0 copy-done.9
  53.4 0.0 copy-done
  53.4 0.0 copy-start.2
  53.4 1.6 %copy-done.2 = bf16[16,512,128]{2,1,0:T(8,128)(2,1)S(1)} copy-done((bf16[16,512,128]{2,1,0:T(8,128)(2,1)S(1)}, bf16[16,512,128]{2,1,0:T(8,128)(2,1)}, u32[]{:S(2)}) %copy-start.2) | copy-done | bytes 2097176
  55.0 0.0 copy-start.3
  55.0 4.7 %layer.3 = (bf16[8,256,512]{2,1,0:T(8,128)(2,1)}, bf16[256,512]{1,0:T(8,128)(2,1)S(1)}) custom-call(s32[1]{0:T(128)} %bitcast.seq_ref.refs_0_, s32[2,384]{1,0:T(2,128)S(1)} %get-tuple-element.30.refs_1_.refs_2_, s32[2,384]{1,0:T(2,128)S(1)} %get-tuple-element.30.refs_1_.refs_2_, bf16[256,512]{1,0:T(8,128)(2,1)S(1)} %compact.1.refs_3_, ...), custom_call_target="tpu_custom_call" | custom-call | tf_op jit(solution)/shard_map/layer/pallas_call | solution.py:397
  59.7 0.1 collective-permute-done.5.refs_9_
  59.7 4.0 %collective-permute-done.4.refs_8_ = bf16[256,512]{1,0:T(8,128)(2,1)S(1)} collective-permute-done((bf16[256,512]{1,0:T(8,128)(2,1)S(1)}, bf16[256,512]{1,0:T(8,128)(2,1)S(1)}, u32[]{:S(2)}, u32[]{:S(2)}) %collective-permute-start.4) | collective-permute-done | bytes 262176 | tf_op jit(solution)/shard_map/ppermute | solution.py:531
  63.7 2.3 %collective-permute-done.3.refs_7_ = bf16[256,512]{1,0:T(8,128)(2,1)S(1)} collective-permute-done((bf16[256,512]{1,0:T(8,128)(2,1)S(1)}, bf16[256,512]{1,0:T(8,128)(2,1)S(1)}, u32[]{:S(2)}, u32[]{:S(2)}) %collective-permute-start.3) | collective-permute-done | bytes 262176 | tf_op jit(solution)/shard_map/ppermute | solution.py:531
  66.0 0.0 copy-done.3
  66.0 19.1 %layer.4 = (bf16[8,256,512]{2,1,0:T(8,128)(2,1)}, bf16[256,512]{1,0:T(8,128)(2,1)S(1)}, bf16[256,512]{1,0:T(8,128)(2,1)S(1)}, bf16[256,512]{1,0:T(8,128)(2,1)S(1)}) custom-call(s32[1]{0:T(128)} %bitcast.seq_ref.refs_0_, s32[2,384]{1,0:T(2,128)S(1)} %collective-permute-done.refs_1_.refs_4_, ...), custom_call_target="tpu_custom_call", output_to_operand_aliasing={{0}: (17, {})} | custom-call | tf_op jit(solution)/shard_map/layer/pallas_call | solution.py:397
  85.1 1.0 collective-permute-start.6
  86.1 0.4 collective-permute-start.7
  86.5 0.7 collective-permute-start.8
  87.3 4.7 %layer.5 = (bf16[8,256,512]{2,1,0:T(8,128)(2,1)}, bf16[256,512]{1,0:T(8,128)(2,1)S(1)}) custom-call(s32[1]{0:T(128)} %bitcast.seq_ref.refs_0_, s32[2,384]{1,0:T(2,128)S(1)} %get-tuple-element.30.refs_1_.refs_2_, s32[2,384]{1,0:T(2,128)S(1)} %get-tuple-element.30.refs_1_.refs_2_, ...), custom_call_target="tpu_custom_call", output_to_operand_aliasing={{0}: (11, {})} | custom-call | tf_op jit(solution)/shard_map/layer/pallas_call | solution.py:397
  92.0 0.5 collective-permute-done.6.refs_1_
  92.4 7.6 %collective-permute-done.7.refs_2_ = bf16[256,512]{1,0:T(8,128)(2,1)S(1)} collective-permute-done((bf16[256,512]{1,0:T(8,128)(2,1)S(1)}, bf16[256,512]{1,0:T(8,128)(2,1)S(1)}, u32[]{:S(2)}, u32[]{:S(2)}) %collective-permute-start.7) | collective-permute-done | bytes 262176 | tf_op jit(solution)/shard_map/ppermute | solution.py:553
  100.0 0.0 collective-permute-done.8.refs_3_
  100.0 1.4 %expand.1 = bf16[1024,256]{1,0:T(8,128)(2,1)} custom-call(s32[1,256]{1,0:T(1,128)S(1)} %get-tuple-element.31.pos_ref, bf16[256,512]{1,0:T(8,128)(2,1)S(1)} %get-tuple-element.43.refs_0_, bf16[256,512]{1,0:T(8,128)(2,1)S(1)} %collective-permute-done.6.refs_1_, bf16[256,512]{1,0:T(8,128)(2,1)S(1)} %collective-permute-done.7.refs_2_, ...), custom_call_target="tpu_custom_call" | custom-call | tf_op jit(solution)/shard_map/expand/pallas_call | solution.py:443
  101.4 5.0 %all-to-all-start.2 = ((bf16[128,8,256]{2,1,0:T(8,128)(2,1)}), bf16[128,8,256]{2,1,0:T(8,128)(2,1)S(1)}, u32[]{:S(2)}, u32[]{:S(2)}) async-start(bf16[128,8,256]{2,1,0:T(8,128)(2,1)} %bitcast.10), calls=%async_computation.2 | async-start | bytes 1048576 | tf_op jit(solution)/shard_map/all_to_all | solution.py:500
  106.4 0.3 asked_line.1.line_ref
  106.7 13.8 %all-to-all-done.2 = bf16[128,8,256]{2,1,0:T(8,128)(2,1)S(1)} async-done(((bf16[128,8,256]{2,1,0:T(8,128)(2,1)}), bf16[128,8,256]{2,1,0:T(8,128)(2,1)S(1)}, u32[]{:S(2)}, u32[]{:S(2)}) %all-to-all-start.2) | async-done | bytes 524320 | tf_op jit(solution)/shard_map/all_to_all | solution.py:500
  120.5 2.9 %scatter.1 = f32[1024,512]{1,0:T(8,128)} custom-call(s32[1,1024]{1,0:T(1,128)S(1)} %asked_line.1.line_ref, bf16[1024,256]{1,0:T(8,128)(2,1)S(1)} %bitcast.13), custom_call_target="tpu_custom_call" | custom-call | tf_op jit(solution)/shard_map/scatter/pallas_call | solution.py:484
Async XLA Ops:
  0.6 39.7 %copy-start.14 = (f32[4,256]{1,0:T(4,128)S(1)}, f32[4,256]{1,0:T(4,128)}, u32[]{:S(2)}) copy-start(f32[4,256]{1,0:T(4,128)} %param.22) | copy-start | bytes 12292
  0.6 0.7 copy-start.10
  1.3 0.7 copy-start.11
  2.0 0.7 copy-start.12
  2.7 0.7 copy-start.13
  25.6 1.2 copy-start.5
  26.9 26.5 %copy-start.7 = (f32[2048]{0:T(1024)S(1)}, f32[2048]{0:T(1024)}, u32[]{:S(2)}) copy-start(f32[2048]{0:T(1024)} %param.18) | copy-start | bytes 24580
  26.9 26.5 %copy-start.8 = (f32[512]{0:T(512)S(1)}, f32[512]{0:T(512)}, u32[]{:S(2)}) copy-start(f32[512]{0:T(512)} %param.19) | copy-start | bytes 6148
  26.9 26.5 %copy-start.9 = (f32[512]{0:T(512)S(1)}, f32[512]{0:T(512)}, u32[]{:S(2)}) copy-start(f32[512]{0:T(512)} %param.20) | copy-start | bytes 6148
  30.0 23.4 %copy-start = (bf16[8,256,512]{2,1,0:T(8,128)(2,1)S(1)}, bf16[8,256,512]{2,1,0:T(8,128)(2,1)}, u32[]{:S(2)}) copy-start(bf16[8,256,512]{2,1,0:T(8,128)(2,1)} %refs_4_.3) | copy-start | bytes 6291460
  30.0 19.0 %all-to-all-start.1 = ((bf16[128,8,256]{2,1,0:T(8,128)(2,1)}), bf16[128,8,256]{2,1,0:T(8,128)(2,1)}, u32[]{:S(2)}, u32[]{:S(2)}) async-start(bf16[128,8,256]{2,1,0:T(8,128)(2,1)} %bitcast.5), calls=%async_computation.1 | async-start | bytes 1048576 | tf_op jit(solution)/shard_map/all_to_all | solution.py:500
  35.3 9.8 %collective-permute-start = (s32[2,384]{1,0:T(2,128)S(1)}, s32[2,384]{1,0:T(2,128)S(1)}, u32[]{:S(2)}, u32[]{:S(2)}) collective-permute-start(s32[2,384]{1,0:T(2,128)S(1)} %get-tuple-element.27), channel_id=1, source_target_pairs={{0,1},{1,2},{2,3},{3,0},{4,5},{5,6},{6,7},{7,4},{8,9},{9,10},{10,1... | collective-permute-start | bytes 9224 | tf_op jit(solution)/shard_map/ppermute | solution.py:524
  36.7 8.4 %collective-permute-start.1 = (s32[2,384]{1,0:T(2,128)S(1)}, s32[2,384]{1,0:T(2,128)S(1)}, u32[]{:S(2)}, u32[]{:S(2)}) collective-permute-start(s32[2,384]{1,0:T(2,128)S(1)} %get-tuple-element.28), channel_id=1, source_target_pairs={{0,2},{1,3},{2,0},{3,1},{4,6},{5,7},{6,4},{7,5},{8,10},{9,11},{10,... | collective-permute-start | bytes 9224 | tf_op jit(solution)/shard_map/ppermute | solution.py:524
  39.2 6.0 %collective-permute-start.2 = (s32[2,384]{1,0:T(2,128)S(1)}, s32[2,384]{1,0:T(2,128)S(1)}, u32[]{:S(2)}, u32[]{:S(2)}) collective-permute-start(s32[2,384]{1,0:T(2,128)S(1)} %get-tuple-element.29), channel_id=1, source_target_pairs={{0,3},{1,0},{2,1},{3,2},{4,7},{5,4},{6,5},{7,6},{8,11},{9,8},{10,9... | collective-permute-start | bytes 9224 | tf_op jit(solution)/shard_map/ppermute | solution.py:524
  40.5 1.6 %copy-start.4 = (bf16[512,2048]{1,0:T(8,128)(2,1)S(1)}, bf16[512,2048]{1,0:T(8,128)(2,1)}, u32[]{:S(2)}) copy-start(bf16[512,2048]{1,0:T(8,128)(2,1)} %win_ref.1) | copy-start | bytes 6291460
  42.1 1.0 copy-start.6
  43.8 1.3 %copy-start.1 = (bf16[16,512,128]{2,1,0:T(8,128)(2,1)}, bf16[16,512,128]{2,1,0:T(8,128)(2,1)S(1)}, u32[]{:S(2)}) copy-start(bf16[16,512,128]{2,1,0:T(8,128)(2,1)S(1)} %get-tuple-element.34.refs_5_.refs_11_) | copy-start | bytes 6291460
  50.6 9.1 %collective-permute-start.5 = (bf16[256,512]{1,0:T(8,128)(2,1)S(1)}, bf16[256,512]{1,0:T(8,128)(2,1)S(1)}, u32[]{:S(2)}, u32[]{:S(2)}) collective-permute-start(bf16[256,512]{1,0:T(8,128)(2,1)S(1)} %compact.1.refs_3_), channel_id=1, source_target_pairs={{0,2},{1,3},{2,0},{3,1},{4,6},{5,7},{6,4},{7,5},{8,10},{9,11},{10,... | collective-permute-start | bytes 786440 | tf_op jit(solution)/shard_map/ppermute | solution.py:531
  51.1 12.6 %collective-permute-start.4 = (bf16[256,512]{1,0:T(8,128)(2,1)S(1)}, bf16[256,512]{1,0:T(8,128)(2,1)S(1)}, u32[]{:S(2)}, u32[]{:S(2)}) collective-permute-start(bf16[256,512]{1,0:T(8,128)(2,1)S(1)} %compact.1.refs_3_), channel_id=1, source_target_pairs={{0,3},{1,0},{2,1},{3,2},{4,7},{5,4},{6,5},{7,6},{8,11},{9,8},{10,9... | collective-permute-start | bytes 786440 | tf_op jit(solution)/shard_map/ppermute | solution.py:531
  53.3 12.7 %collective-permute-start.3 = (bf16[256,512]{1,0:T(8,128)(2,1)S(1)}, bf16[256,512]{1,0:T(8,128)(2,1)S(1)}, u32[]{:S(2)}, u32[]{:S(2)}) collective-permute-start(bf16[256,512]{1,0:T(8,128)(2,1)S(1)} %compact.1.refs_3_), channel_id=1, source_target_pairs={{0,1},{1,2},{2,3},{3,0},{4,5},{5,6},{6,7},{7,4},{8,9},{9,10},{10,1... | collective-permute-start | bytes 786440 | tf_op jit(solution)/shard_map/ppermute | solution.py:531
  53.4 1.6 %copy-start.2 = (bf16[16,512,128]{2,1,0:T(8,128)(2,1)S(1)}, bf16[16,512,128]{2,1,0:T(8,128)(2,1)}, u32[]{:S(2)}) copy-start(bf16[16,512,128]{2,1,0:T(8,128)(2,1)} %copy-done.1) | copy-start | bytes 6291460
  55.0 11.0 %copy-start.3 = (bf16[16,512,128]{2,1,0:T(8,128)(2,1)S(1)}, bf16[16,512,128]{2,1,0:T(8,128)(2,1)}, u32[]{:S(2)}) copy-start(bf16[16,512,128]{2,1,0:T(8,128)(2,1)} %copy-done.1) | copy-start | bytes 6291460
  85.1 7.4 %collective-permute-start.6 = (bf16[256,512]{1,0:T(8,128)(2,1)S(1)}, bf16[256,512]{1,0:T(8,128)(2,1)S(1)}, u32[]{:S(2)}, u32[]{:S(2)}) collective-permute-start(bf16[256,512]{1,0:T(8,128)(2,1)S(1)} %get-tuple-element.44), channel_id=1, source_target_pairs={{0,3},{1,0},{2,1},{3,2},{4,7},{5,4},{6,5},{7,6},{8,11},{9,8},{10,9... | collective-permute-start | bytes 786440 | tf_op jit(solution)/shard_map/ppermute | solution.py:553
  86.1 13.9 %collective-permute-start.7 = (bf16[256,512]{1,0:T(8,128)(2,1)S(1)}, bf16[256,512]{1,0:T(8,128)(2,1)S(1)}, u32[]{:S(2)}, u32[]{:S(2)}) collective-permute-start(bf16[256,512]{1,0:T(8,128)(2,1)S(1)} %get-tuple-element.45), channel_id=1, source_target_pairs={{0,1},{1,2},{2,3},{3,0},{4,5},{5,6},{6,7},{7,4},{8,9},{9,10},{10,1... | collective-permute-start | bytes 786440 | tf_op jit(solution)/shard_map/ppermute | solution.py:553
  86.5 13.5 %collective-permute-start.8 = (bf16[256,512]{1,0:T(8,128)(2,1)S(1)}, bf16[256,512]{1,0:T(8,128)(2,1)S(1)}, u32[]{:S(2)}, u32[]{:S(2)}) collective-permute-start(bf16[256,512]{1,0:T(8,128)(2,1)S(1)} %get-tuple-element.46), channel_id=1, source_target_pairs={{0,2},{1,3},{2,0},{3,1},{4,6},{5,7},{6,4},{7,5},{8,10},{9,11},{10,... | collective-permute-start | bytes 786440 | tf_op jit(solution)/shard_map/ppermute | solution.py:553
  101.4 19.1 %all-to-all-start.2 = ((bf16[128,8,256]{2,1,0:T(8,128)(2,1)}), bf16[128,8,256]{2,1,0:T(8,128)(2,1)S(1)}, u32[]{:S(2)}, u32[]{:S(2)}) async-start(bf16[128,8,256]{2,1,0:T(8,128)(2,1)} %bitcast.10), calls=%async_computation.2 | async-start | bytes 1048576 | tf_op jit(solution)/shard_map/all_to_all | solution.py:500

commit v4 on v3

v4 whole, which is shorter than its diff:
```python
import functools

import jax
import jax.numpy as jnp
from jax import lax
from jax.experimental import pallas as pl
from jax.experimental.pallas import tpu as pltpu
from jax.sharding import PartitionSpec as P

D = 512
HEADS = 4
HEAD = 128
MAXLEN = 256
UNIQ = 256
ROWS_DEV = 1024
DEVICES = 128
SCALE = HEAD**-0.5
EPS = 1e-05
MASKED = -1e30
BF = jnp.bfloat16
F32 = jnp.float32
I32 = jnp.int32


def nn(a, b):
    return lax.dot_general(a, b, (((1,), (0,)), ((), ())), preferred_element_type=F32)


def nt(a, b):
    return lax.dot_general(a, b, (((1,), (1,)), ((), ())), preferred_element_type=F32)


def tn(a, b):
    return lax.dot_general(a, b, (((0,), (0,)), ((), ())), preferred_element_type=F32)


def iota(shape, dim):
    return lax.broadcasted_iota(I32, shape, dim)


def onehot(mask):
    return jnp.where(mask, 1.0, 0.0).astype(BF)


def in_hbm(x):
    return pltpu.with_memory_space_constraint(x, pltpu.HBM)


def params(**kw):
    return pltpu.CompilerParams(vmem_limit_bytes=24 << 20, **kw)


def pack_kernel(assign_hbm, len_hbm, seq_ref, ids_hbm, inv_hbm, req_ref, pos_ref, *refs):
    msg_refs = refs[:4]
    assign_ref, len_ref, ids_ref, inv_ref, sems = refs[4:]
    loads = [
        pltpu.make_async_copy(src, dst, sems.at[k])
        for k, (src, dst) in enumerate(
            (
                (ids_hbm, ids_ref),
                (inv_hbm, inv_ref),
                (assign_hbm, assign_ref),
                (len_hbm, len_ref),
            )
        )
    ]
    for load in loads:
        load.start()
    loads[0].wait()
    ids = ids_ref[...]
    owner = ids >> 10
    local = (ids & (ROWS_DEV - 1)).astype(F32)
    held = iota((DEVICES, UNIQ), 0) == owner
    earlier = onehot(iota((UNIQ, UNIQ), 0) < iota((UNIQ, UNIQ), 1))
    before = nn(onehot(held), earlier)
    rank = jnp.sum(jnp.where(held, before, 0.0), axis=0, keepdims=True)
    pos_ref[...] = owner * 8 + rank.astype(I32)
    lane = iota((DEVICES, 4), 1)
    req = jnp.zeros((DEVICES, 4), F32)
    for r in range(4):
        chosen = held & (before == float(r))
        col = jnp.sum(jnp.where(chosen, ROWS_DEV - local, 0.0), axis=1, keepdims=True)
        req = jnp.where(lane == r, ROWS_DEV - col, req)
    req_ref[...] = req.astype(I32)
    for load in loads[1:]:
        load.wait()
    seq = seq_ref[0]
    for j in range(8):
        place = assign_ref[j]
        delta = (place // 8 - seq + 4) % 4
        half = place % 2
        row = jnp.concatenate(
            [inv_ref[j : j + 1, :], jnp.full((1, 128), len_ref[j], I32)], axis=1
        )
        for d in range(4):
            for b in range(2):

                @pl.when((delta == d) & (half == b))
                def _():
                    msg_refs[d][b : b + 1, :] = row


def pack(assignment, lengths, seq, ids, inverse):
    smem = pl.BlockSpec(memory_space=pltpu.SMEM)
    vmem = pl.BlockSpec(memory_space=pltpu.VMEM)
    hbm = pl.BlockSpec(memory_space=pltpu.HBM)
    return pl.pallas_call(
        pack_kernel,
        in_specs=[hbm, hbm, smem, hbm, hbm],
        scratch_shapes=[
            pltpu.SMEM((8,), I32),
            pltpu.SMEM((8,), I32),
            pltpu.VMEM((1, UNIQ), I32),
            pltpu.VMEM((8, MAXLEN), I32),
            pltpu.SemaphoreType.DMA((4,)),
        ],
        out_specs=[vmem] * 6,
        out_shape=[
            jax.ShapeDtypeStruct((DEVICES, 4), I32),
            jax.ShapeDtypeStruct((1, UNIQ), I32),
        ]
        + [jax.ShapeDtypeStruct((2, MAXLEN + 128), I32)] * 4,
        compiler_params=params(),
        name="pack",
    )(in_hbm(assignment), in_hbm(lengths), seq, in_hbm(ids.reshape(1, UNIQ)), in_hbm(inverse))


def tables_kernel(flipped_ref, pos_ref, win_hbm, wout_hbm, *refs):
    bias_ref, pos_rows_ref, winb_hbm, woutb_hbm, win_ref, wout_ref, winb_ref, woutb_ref, sems = refs
    loads = [
        pltpu.make_async_copy(win_hbm, win_ref, sems.at[0]),
        pltpu.make_async_copy(wout_hbm, wout_ref, sems.at[1]),
    ]
    stores = [
        pltpu.make_async_copy(winb_ref, winb_hbm, sems.at[2]),
        pltpu.make_async_copy(woutb_ref, woutb_hbm, sems.at[3]),
    ]
    for load in loads:
        load.start()
    i = iota((MAXLEN, MAXLEN), 0)
    j = iota((MAXLEN, MAXLEN), 1)
    for h in range(HEADS):
        line = jnp.broadcast_to(flipped_ref[h : h + 1, :], (MAXLEN, MAXLEN))
        spread = pltpu.roll(line, 1, 1, stride=1, stride_axis=0)
        full = jnp.where(j <= i, 0.5 * spread, MASKED)
        bias_ref[h] = full[:, :128]
    pos = jnp.broadcast_to(pos_ref[...], (UNIQ, UNIQ)).astype(F32)
    col = jnp.sum(jnp.where(i == j, pos, 0.0), axis=1, keepdims=True)
    pos_rows_ref[...] = jnp.broadcast_to(col.astype(I32), (UNIQ, 128))
    for load, store, src, dst in zip(loads, stores, (win_ref, wout_ref), (winb_ref, woutb_ref)):
        load.wait()
        for c in range(dst.shape[0]):
            dst[c] = src[:, pl.ds(c * 128, 128)]
        store.start()
    for store in stores:
        store.wait()


def tables(position_bias, pos, proj_in, proj_out):
    vmem = pl.BlockSpec(memory_space=pltpu.VMEM)
    hbm = pl.BlockSpec(memory_space=pltpu.HBM)
    return pl.pallas_call(
        tables_kernel,
        out_shape=[
            jax.ShapeDtypeStruct((HEADS, MAXLEN, 128), F32),
            jax.ShapeDtypeStruct((UNIQ, 128), I32),
            pltpu.HBM((16, D, 128), BF),
            pltpu.HBM((4, D, 128), BF),
        ],
        in_specs=[vmem, vmem, hbm, hbm],
        out_specs=[vmem, vmem, hbm, hbm],
        scratch_shapes=[
            pltpu.VMEM((D, 4 * D), BF),
            pltpu.VMEM((D, D), BF),
            pltpu.VMEM((16, D, 128), BF),
            pltpu.VMEM((4, D, 128), BF),
            pltpu.SemaphoreType.DMA((4,)),
        ],
        compiler_params=params(),
        name="tables",
    )(position_bias[:, ::-1], pos, in_hbm(proj_in), in_hbm(proj_out))


def asked_parts(asked_ref):
    asked = asked_ref[...]
    return (asked >> 5).astype(BF), (asked & 31).astype(BF)


def to_halves(x):
    groups = x.shape[0] // 8
    upper = iota((groups, 8, D // 2), 1) < 4
    low = x[:, : D // 2].reshape(groups, 8, D // 2)
    high = x[:, D // 2 :].reshape(groups, 8, D // 2)
    even = jnp.where(upper, low, pltpu.roll(high, 4, 1))
    odd = jnp.where(upper, pltpu.roll(low, 4, 1), high)
    both = jnp.concatenate([even[:, None], odd[:, None]], axis=1)
    return both.reshape(groups * 16, D // 2)


def from_halves(x):
    groups = x.shape[0] // 16
    upper = iota((groups, 8, D // 2), 1) < 4
    pairs = x.reshape(groups, 2, 8, D // 2)
    even = pairs[:, 0]
    odd = pairs[:, 1]
    low = jnp.where(upper, even, pltpu.roll(odd, 4, 1))
    high = jnp.where(upper, pltpu.roll(even, 4, 1), odd)
    flat = (groups * 8, D // 2)
    return jnp.concatenate([low.reshape(flat), high.reshape(flat)], axis=1)


def answer_kernel(asked_ref, table_hbm, out_ref, table_ref, pick_ref, sem):
    load = pltpu.make_async_copy(table_hbm, table_ref, sem.at[0])
    load.start()
    high, low = asked_parts(asked_ref)
    count = 4 * DEVICES
    spread = onehot((iota((count, DEVICES), 0) >> 2) == iota((count, DEVICES), 1))
    value = nn(spread, high) * 32.0 + nn(spread, low)
    mine = iota((count, 4), 1) == (iota((count, 4), 0) & 3)
    col = jnp.sum(jnp.where(mine, value, 0.0), axis=1, keepdims=True).astype(I32)
    pick_ref[...] = onehot(iota((count, ROWS_DEV), 1) == col)
    load.wait()
    for c in range(2):
        rows = nn(pick_ref[pl.ds(c * 256, 256), :], table_ref[...])
        out_ref[pl.ds(c * 512, 512), :] = to_halves(rows).astype(BF)


def answer_rows(asked, table):
    return pl.pallas_call(
        answer_kernel,
        in_specs=[pl.BlockSpec(memory_space=pltpu.VMEM), pl.BlockSpec(memory_space=pltpu.HBM)],
        out_shape=jax.ShapeDtypeStruct((8 * DEVICES, D // 2), BF),
        scratch_shapes=[
            pltpu.VMEM((ROWS_DEV, D), BF),
            pltpu.VMEM((4 * DEVICES, ROWS_DEV), BF),
            pltpu.SemaphoreType.DMA((1,)),
        ],
        compiler_params=params(),
        name="answer",
    )(asked, in_hbm(table))


def compact_kernel(pos_ref, got_ref, out_ref):
    pos = pos_ref[:, :1]
    lane = iota((UNIQ, 8 * DEVICES), 1)
    for half in range(2):
        pick = onehot(lane == pos + 4 * half)
        out_ref[:, pl.ds(half * 256, 256)] = nn(pick, got_ref[...]).astype(BF)


def compact(pos_rows, got):
    return pl.pallas_call(
        compact_kernel,
        out_shape=jax.ShapeDtypeStruct((UNIQ, D), BF),
        compiler_params=params(),
        name="compact",
    )(pos_rows, got)


def row_mean(x):
    return jnp.sum(x, axis=-1, keepdims=True) * (1.0 / D)


def norm_parts(x):
    center = x - row_mean(x)
    spread = row_mean(center * center)
    inv = lax.rsqrt(spread + EPS)
    return center * inv, inv


def norm_grad(g, unit, inv):
    return inv * (g - row_mean(g) - unit * row_mean(g * unit))


def chunks(size, step=64):
    return [slice(r, r + step) for r in range(0, size, step)]


def side(ref, first, count, rs=slice(None)):
    return jnp.concatenate([ref[c, rs] for c in range(first, first + count)], axis=1)


def lay(ref, rs, value):
    for c in range(value.shape[1] // 128):
        ref[c, rs] = value[:, c * 128 : (c + 1) * 128].astype(BF)


ORDER = (6, 7, 4, 5, 2, 3, 0, 1)


def rows_body(long, one, two, counts, msg, rows, cot_ref, stage_ref, send, ready, acc_ref, fresh, refs):
    (win_ref, bin_ref, gin_ref, gmid_ref, wout_ref, bias_ref) = refs[:6]
    (hid, slope, wts, wslope, dpre, xs, unit_in, unit_mid, invs, narrow, wide) = refs[6:]
    size = MAXLEN
    every = slice(0, size)
    firsts, seconds = slice(0, 128), slice(128, 256)
    gin_half = 0.5 * gin_ref[...]
    start = jnp.where(long, 128, 0)
    lane = iota((1, 128), 1)
    ids_one, ids_two = msg
    line = jnp.concatenate(
        [
            jnp.where(lane < counts[0], ids_one[:, :128], -1),
            jnp.where(lane + start < counts[1], jnp.where(long, ids_one[:, 128:], ids_two[:, :128]), -1),
        ],
        axis=1,
    )
    cols = jnp.broadcast_to(line, (8, size)).astype(F32).T[:, :1].astype(I32)
    xs[...] = nn(onehot(iota((size, UNIQ), 1) == cols), rows)
    for rs in chunks(size):
        unit, inv = norm_parts(xs[rs])
        unit_in[rs] = unit
        invs[rs] = jnp.broadcast_to(inv, (rs.stop - rs.start, 128))
        lay(narrow, rs, unit * gin_half)
    for c in ORDER:
        ready(c)
        pre = nn(side(narrow, 0, 4, every), side(win_ref, 2 * c, 2))
        for k in range(2):
            blk = 2 * c + k
            half = pre[:, k * 128 : (k + 1) * 128] + 0.5 * bin_ref[:, pl.ds(blk * 128, 128)]
            up = 1.0 + jnp.tanh(half)
            act = half * up
            hid[blk] = act.astype(BF)
            slope[blk] = (up + act * (2.0 - up)).astype(BF)
    valid = [iota((128, 1), 0) < counts[0], iota((128, 1), 0) + start < counts[1]]
    per = []
    for part in range(2):
        inverse = 1.0 / jnp.full((1, 1), jnp.maximum(counts[part], 1), I32).astype(F32)
        per.append(jnp.where(valid[part], inverse, 0.0))
    cross = per[1] * jnp.where(long, 1.0, 0.0)
    blocks = ((0, 0, per[0]), (1, 1, per[1]), (1, 0, cross))
    cut = lambda i: slice(i * 128, i * 128 + 128)
    for h in range(HEADS):
        for bi, bj, scale in blocks:
            bias = bias_ref[h, (bi - bj) * 128 : (bi - bj) * 128 + 128, :]
            half = nt(hid[8 + h, cut(bi)], hid[12 + h, cut(bj)]) * (0.5 * SCALE) + bias
            up = 1.0 + jnp.tanh(half)
            act = half * up
            wts[h, bj, cut(bi)] = (act * scale).astype(BF)
            wslope[h, bj, cut(bi)] = ((up + act * (2.0 - up)) * (scale * (0.5 * SCALE))).astype(BF)
    for h in range(HEADS):
        for bi in range(2):
            wide[cut(bi), pl.ds(h * HEAD, HEAD)] = nn(
                side(wts.at[h], 0, bi + 1, cut(bi)), hid[4 + h, : (bi + 1) * 128]
            )
    for rs in chunks(size):
        unit, inv = norm_parts(wide[rs])
        unit_mid[rs] = unit
        lay(narrow, rs, unit * gmid_ref[...] * side(hid, 0, 4, rs).astype(F32))
        wide[rs, :128] = jnp.broadcast_to(inv, (rs.stop - rs.start, 128))
    ready(8)
    result = nn(side(narrow, 0, 4, every), side(wout_ref, 0, 4))
    other = jnp.where(long, one, two)
    for half, rs in enumerate((firsts, seconds)):
        stage_ref[rs] = jnp.where(valid[half], xs[rs] + result[rs], 0.0).astype(BF)
    send(one, 0, 0)
    send(other, pl.multiple_of(start, 128), 1)
    zero = jnp.zeros((), BF)
    lay(narrow, firsts, jnp.where(valid[0], cot_ref[one, :128, :], zero))
    lay(
        narrow,
        seconds,
        jnp.where(valid[1], cot_ref[other, pl.ds(pl.multiple_of(start, 128), 128), :], zero),
    )
    xs[...] = nt(side(narrow, 0, 4, every), side(wout_ref, 0, 4))
    for rs in chunks(size):
        unit = unit_mid[rs]
        inv = wide[rs, :1]
        grown = xs[rs] * gmid_ref[...]
        scaled = grown * unit
        for c in range(4):
            dpre[c, rs] = scaled[:, c * 128 : (c + 1) * 128].astype(BF) * slope[c, rs]
        lay(hid, rs, norm_grad(grown * side(hid, 0, 4, rs).astype(F32), unit, inv))
    for h in range(HEADS):
        for bi, bj, scale in blocks:
            ds = nt(hid[h, cut(bi)], hid[4 + h, cut(bj)]).astype(BF)
            wslope[h, bj, cut(bi)] = ds * wslope[h, bj, cut(bi)]
    for h in range(HEADS):
        for bi in range(2):
            dq = nn(side(wslope.at[h], 0, bi + 1, cut(bi)), hid[12 + h, : (bi + 1) * 128])
            dpre[8 + h, cut(bi)] = dq.astype(BF) * slope[8 + h, cut(bi)]
    for h in range(HEADS):
        for bj in range(2):
            qs = slice(bj * 128, size)
            dv = tn(wts[h, bj, qs], hid[h, qs])
            dpre[4 + h, cut(bj)] = dv.astype(BF) * slope[4 + h, cut(bj)]
            dk = tn(wslope[h, bj, qs], hid[8 + h, qs])
            dpre[12 + h, cut(bj)] = dk.astype(BF) * slope[12 + h, cut(bj)]
    wide[...] = nt(side(dpre, 0, 16, every), side(win_ref, 0, 16))
    for rs in chunks(size):
        dx = norm_grad(wide[rs] * gin_half, unit_in[rs], invs[rs, :1])
        lay(narrow, rs, dx + side(narrow, 0, 4, rs).astype(F32))
    sums = nn(onehot(iota((UNIQ, size), 0) == line), side(narrow, 0, 4, every))
    acc_ref[...] = jnp.where(fresh, sums, sums + acc_ref[...])


def layer_kernel(plan, aliased, *refs):
    deltas, each = plan
    n_src = len(deltas)
    n_each = len(each)
    refs = list(refs)
    info_ref = refs.pop(0)
    msgs = [refs.pop(0) for _ in range(n_src)]
    rows_refs = [refs.pop(0) for _ in range(n_src)]
    cot_ref = refs.pop(0)
    win_ref, bin_ref, gin_ref, gmid_ref, wout_ref, bias_ref = (refs.pop(0) for _ in range(6))
    if aliased:
        refs.pop(0)
    out_ref = refs.pop(0)
    part_refs = [refs.pop(0) for _ in range(n_src)]
    loads = {}
    if not aliased:
        win_hbm, wout_hbm = win_ref, wout_ref
        win_ref, wout_ref = refs.pop(0), refs.pop(0)
    rows, ids_sc, acc, stages, blank, wsems, osems, zsems = (refs.pop(0) for _ in range(8))
    if not aliased:
        for c in ORDER:
            part = pl.ds(2 * c, 2)
            loads[c] = pltpu.make_async_copy(win_hbm.at[part], win_ref.at[part], wsems.at[c])
        loads[8] = pltpu.make_async_copy(wout_hbm, wout_ref, wsems.at[8])
    for load in loads.values():
        load.start()
    work = (win_ref, bin_ref, gin_ref, gmid_ref, wout_ref, bias_ref, *refs)
    steps = n_src * n_each

    def place_of(d):
        delta = jnp.int32(deltas[0])
        for k in range(1, n_src):
            delta = jnp.where(d == k, deltas[k], delta)
        return ((info_ref[8] - delta + 4) % 4) * 2, [info_ref[delta * 2 + b] for b in each]

    def out_copy(t, place, start, half):
        return pltpu.make_async_copy(
            stages.at[t, pl.ds(half * 128, 128)],
            out_ref.at[place, pl.ds(start, 128)],
            osems.at[t, half],
        )

    def blank_copy(d, place, k):
        return pltpu.make_async_copy(
            blank, out_ref.at[place, pl.ds(128, 128)], zsems.at[d, k]
        )

    if n_each == 2:
        blank[...] = jnp.zeros((128, D), BF)

    def step(t, carry):
        d = t // n_each
        turn = t % n_each
        base, lens = place_of(d)
        if n_each == 1:
            one = base + each[0]
            two = one
            count, count_two = lens[0], lens[0]
            long = jnp.bool_(True)
        else:
            short = (lens[0] <= 128) & (lens[1] <= 128)
            one = base + turn
            two = base + 1
            count = jnp.where(turn == 0, lens[0], lens[1])
            count_two = lens[1]
            long = jnp.logical_not(short)

        def ready(c):
            if c in loads:
                loads[c].wait()

        def work_on():
            for k in range(n_src):

                @pl.when(d == k)
                def _():
                    for b in range(n_each):
                        ids_sc[b : b + 1, :] = msgs[k][each[b] : each[b] + 1, :MAXLEN]
                    rows[...] = rows_refs[k][...]

            if n_each == 2:

                @pl.when(short)
                def _():
                    for k in range(2):
                        blank_copy(d, base + k, k).start()

            ids_one = ids_sc[pl.ds(turn, 1), :]
            ids_two = ids_sc[n_each - 1 : n_each, :]
            rows_body(
                long,
                one,
                two,
                (count, jnp.where(long, count, count_two)),
                (ids_one, ids_two),
                rows[...],
                cot_ref,
                stages.at[t],
                lambda place, start, half: out_copy(t, place, start, half).start(),
                ready,
                acc,
                turn == 0,
                work,
            )
            for k in range(n_src):

                @pl.when(d == k)
                def _():
                    part_refs[k][...] = acc[...].astype(BF)

        if n_each == 1:
            work_on()
        else:
            pl.when((turn == 0) | long)(work_on)
        return carry

    if steps == 1:
        step(jnp.int32(0), 0)
    else:
        lax.fori_loop(0, steps, step, 0)
    for d in range(n_src):
        base, lens = place_of(d)
        for half in range(2):
            out_copy(d * n_each, base, 0, half).wait()
        if n_each == 2:
            short = (lens[0] <= 128) & (lens[1] <= 128)

            @pl.when(short)
            def _():
                for k in range(2):
                    blank_copy(d, base, k).wait()

            @pl.when(jnp.logical_not(short))
            def _():
                for half in range(2):
                    out_copy(d * 2 + 1, base, 0, half).wait()


def layer(plan, info, msgs, rows, cot, weights, prior):
    deltas, each = plan
    n_src = len(deltas)
    vmem = pl.BlockSpec(memory_space=pltpu.VMEM)
    hbm = pl.BlockSpec(memory_space=pltpu.HBM)
    args = [info, *msgs, *rows, cot, *weights]
    in_specs = [pl.BlockSpec(memory_space=pltpu.SMEM)] + [vmem] * (2 * n_src + 1)
    keep = [] if prior is not None else [weights[0], weights[4]]
    spec = vmem if prior is not None else hbm
    in_specs += [spec, vmem, vmem, vmem, spec, vmem]
    alias = {}
    if prior is not None:
        alias = {len(args): 0}
        args.append(prior)
        in_specs.append(hbm)
    part = jax.ShapeDtypeStruct((UNIQ, D), BF)
    dma = pltpu.SemaphoreType.DMA
    return pl.pallas_call(
        functools.partial(layer_kernel, plan, prior is not None),
        in_specs=in_specs,
        out_specs=[hbm] + [vmem] * (n_src + len(keep)),
        scratch_shapes=[
            pltpu.VMEM((UNIQ, D), BF),
            pltpu.VMEM((8, MAXLEN), I32),
            pltpu.VMEM((UNIQ, D), F32),
            pltpu.VMEM((n_src * len(each), MAXLEN, D), BF),
            pltpu.VMEM((128, D), BF),
            dma((9,)),
            dma((n_src * len(each), 2)),
            dma((n_src, 2)),
            pltpu.VMEM((16, MAXLEN, 128), BF),
            pltpu.VMEM((16, MAXLEN, 128), BF),
            pltpu.VMEM((HEADS, 2, MAXLEN, 128), BF),
            pltpu.VMEM((HEADS, 2, MAXLEN, 128), BF),
            pltpu.VMEM((16, MAXLEN, 128), BF),
            pltpu.VMEM((MAXLEN, D), F32),
            pltpu.VMEM((MAXLEN, D), F32),
            pltpu.VMEM((MAXLEN, D), F32),
            pltpu.VMEM((MAXLEN, 128), F32),
            pltpu.VMEM((4, MAXLEN, 128), BF),
            pltpu.VMEM((MAXLEN, D), F32),
        ],
        out_shape=[jax.ShapeDtypeStruct(cot.shape, BF)]
        + [part] * n_src
        + [jax.ShapeDtypeStruct(w.shape, BF) for w in keep],
        input_output_aliases=alias,
        compiler_params=params(),
        name="layer",
    )(*args)


def info_kernel(seq_ref, *refs):
    out_ref = refs[-1]
    for d in range(4):
        for b in range(2):
            out_ref[2 * d + b] = refs[d][b, MAXLEN]
    out_ref[8] = seq_ref[0]


def scalars(seq, msgs):
    smem = pl.BlockSpec(memory_space=pltpu.SMEM)
    return pl.pallas_call(
        info_kernel,
        in_specs=[smem] * 5,
        out_specs=smem,
        out_shape=jax.ShapeDtypeStruct((16,), I32),
        compiler_params=params(),
        name="scalars",
    )(seq, *msgs)


def expand_kernel(pos_ref, *refs):
    out_ref = refs[-1]
    total = refs[0][...].astype(F32)
    for r in refs[1:-1]:
        total = total + r[...].astype(F32)
    total = total.astype(BF)
    row = iota((8 * DEVICES, UNIQ), 0)
    pos = pos_ref[...]
    upper = nn(onehot(row == pos), total[:, : D // 2])
    lower = nn(onehot(row == pos + 4), total[:, D // 2 :])
    out_ref[...] = (upper + lower).astype(BF)


def expand(pos, parts):
    return pl.pallas_call(
        expand_kernel,
        out_shape=jax.ShapeDtypeStruct((8 * DEVICES, D // 2), BF),
        compiler_params=params(),
        name="expand",
    )(pos, *parts)


def asked_line_kernel(asked_ref, out_ref):
    parts = []
    shape = (DEVICES, 4 * DEVICES)
    spread = onehot(iota(shape, 0) == (iota(shape, 1) >> 2))
    for part in asked_parts(asked_ref):
        square = jnp.concatenate([part.astype(F32), jnp.zeros((DEVICES, 124), F32)], axis=1)
        parts.append(nn(square.T[:8].astype(BF), spread))
    value = parts[0] * 32.0 + parts[1]
    mine = iota((8, 4 * DEVICES), 0) == (iota((8, 4 * DEVICES), 1) & 3)
    out_ref[...] = jnp.sum(jnp.where(mine, value, 0.0), axis=0, keepdims=True).astype(I32)


def asked_line(asked):
    return pl.pallas_call(
        asked_line_kernel,
        out_shape=jax.ShapeDtypeStruct((1, 4 * DEVICES), I32),
        compiler_params=params(),
        name="asked_line",
    )(asked)


def scatter_kernel(line_ref, landed_ref, out_ref, whole_ref):
    size = out_ref.shape[0]

    @pl.when(pl.program_id(0) == 0)
    def _():
        whole_ref[...] = from_halves(landed_ref[...].astype(F32)).astype(BF)

    row = iota((size, 4 * DEVICES), 0) + pl.program_id(0) * size
    out_ref[...] = nn(onehot(row == line_ref[...]), whole_ref[...])


def scatter(line, landed):
    size = 256
    whole = lambda a: pl.BlockSpec(a.shape, lambda i: (0, 0), pipeline_mode=pl.Buffered(1))
    return pl.pallas_call(
        scatter_kernel,
        grid=(ROWS_DEV // size,),
        in_specs=[whole(line), whole(landed)],
        out_specs=pl.BlockSpec((size, D), lambda i: (i, 0)),
        out_shape=jax.ShapeDtypeStruct((ROWS_DEV, D), F32),
        scratch_shapes=[pltpu.VMEM((4 * DEVICES, D), BF)],
        compiler_params=params(dimension_semantics=("arbitrary",)),
        name="scatter",
    )(line, landed)


def ring(delta):
    return [(i, (i + delta) % 4) for i in range(4)]


def exchange(x, shape):
    got = lax.all_to_all(x.reshape(shape), ("emb", "seq"), split_axis=0, concat_axis=0, tiled=True)
    return got.reshape(x.shape)


PLANS = (((0,), (0,)), ((1,), (0, 1)), ((3, 2), (0, 1)), ((0,), (1,)))


def program(
    item_table,
    unique_ids,
    inverse,
    lengths,
    assignment,
    proj_in,
    bias_in,
    gain_in,
    gain_mid,
    proj_out,
    position_bias,
    cotangent,
):
    seq = lax.axis_index("seq").astype(I32).reshape(1)
    req, pos, *sent = pack(assignment, lengths, seq, unique_ids, inverse)
    asked = exchange(req, (DEVICES, 1, 4))
    msgs = [sent[0]] + [lax.ppermute(sent[d], "seq", ring(d)) for d in (1, 2, 3)]
    bias, pos_rows, win, wout = tables(position_bias, pos, proj_in, proj_out)
    answer = answer_rows(asked, item_table)
    got = exchange(answer, (DEVICES, 8, D // 2))
    info = scalars(seq, msgs)
    got, info = lax.optimization_barrier((got, info))
    line = asked_line(asked)
    own = compact(pos_rows, got)
    rows = [own]
    for d in (1, 2, 3):
        rows.append(lax.ppermute(own, "seq", ring(d)))
    weights = (
        in_hbm(win),
        bias_in.reshape(1, 4 * D),
        gain_in.reshape(1, D),
        gain_mid.reshape(1, D),
        in_hbm(wout),
        bias,
    )
    outputs = None
    sums = []
    for plan in PLANS:
        outputs, *parts = layer(
            plan,
            info,
            [msgs[d] for d in plan[0]],
            [rows[d] for d in plan[0]],
            cotangent,
            weights,
            outputs,
        )
        if len(parts) > len(plan[0]):
            weights = (parts[-2], *weights[1:4], parts[-1], weights[5])
        for d, part in zip(plan[0], parts):
            sums.append(part if d == 0 else lax.ppermute(part, "seq", ring(-d)))
    landed = exchange(expand(pos, sums), (DEVICES, 8, D // 2))
    return (outputs, scatter(line, landed))


def solution(mesh):
    both = ("emb", "seq")
    in_specs = (
        P(both, None),
        P(both),
        P(both, None),
        P(both),
        P(both),
        P(),
        P(),
        P(),
        P(),
        P(),
        P(),
        P(both, None, None),
    )
    out_specs = (P(both, None, None), P(both, None))
    return jax.shard_map(program, mesh=mesh, in_specs=in_specs, out_specs=out_specs, check_vma=False)
```

time: 124 us -> 115 us (0.927)
  waiting for transfers between devices: 32.1 us -> 19.8 us
  local copies, waits for them, and re-layouts: 9.64 us -> 0.21 us
  Pallas kernels: 39.6 us -> 46.9 us
  starting transfers between devices: 20.3 us -> 26.3 us
    unnamed x30 -> x10, local copies, waits for them, and re-layouts: 9.46 us -> 0.03 us
    ppermute x3, waiting for transfers between devices: 6.34 us -> 0.01 us  [program(): rows.append(lax.ppermute(own, 'seq', ring(d)))]
    ppermute x3, waiting for transfers between devices: 8.06 us -> 2.18 us  [program(): sums.append(part if d == 0 else lax.ppermute(part, 'seq', ring(-d)))]
    pallas_call x3 -> x4, Pallas kernels: 28.4 us -> 33 us  [layer(): pl.pallas_call(functools.partial(layer_kernel, plan, prior is not None),...]
    all_to_all x2, starting transfers between devices: 10.3 us -> 14.1 us  [exchange(): lax.all_to_all(x.reshape(shape), ('emb', 'seq'), split_axis=0, concat_axi...]
    pallas_call x1, Pallas kernels: 0.65 us -> 3.6 us  [tables(): pl.pallas_call(tables_kernel, out_shape=[jax.ShapeDtypeStruct((HEADS, MAX...]
    ppermute x3, starting transfers between devices: 2.2 us -> 4.38 us  [program(): sums.append(part if d == 0 else lax.ppermute(part, 'seq', ring(-d)))]
    pallas_call x3 -> x4, Pallas kernels: 4.68 us -> 5.79 us  [the longest x1 2.74 us: answer_rows(): pl.pallas_call(answer_kernel, in_specs=[pl.BlockSpec(memory_space=pltpu.V...]
  transfers between devices with their start and end apart: 11 -> 11, of which waited for: 7 -> 3; matrix products, arithmetic and copies ran while one was open for 0% -> 0% of each run, Pallas kernels for 8% -> 20%
where the time goes in v4:
time: 115 us
  Pallas kernels  46.9 us (41%)
  starting transfers between devices  26.3 us (23%)
  blocking collectives  21 us (18%)
  waiting for transfers between devices  19.8 us (17%)
    pallas_call x4, Pallas kernels, layer(): pl.pallas_call(functools.partial(layer_kernel, plan, prior is not None),...  33 us
    all_to_all x1, blocking collectives, exchange(): lax.all_to_all(x.reshape(shape), ('emb', 'seq'), split_axis=0, concat_axi...  21 us
    all_to_all x2, waiting for transfers between devices, exchange(): lax.all_to_all(x.reshape(shape), ('emb', 'seq'), split_axis=0, concat_axi...  17.6 us
    all_to_all x2, starting transfers between devices, exchange(): lax.all_to_all(x.reshape(shape), ('emb', 'seq'), split_axis=0, concat_axi...  14.1 us
    ppermute x3, starting transfers between devices, program(): lax.ppermute(sent[d], 'seq', ring(d))  5.01 us
    ppermute x3, starting transfers between devices, program(): sums.append(part if d == 0 else lax.ppermute(part, 'seq', ring(-d)))  4.38 us
    pallas_call x1, Pallas kernels, tables(): pl.pallas_call(tables_kernel, out_shape=[jax.ShapeDtypeStruct((HEADS, MAX...  3.6 us
    ppermute x3, starting transfers between devices, program(): rows.append(lax.ppermute(own, 'seq', ring(d)))  2.85 us
  transfers between devices with their start and end apart: 11, of which 3 were waited for; matrix products, arithmetic and copies ran while one was open for 0% of the time, Pallas kernels for 20%

profile of v4, /device:TPU:1, one launch (start us, length us, event | category | flops | bytes accessed | tf_op | source)
XLA Modules:
  0.0 115.1 jit_solution(3256151937779112623)
XLA Ops:
  0.6 0.0 copy-start.4
  0.6 1.5 %pack.1 = (s32[128,4]{1,0:T(8,128)S(1)}, s32[1,256]{1,0:T(1,128)S(1)}, s32[2,384]{1,0:T(2,128)S(1)}, s32[2,384]{1,0:T(2,128)S(1)}, s32[2,384]{1,0:T(2,128)S(1)}, /*index=5*/s32[2,384]{1,0:T(2,128)S(1)}) custom-call(s32[8]{0:T(128)} %assign_hbm.1, s32[8]{0:T(128)} %len_hbm.1, s32[1]{0:T(128)} %bitcast.seq_ref, s32[1,256]{1,0:T(1,128)} %bitcast.30, ...), custom_call_target="tpu_custom_call" | custom-call | tf_op jit(solution)/shard_map/pack/pallas_call | solution.py:107
  2.2 21.0 %all_to_all.15 = s32[128,1,4]{2,1,0:T(1,128)S(1)} all-to-all(s32[128,1,4]{2,1,0:T(1,128)S(1)} %bitcast.21), channel_id=1, replica_groups=mesh['emb'=32,'seq'=4] {'emb','seq'}, dimensions={0} | all-to-all | bytes 4096 | tf_op jit(solution)/shard_map/all_to_all | solution.py:680
  23.2 2.7 %answer.1 = bf16[1024,256]{1,0:T(8,128)(2,1)} custom-call(s32[128,4]{1,0:T(8,128)S(1)} %bitcast.15, bf16[1024,512]{1,0:T(8,128)(2,1)} %table_hbm.1), custom_call_target="tpu_custom_call" | custom-call | tf_op jit(solution)/shard_map/answer/pallas_call | solution.py:229
  25.9 0.0 copy-start
  25.9 0.0 copy-start.1
  25.9 0.0 copy-start.2
  25.9 0.0 copy-start.3
  26.0 4.3 %all-to-all-start.1 = ((bf16[128,8,256]{2,1,0:T(8,128)(2,1)}), bf16[128,8,256]{2,1,0:T(8,128)(2,1)S(1)}, u32[]{:S(2)}, u32[]{:S(2)}) async-start(bf16[128,8,256]{2,1,0:T(8,128)(2,1)} %bitcast.5), calls=%async_computation.1 | async-start | bytes 1048576 | tf_op jit(solution)/shard_map/all_to_all | solution.py:680
  30.2 1.4 %collective-permute-start = (s32[2,384]{1,0:T(2,128)S(1)}, s32[2,384]{1,0:T(2,128)S(1)}, u32[]{:S(2)}, u32[]{:S(2)}) collective-permute-start(s32[2,384]{1,0:T(2,128)S(1)} %get-tuple-element.27), channel_id=1, source_target_pairs={{0,1},{1,2},{2,3},{3,0},{4,5},{5,6},{6,7},{7,4},{8,9},{9,10},{10,1... | collective-permute-start | bytes 9224 | tf_op jit(solution)/shard_map/ppermute | solution.py:704
  31.7 2.4 %collective-permute-start.1 = (s32[2,384]{1,0:T(2,128)S(1)}, s32[2,384]{1,0:T(2,128)S(1)}, u32[]{:S(2)}, u32[]{:S(2)}) collective-permute-start(s32[2,384]{1,0:T(2,128)S(1)} %get-tuple-element.28), channel_id=1, source_target_pairs={{0,2},{1,3},{2,0},{3,1},{4,6},{5,7},{6,4},{7,5},{8,10},{9,11},{10,... | collective-permute-start | bytes 9224 | tf_op jit(solution)/shard_map/ppermute | solution.py:704
  34.1 1.2 %collective-permute-start.2 = (s32[2,384]{1,0:T(2,128)S(1)}, s32[2,384]{1,0:T(2,128)S(1)}, u32[]{:S(2)}, u32[]{:S(2)}) collective-permute-start(s32[2,384]{1,0:T(2,128)S(1)} %get-tuple-element.29), channel_id=1, source_target_pairs={{0,3},{1,0},{2,1},{3,2},{4,7},{5,4},{6,5},{7,6},{8,11},{9,8},{10,9... | collective-permute-start | bytes 9224 | tf_op jit(solution)/shard_map/ppermute | solution.py:704
  35.2 0.0 copy-done.4
  35.2 0.2 rev.3.flipped_ref
  35.4 3.6 %tables.1 = (f32[4,256,128]{2,1,0:T(8,128)S(1)}, s32[256,128]{1,0:T(8,128)S(1)}, bf16[16,512,128]{2,1,0:T(8,128)(2,1)}, bf16[4,512,128]{2,1,0:T(8,128)(2,1)}) custom-call(f32[4,256]{1,0:T(4,128)S(1)} %rev.3.flipped_ref, s32[1,256]{1,0:T(1,128)S(1)} %get-tuple-element.31.pos_ref, bf16[512,2048]{1,0:T(8,128)(2,1)} %win_hbm.1, bf16[512,512]{1,0:T(8,128)(2,1)} %wout_hbm.1), custom_call_target="tpu_custom_call" | custom-call | tf_op jit(solution)/shard_map/tables/pallas_call | solution.py:162
  39.0 0.0 collective-permute-done.refs_1_
  39.1 0.0 collective-permute-done.1.refs_2_
  39.1 0.0 collective-permute-done.2.refs_3_.refs_1_
  39.1 1.3 %scalars.1.refs_0_ = s32[16]{0:T(128)S(1)} custom-call(s32[1]{0:T(128)} %bitcast.seq_ref, s32[2,384]{1,0:T(2,128)S(1)} %get-tuple-element.26.refs_0_.refs_1_, s32[2,384]{1,0:T(2,128)S(1)} %collective-permute-done.refs_1_, s32[2,384]{1,0:T(2,128)S(1)} %collective-permute-done.1.refs_2_, s32[2,384]{1,0:T(2,128)S(1)} %collective-permute-done.2.refs_3_.refs_1_), custom_call_target="tpu_custom_call" | custom-call | tf_op jit(solution)/shard_map/scalars/pallas_call | solution.py:596
  40.4 3.9 %all-to-all-done.1 = bf16[128,8,256]{2,1,0:T(8,128)(2,1)S(1)} async-done(((bf16[128,8,256]{2,1,0:T(8,128)(2,1)}), bf16[128,8,256]{2,1,0:T(8,128)(2,1)S(1)}, u32[]{:S(2)}, u32[]{:S(2)}) %all-to-all-start.1) | async-done | bytes 524320 | tf_op jit(solution)/shard_map/all_to_all | solution.py:680
  44.3 0.5 compact.1.refs_2_
  44.8 0.4 collective-permute-start.5
  45.2 1.9 %collective-permute-start.4 = (bf16[256,512]{1,0:T(8,128)(2,1)S(1)}, bf16[256,512]{1,0:T(8,128)(2,1)S(1)}, u32[]{:S(2)}, u32[]{:S(2)}) collective-permute-start(bf16[256,512]{1,0:T(8,128)(2,1)S(1)} %compact.1.refs_2_), channel_id=1, source_target_pairs={{0,2},{1,3},{2,0},{3,1},{4,6},{5,7},{6,4},{7,5},{8,10},{9,11},{10,... | collective-permute-start | bytes 786440 | tf_op jit(solution)/shard_map/ppermute | solution.py:714
  47.0 0.6 collective-permute-start.3
  47.7 0.0 copy-done
  47.7 0.0 copy-done.1
  47.7 0.0 copy-done.2
  47.7 0.0 copy-done.3
  47.7 7.2 %layer.4 = (bf16[8,256,512]{2,1,0:T(8,128)(2,1)}, bf16[256,512]{1,0:T(8,128)(2,1)S(1)}, bf16[16,512,128]{2,1,0:T(8,128)(2,1)S(1)}, bf16[4,512,128]{2,1,0:T(8,128)(2,1)S(1)}) custom-call(s32[16]{0:T(128)S(1)} %scalars.1.refs_0_, s32[2,384]{1,0:T(2,128)S(1)} %get-tuple-element.26.refs_0_.refs_1_, bf16[256,512]{1,0:T(8,128)(2,1)S(1)} %compact.1.refs_2_, ...), custom_call_target="tpu_custom_call" | custom-call | tf_op jit(solution)/shard_map/layer/pallas_call | solution.py:552
  54.9 0.0 collective-permute-done.5.refs_2_
  54.9 5.8 %layer.5 = (bf16[8,256,512]{2,1,0:T(8,128)(2,1)}, bf16[256,512]{1,0:T(8,128)(2,1)S(1)}) custom-call(s32[16]{0:T(128)S(1)} %scalars.1.refs_0_, s32[2,384]{1,0:T(2,128)S(1)} %collective-permute-done.refs_1_, bf16[256,512]{1,0:T(8,128)(2,1)S(1)} %collective-permute-done.5.refs_2_, bf16[8,256,512]{2,1,0:T(8,128)(2,1)S(1)} %copy-done, ...), custom_call_target="tpu_custom_call", output_to_operand_aliasing={{0}: (10, {})} | custom-call | tf_op jit(solution)/shard_map/layer/pallas_call | solution.py:552
  60.7 0.0 collective-permute-done.4.refs_4_
  60.7 0.0 collective-permute-done.3.refs_3_
  60.7 14.8 %layer.6 = (bf16[8,256,512]{2,1,0:T(8,128)(2,1)}, bf16[256,512]{1,0:T(8,128)(2,1)S(1)}, bf16[256,512]{1,0:T(8,128)(2,1)S(1)}) custom-call(s32[16]{0:T(128)S(1)} %scalars.1.refs_0_, s32[2,384]{1,0:T(2,128)S(1)} %collective-permute-done.2.refs_3_.refs_1_, s32[2,384]{1,0:T(2,128)S(1)} %collective-permute-done.1.refs_2_, ...), custom_call_target="tpu_custom_call", output_to_operand_aliasing={{0}: (12, {})} | custom-call | tf_op jit(solution)/shard_map/layer/pallas_call | solution.py:552
  75.6 0.1 collective-permute-start.7
  75.6 3.0 %collective-permute-start.8 = (bf16[256,512]{1,0:T(8,128)(2,1)S(1)}, bf16[256,512]{1,0:T(8,128)(2,1)S(1)}, u32[]{:S(2)}, u32[]{:S(2)}) collective-permute-start(bf16[256,512]{1,0:T(8,128)(2,1)S(1)} %get-tuple-element.46), channel_id=1, source_target_pairs={{0,2},{1,3},{2,0},{3,1},{4,6},{5,7},{6,4},{7,5},{8,10},{9,11},{10,... | collective-permute-start | bytes 786440 | tf_op jit(solution)/shard_map/ppermute | solution.py:738
  78.6 1.3 %collective-permute-start.6 = (bf16[256,512]{1,0:T(8,128)(2,1)S(1)}, bf16[256,512]{1,0:T(8,128)(2,1)S(1)}, u32[]{:S(2)}, u32[]{:S(2)}) collective-permute-start(bf16[256,512]{1,0:T(8,128)(2,1)S(1)} %get-tuple-element.44), channel_id=1, source_target_pairs={{0,3},{1,0},{2,1},{3,2},{4,7},{5,4},{6,5},{7,6},{8,11},{9,8},{10,9... | collective-permute-start | bytes 786440 | tf_op jit(solution)/shard_map/ppermute | solution.py:738
  79.9 5.2 %layer.7 = (bf16[8,256,512]{2,1,0:T(8,128)(2,1)}, bf16[256,512]{1,0:T(8,128)(2,1)S(1)}) custom-call(s32[16]{0:T(128)S(1)} %scalars.1.refs_0_, s32[2,384]{1,0:T(2,128)S(1)} %get-tuple-element.26.refs_0_.refs_1_, bf16[256,512]{1,0:T(8,128)(2,1)S(1)} %compact.1.refs_2_, bf16[8,256,512]{2,1,0:T(8,128)(2,1)S(1)} %copy-done, ...), custom_call_target="tpu_custom_call", output_to_operand_aliasing={{0}: (10, {})} | custom-call | tf_op jit(solution)/shard_map/layer/pallas_call | solution.py:552
  85.2 0.0 collective-permute-done.7.refs_2_
  85.2 2.2 %collective-permute-done.8.refs_3_ = bf16[256,512]{1,0:T(8,128)(2,1)S(1)} collective-permute-done((bf16[256,512]{1,0:T(8,128)(2,1)S(1)}, bf16[256,512]{1,0:T(8,128)(2,1)S(1)}, u32[]{:S(2)}, u32[]{:S(2)}) %collective-permute-start.8) | collective-permute-done | bytes 262176 | tf_op jit(solution)/shard_map/ppermute | solution.py:738
  87.3 0.0 collective-permute-done.6.refs_1_
  87.3 1.4 %expand.1 = bf16[1024,256]{1,0:T(8,128)(2,1)} custom-call(s32[1,256]{1,0:T(1,128)S(1)} %get-tuple-element.31.pos_ref, bf16[256,512]{1,0:T(8,128)(2,1)S(1)} %get-tuple-element.43.refs_0_, bf16[256,512]{1,0:T(8,128)(2,1)S(1)} %collective-permute-done.6.refs_1_, bf16[256,512]{1,0:T(8,128)(2,1)S(1)} %collective-permute-done.7.refs_2_, ...), custom_call_target="tpu_custom_call" | custom-call | tf_op jit(solution)/shard_map/expand/pallas_call | solution.py:620
  88.7 9.8 %all-to-all-start.2 = ((bf16[128,8,256]{2,1,0:T(8,128)(2,1)}), bf16[128,8,256]{2,1,0:T(8,128)(2,1)S(1)}, u32[]{:S(2)}, u32[]{:S(2)}) async-start(bf16[128,8,256]{2,1,0:T(8,128)(2,1)} %bitcast.10), calls=%async_computation.2 | async-start | bytes 1048576 | tf_op jit(solution)/shard_map/all_to_all | solution.py:680
  98.6 0.2 asked_line.1.line_ref
  98.8 13.7 %all-to-all-done.2 = bf16[128,8,256]{2,1,0:T(8,128)(2,1)S(1)} async-done(((bf16[128,8,256]{2,1,0:T(8,128)(2,1)}), bf16[128,8,256]{2,1,0:T(8,128)(2,1)S(1)}, u32[]{:S(2)}, u32[]{:S(2)}) %all-to-all-start.2) | async-done | bytes 524320 | tf_op jit(solution)/shard_map/all_to_all | solution.py:680
  112.5 2.6 %scatter.1 = f32[1024,512]{1,0:T(8,128)} custom-call(s32[1,512]{1,0:T(1,128)S(1)} %asked_line.1.line_ref, bf16[1024,256]{1,0:T(8,128)(2,1)S(1)} %bitcast.14), custom_call_target="tpu_custom_call" | custom-call | tf_op jit(solution)/shard_map/scatter/pallas_call | solution.py:663
Async XLA Ops:
  0.6 34.6 %copy-start.4 = (f32[4,256]{1,0:T(4,128)S(1)}, f32[4,256]{1,0:T(4,128)}, u32[]{:S(2)}) copy-start(f32[4,256]{1,0:T(4,128)} %param.22) | copy-start | bytes 12292
  25.9 21.8 %copy-start = (bf16[8,256,512]{2,1,0:T(8,128)(2,1)S(1)}, bf16[8,256,512]{2,1,0:T(8,128)(2,1)}, u32[]{:S(2)}) copy-start(bf16[8,256,512]{2,1,0:T(8,128)(2,1)} %refs_3_.5) | copy-start | bytes 6291460
  25.9 21.7 %copy-start.1 = (f32[2048]{0:T(1024)S(1)}, f32[2048]{0:T(1024)}, u32[]{:S(2)}) copy-start(f32[2048]{0:T(1024)} %param.18) | copy-start | bytes 24580
  25.9 21.7 %copy-start.2 = (f32[512]{0:T(512)S(1)}, f32[512]{0:T(512)}, u32[]{:S(2)}) copy-start(f32[512]{0:T(512)} %param.19) | copy-start | bytes 6148
  25.9 21.7 %copy-start.3 = (f32[512]{0:T(512)S(1)}, f32[512]{0:T(512)}, u32[]{:S(2)}) copy-start(f32[512]{0:T(512)} %param.20) | copy-start | bytes 6148
  26.0 18.4 %all-to-all-start.1 = ((bf16[128,8,256]{2,1,0:T(8,128)(2,1)}), bf16[128,8,256]{2,1,0:T(8,128)(2,1)S(1)}, u32[]{:S(2)}, u32[]{:S(2)}) async-start(bf16[128,8,256]{2,1,0:T(8,128)(2,1)} %bitcast.5), calls=%async_computation.1 | async-start | bytes 1048576 | tf_op jit(solution)/shard_map/all_to_all | solution.py:680
  30.2 8.8 %collective-permute-start = (s32[2,384]{1,0:T(2,128)S(1)}, s32[2,384]{1,0:T(2,128)S(1)}, u32[]{:S(2)}, u32[]{:S(2)}) collective-permute-start(s32[2,384]{1,0:T(2,128)S(1)} %get-tuple-element.27), channel_id=1, source_target_pairs={{0,1},{1,2},{2,3},{3,0},{4,5},{5,6},{6,7},{7,4},{8,9},{9,10},{10,1... | collective-permute-start | bytes 9224 | tf_op jit(solution)/shard_map/ppermute | solution.py:704
  31.7 7.4 %collective-permute-start.1 = (s32[2,384]{1,0:T(2,128)S(1)}, s32[2,384]{1,0:T(2,128)S(1)}, u32[]{:S(2)}, u32[]{:S(2)}) collective-permute-start(s32[2,384]{1,0:T(2,128)S(1)} %get-tuple-element.28), channel_id=1, source_target_pairs={{0,2},{1,3},{2,0},{3,1},{4,6},{5,7},{6,4},{7,5},{8,10},{9,11},{10,... | collective-permute-start | bytes 9224 | tf_op jit(solution)/shard_map/ppermute | solution.py:704
  34.1 5.0 %collective-permute-start.2 = (s32[2,384]{1,0:T(2,128)S(1)}, s32[2,384]{1,0:T(2,128)S(1)}, u32[]{:S(2)}, u32[]{:S(2)}) collective-permute-start(s32[2,384]{1,0:T(2,128)S(1)} %get-tuple-element.29), channel_id=1, source_target_pairs={{0,3},{1,0},{2,1},{3,2},{4,7},{5,4},{6,5},{7,6},{8,11},{9,8},{10,9... | collective-permute-start | bytes 9224 | tf_op jit(solution)/shard_map/ppermute | solution.py:704
  44.8 10.1 %collective-permute-start.5 = (bf16[256,512]{1,0:T(8,128)(2,1)S(1)}, bf16[256,512]{1,0:T(8,128)(2,1)S(1)}, u32[]{:S(2)}, u32[]{:S(2)}) collective-permute-start(bf16[256,512]{1,0:T(8,128)(2,1)S(1)} %compact.1.refs_2_), channel_id=1, source_target_pairs={{0,1},{1,2},{2,3},{3,0},{4,5},{5,6},{6,7},{7,4},{8,9},{9,10},{10,1... | collective-permute-start | bytes 786440 | tf_op jit(solution)/shard_map/ppermute | solution.py:714
  45.2 15.5 %collective-permute-start.4 = (bf16[256,512]{1,0:T(8,128)(2,1)S(1)}, bf16[256,512]{1,0:T(8,128)(2,1)S(1)}, u32[]{:S(2)}, u32[]{:S(2)}) collective-permute-start(bf16[256,512]{1,0:T(8,128)(2,1)S(1)} %compact.1.refs_2_), channel_id=1, source_target_pairs={{0,2},{1,3},{2,0},{3,1},{4,6},{5,7},{6,4},{7,5},{8,10},{9,11},{10,... | collective-permute-start | bytes 786440 | tf_op jit(solution)/shard_map/ppermute | solution.py:714
  47.0 13.7 %collective-permute-start.3 = (bf16[256,512]{1,0:T(8,128)(2,1)S(1)}, bf16[256,512]{1,0:T(8,128)(2,1)S(1)}, u32[]{:S(2)}, u32[]{:S(2)}) collective-permute-start(bf16[256,512]{1,0:T(8,128)(2,1)S(1)} %compact.1.refs_2_), channel_id=1, source_target_pairs={{0,3},{1,0},{2,1},{3,2},{4,7},{5,4},{6,5},{7,6},{8,11},{9,8},{10,9... | collective-permute-start | bytes 786440 | tf_op jit(solution)/shard_map/ppermute | solution.py:714
  75.6 9.6 %collective-permute-start.7 = (bf16[256,512]{1,0:T(8,128)(2,1)S(1)}, bf16[256,512]{1,0:T(8,128)(2,1)S(1)}, u32[]{:S(2)}, u32[]{:S(2)}) collective-permute-start(bf16[256,512]{1,0:T(8,128)(2,1)S(1)} %get-tuple-element.45), channel_id=1, source_target_pairs={{0,1},{1,2},{2,3},{3,0},{4,5},{5,6},{6,7},{7,4},{8,9},{9,10},{10,1... | collective-permute-start | bytes 786440 | tf_op jit(solution)/shard_map/ppermute | solution.py:738
  75.6 11.7 %collective-permute-start.8 = (bf16[256,512]{1,0:T(8,128)(2,1)S(1)}, bf16[256,512]{1,0:T(8,128)(2,1)S(1)}, u32[]{:S(2)}, u32[]{:S(2)}) collective-permute-start(bf16[256,512]{1,0:T(8,128)(2,1)S(1)} %get-tuple-element.46), channel_id=1, source_target_pairs={{0,2},{1,3},{2,0},{3,1},{4,6},{5,7},{6,4},{7,5},{8,10},{9,11},{10,... | collective-permute-start | bytes 786440 | tf_op jit(solution)/shard_map/ppermute | solution.py:738
  78.6 8.7 %collective-permute-start.6 = (bf16[256,512]{1,0:T(8,128)(2,1)S(1)}, bf16[256,512]{1,0:T(8,128)(2,1)S(1)}, u32[]{:S(2)}, u32[]{:S(2)}) collective-permute-start(bf16[256,512]{1,0:T(8,128)(2,1)S(1)} %get-tuple-element.44), channel_id=1, source_target_pairs={{0,3},{1,0},{2,1},{3,2},{4,7},{5,4},{6,5},{7,6},{8,11},{9,8},{10,9... | collective-permute-start | bytes 786440 | tf_op jit(solution)/shard_map/ppermute | solution.py:738
  88.7 23.8 %all-to-all-start.2 = ((bf16[128,8,256]{2,1,0:T(8,128)(2,1)}), bf16[128,8,256]{2,1,0:T(8,128)(2,1)S(1)}, u32[]{:S(2)}, u32[]{:S(2)}) async-start(bf16[128,8,256]{2,1,0:T(8,128)(2,1)} %bitcast.10), calls=%async_computation.2 | async-start | bytes 1048576 | tf_op jit(solution)/shard_map/all_to_all | solution.py:680

commit v5 on v4

--- a/solution.py
+++ b/solution.py
@@ -210,8 +210,12 @@
 
 
 def answer_kernel(asked_ref, table_hbm, out_ref, table_ref, pick_ref, sem):
-    load = pltpu.make_async_copy(table_hbm, table_ref, sem.at[0])
-    load.start()
+    loads = []
+    for c in range(4):
+        part = pl.ds(c * 256, 256)
+        loads.append(pltpu.make_async_copy(table_hbm.at[part], table_ref.at[part], sem.at[c]))
+    for load in loads:
+        load.start()
     high, low = asked_parts(asked_ref)
     count = 4 * DEVICES
     spread = onehot((iota((count, DEVICES), 0) >> 2) == iota((count, DEVICES), 1))
@@ -219,7 +223,8 @@
     mine = iota((count, 4), 1) == (iota((count, 4), 0) & 3)
     col = jnp.sum(jnp.where(mine, value, 0.0), axis=1, keepdims=True).astype(I32)
     pick_ref[...] = onehot(iota((count, ROWS_DEV), 1) == col)
-    load.wait()
+    for load in loads:
+        load.wait()
     for c in range(2):
         rows = nn(pick_ref[pl.ds(c * 256, 256), :], table_ref[...])
         out_ref[pl.ds(c * 512, 512), :] = to_halves(rows).astype(BF)
@@ -233,7 +238,7 @@
         scratch_shapes=[
             pltpu.VMEM((ROWS_DEV, D), BF),
             pltpu.VMEM((4 * DEVICES, ROWS_DEV), BF),
-            pltpu.SemaphoreType.DMA((1,)),
+            pltpu.SemaphoreType.DMA((4,)),
         ],
         compiler_params=params(),
         name="answer",
@@ -319,9 +324,10 @@
             blk = 2 * c + k
             half = pre[:, k * 128 : (k + 1) * 128] + 0.5 * bin_ref[:, pl.ds(blk * 128, 128)]
             up = 1.0 + jnp.tanh(half)
-            act = half * up
-            hid[blk] = act.astype(BF)
-            slope[blk] = (up + act * (2.0 - up)).astype(BF)
+            act = (half * up).astype(BF)
+            up = up.astype(BF)
+            hid[blk] = act
+            slope[blk] = up + act * (jnp.array(2.0, BF) - up)
     valid = [iota((128, 1), 0) < counts[0], iota((128, 1), 0) + start < counts[1]]
     per = []
     for part in range(2):
@@ -394,10 +400,12 @@
     acc_ref[...] = jnp.where(fresh, sums, sums + acc_ref[...])
 
 
+BOTH, EARLY, LATE = range(3)
+
+
 def layer_kernel(plan, aliased, *refs):
-    deltas, each = plan
+    deltas, mode = plan
     n_src = len(deltas)
-    n_each = len(each)
     refs = list(refs)
     info_ref = refs.pop(0)
     msgs = [refs.pop(0) for _ in range(n_src)]
@@ -408,11 +416,11 @@
         refs.pop(0)
     out_ref = refs.pop(0)
     part_refs = [refs.pop(0) for _ in range(n_src)]
-    loads = {}
+    win_hbm, wout_hbm = win_ref, wout_ref
     if not aliased:
-        win_hbm, wout_hbm = win_ref, wout_ref
         win_ref, wout_ref = refs.pop(0), refs.pop(0)
     rows, ids_sc, acc, stages, blank, wsems, osems, zsems = (refs.pop(0) for _ in range(8))
+    loads = {}
     if not aliased:
         for c in ORDER:
             part = pl.ds(2 * c, 2)
@@ -421,13 +429,22 @@
     for load in loads.values():
         load.start()
     work = (win_ref, bin_ref, gin_ref, gmid_ref, wout_ref, bias_ref, *refs)
-    steps = n_src * n_each
-
-    def place_of(d):
+
+    def ready(c):
+        if c in loads:
+            loads[c].wait()
+
+    turns = 2 if mode == BOTH else 1
+    steps = n_src * turns
+    blank[...] = jnp.zeros((128, D), BF)
+
+    def source(d):
         delta = jnp.int32(deltas[0])
         for k in range(1, n_src):
             delta = jnp.where(d == k, deltas[k], delta)
-        return ((info_ref[8] - delta + 4) % 4) * 2, [info_ref[delta * 2 + b] for b in each]
+        lens = [info_ref[delta * 2 + b] for b in range(2)]
+        base = ((info_ref[8] - delta + 4) % 4) * 2
+        return base, lens, (lens[0] <= 128) & (lens[1] <= 128)
 
     def out_copy(t, place, start, half):
         return pltpu.make_async_copy(
@@ -441,61 +458,49 @@
             blank, out_ref.at[place, pl.ds(128, 128)], zsems.at[d, k]
         )
 
-    if n_each == 2:
-        blank[...] = jnp.zeros((128, D), BF)
-
     def step(t, carry):
-        d = t // n_each
-        turn = t % n_each
-        base, lens = place_of(d)
-        if n_each == 1:
-            one = base + each[0]
-            two = one
-            count, count_two = lens[0], lens[0]
-            long = jnp.bool_(True)
+        d = t // turns
+        base, lens, short = source(d)
+        long = jnp.logical_not(short)
+        if mode == BOTH:
+            turn = t % turns
+            go = (turn == 0) | long
+        elif mode == EARLY:
+            turn = jnp.int32(0)
+            go = long
         else:
-            short = (lens[0] <= 128) & (lens[1] <= 128)
-            one = base + turn
-            two = base + 1
-            count = jnp.where(turn == 0, lens[0], lens[1])
-            count_two = lens[1]
-            long = jnp.logical_not(short)
-
-        def ready(c):
-            if c in loads:
-                loads[c].wait()
+            turn = jnp.where(short, 0, 1)
+            go = None
+        count = jnp.where(turn == 0, lens[0], lens[1])
 
         def work_on():
             for k in range(n_src):
 
                 @pl.when(d == k)
                 def _():
-                    for b in range(n_each):
-                        ids_sc[b : b + 1, :] = msgs[k][each[b] : each[b] + 1, :MAXLEN]
+                    ids_sc[:2, :] = msgs[k][:, :MAXLEN]
                     rows[...] = rows_refs[k][...]
 
-            if n_each == 2:
+            if mode != EARLY:
 
                 @pl.when(short)
                 def _():
                     for k in range(2):
                         blank_copy(d, base + k, k).start()
 
-            ids_one = ids_sc[pl.ds(turn, 1), :]
-            ids_two = ids_sc[n_each - 1 : n_each, :]
             rows_body(
                 long,
-                one,
-                two,
-                (count, jnp.where(long, count, count_two)),
-                (ids_one, ids_two),
+                base + turn,
+                base + 1,
+                (count, jnp.where(long, count, lens[1])),
+                (ids_sc[pl.ds(turn, 1), :], ids_sc[1:2, :]),
                 rows[...],
                 cot_ref,
                 stages.at[t],
                 lambda place, start, half: out_copy(t, place, start, half).start(),
                 ready,
                 acc,
-                turn == 0,
+                (turn == 0) | (mode == LATE),
                 work,
             )
             for k in range(n_src):
@@ -504,10 +509,18 @@
                 def _():
                     part_refs[k][...] = acc[...].astype(BF)
 
-        if n_each == 1:
+        if mode == EARLY:
+
+            @pl.when(short)
+            def _():
+                part_refs[0][...] = jnp.zeros((UNIQ, D), BF)
+                for load in loads.values():
+                    load.wait()
+
+        if go is None:
             work_on()
         else:
-            pl.when((turn == 0) | long)(work_on)
+            pl.when(go)(work_on)
         return carry
 
     if steps == 1:
@@ -515,32 +528,36 @@
     else:
         lax.fori_loop(0, steps, step, 0)
     for d in range(n_src):
-        base, lens = place_of(d)
-        for half in range(2):
-            out_copy(d * n_each, base, 0, half).wait()
-        if n_each == 2:
-            short = (lens[0] <= 128) & (lens[1] <= 128)
+        base, _, short = source(d)
+
+        def sent(t):
+            for half in range(2):
+                out_copy(t, base, 0, half).wait()
+
+        if mode == EARLY:
+            pl.when(jnp.logical_not(short))(functools.partial(sent, 0))
+        else:
+            sent(d * turns)
 
             @pl.when(short)
             def _():
                 for k in range(2):
                     blank_copy(d, base, k).wait()
 
-            @pl.when(jnp.logical_not(short))
-            def _():
-                for half in range(2):
-                    out_copy(d * 2 + 1, base, 0, half).wait()
+            if mode == BOTH:
+                pl.when(jnp.logical_not(short))(functools.partial(sent, d * turns + 1))
 
 
 def layer(plan, info, msgs, rows, cot, weights, prior):
-    deltas, each = plan
+    deltas, mode = plan
     n_src = len(deltas)
+    steps = n_src * (2 if mode == BOTH else 1)
     vmem = pl.BlockSpec(memory_space=pltpu.VMEM)
     hbm = pl.BlockSpec(memory_space=pltpu.HBM)
     args = [info, *msgs, *rows, cot, *weights]
-    in_specs = [pl.BlockSpec(memory_space=pltpu.SMEM)] + [vmem] * (2 * n_src + 1)
     keep = [] if prior is not None else [weights[0], weights[4]]
     spec = vmem if prior is not None else hbm
+    in_specs = [pl.BlockSpec(memory_space=pltpu.SMEM)] + [vmem] * (2 * n_src + 1)
     in_specs += [spec, vmem, vmem, vmem, spec, vmem]
     alias = {}
     if prior is not None:
@@ -557,10 +574,10 @@
             pltpu.VMEM((UNIQ, D), BF),
             pltpu.VMEM((8, MAXLEN), I32),
             pltpu.VMEM((UNIQ, D), F32),
-            pltpu.VMEM((n_src * len(each), MAXLEN, D), BF),
+            pltpu.VMEM((steps, MAXLEN, D), BF),
             pltpu.VMEM((128, D), BF),
             dma((9,)),
-            dma((n_src * len(each), 2)),
+            dma((steps, 2)),
             dma((n_src, 2)),
             pltpu.VMEM((16, MAXLEN, 128), BF),
             pltpu.VMEM((16, MAXLEN, 128), BF),
@@ -646,28 +663,35 @@
     )(asked)
 
 
-def scatter_kernel(line_ref, landed_ref, out_ref, whole_ref):
-    size = out_ref.shape[0]
-
-    @pl.when(pl.program_id(0) == 0)
-    def _():
-        whole_ref[...] = from_halves(landed_ref[...].astype(F32)).astype(BF)
-
-    row = iota((size, 4 * DEVICES), 0) + pl.program_id(0) * size
-    out_ref[...] = nn(onehot(row == line_ref[...]), whole_ref[...])
+def scatter_kernel(line_ref, landed_ref, out_hbm, whole_ref, rows_ref, sems):
+    whole_ref[...] = from_halves(landed_ref[...].astype(F32)).astype(BF)
+    size = 256
+    moves = []
+    for c in range(ROWS_DEV // size):
+        row = iota((size, 4 * DEVICES), 0) + c * size
+        rows_ref[pl.ds(c * size, size), :] = nn(onehot(row == line_ref[...]), whole_ref[...])
+        for k in range(2):
+            part = pl.ds(c * size + k * 128, 128)
+            move = pltpu.make_async_copy(rows_ref.at[part], out_hbm.at[part], sems.at[2 * c + k])
+            move.start()
+            moves.append(move)
+    for move in moves:
+        move.wait()
 
 
 def scatter(line, landed):
-    size = 256
-    whole = lambda a: pl.BlockSpec(a.shape, lambda i: (0, 0), pipeline_mode=pl.Buffered(1))
+    vmem = pl.BlockSpec(memory_space=pltpu.VMEM)
     return pl.pallas_call(
         scatter_kernel,
-        grid=(ROWS_DEV // size,),
-        in_specs=[whole(line), whole(landed)],
-        out_specs=pl.BlockSpec((size, D), lambda i: (i, 0)),
+        in_specs=[vmem, vmem],
+        out_specs=pl.BlockSpec(memory_space=pltpu.HBM),
         out_shape=jax.ShapeDtypeStruct((ROWS_DEV, D), F32),
-        scratch_shapes=[pltpu.VMEM((4 * DEVICES, D), BF)],
-        compiler_params=params(dimension_semantics=("arbitrary",)),
+        scratch_shapes=[
+            pltpu.VMEM((4 * DEVICES, D), BF),
+            pltpu.VMEM((ROWS_DEV, D), F32),
+            pltpu.SemaphoreType.DMA((8,)),
+        ],
+        compiler_params=params(),
         name="scatter",
     )(line, landed)
 
@@ -681,7 +705,7 @@
     return got.reshape(x.shape)
 
 
-PLANS = (((0,), (0,)), ((1,), (0, 1)), ((3, 2), (0, 1)), ((0,), (1,)))
+PLANS = (((0,), EARLY), ((1,), BOTH), ((3, 2), BOTH), ((0,), LATE))
 
 
 def program(

time: 115 us -> 114 us (level)
  Pallas kernels: 46.9 us -> 40.9 us
  waiting for transfers between devices: 19.8 us -> 25.5 us
    pallas_call x4, Pallas kernels: 33 us -> 27.9 us  [layer(): pl.pallas_call(functools.partial(layer_kernel, plan, prior is not None),...]
    ppermute x3, waiting for transfers between devices: 0.01 us -> 4.4 us  [program(): rows.append(lax.ppermute(own, 'seq', ring(d)))]
    ppermute x3, waiting for transfers between devices: 2.18 us -> 3.54 us  [program(): sums.append(part if d == 0 else lax.ppermute(part, 'seq', ring(-d)))]
  transfers between devices with their start and end apart: 11 -> 11, of which waited for: 3 -> 4; matrix products, arithmetic and copies ran while one was open for 0% -> 0% of each run, Pallas kernels for 20% -> 16%
where the time goes in v5:
time: 114 us
  Pallas kernels  40.9 us (36%)
  waiting for transfers between devices  25.5 us (22%)
  starting transfers between devices  25.4 us (22%)
  blocking collectives  21 us (18%)
    pallas_call x4, Pallas kernels, layer(): pl.pallas_call(functools.partial(layer_kernel, plan, prior is not None),...  27.9 us
    all_to_all x1, blocking collectives, exchange(): lax.all_to_all(x.reshape(shape), ('emb', 'seq'), split_axis=0, concat_axi...  21 us
    all_to_all x2, waiting for transfers between devices, exchange(): lax.all_to_all(x.reshape(shape), ('emb', 'seq'), split_axis=0, concat_axi...  17.6 us
    all_to_all x2, starting transfers between devices, exchange(): lax.all_to_all(x.reshape(shape), ('emb', 'seq'), split_axis=0, concat_axi...  14 us
    ppermute x3, starting transfers between devices, program(): lax.ppermute(sent[d], 'seq', ring(d))  5.01 us
    ppermute x3, waiting for transfers between devices, program(): rows.append(lax.ppermute(own, 'seq', ring(d)))  4.4 us
    pallas_call x1, Pallas kernels, tables(): pl.pallas_call(tables_kernel, out_shape=[jax.ShapeDtypeStruct((HEADS, MAX...  3.6 us
    ppermute x3, starting transfers between devices, program(): sums.append(part if d == 0 else lax.ppermute(part, 'seq', ring(-d)))  3.57 us
  transfers between devices with their start and end apart: 11, of which 4 were waited for; matrix products, arithmetic and copies ran while one was open for 0% of the time, Pallas kernels for 16%

profile of v5, /device:TPU:1, one launch (start us, length us, event | category | flops | bytes accessed | tf_op | source)
XLA Modules:
  0.0 114.1 jit_solution(7592736571074856413)
XLA Ops:
  0.6 0.0 copy-start.4
  0.6 1.5 %pack.1 = (s32[128,4]{1,0:T(8,128)S(1)}, s32[1,256]{1,0:T(1,128)S(1)}, s32[2,384]{1,0:T(2,128)S(1)}, s32[2,384]{1,0:T(2,128)S(1)}, s32[2,384]{1,0:T(2,128)S(1)}, /*index=5*/s32[2,384]{1,0:T(2,128)S(1)}) custom-call(s32[8]{0:T(128)} %assign_hbm.1, s32[8]{0:T(128)} %len_hbm.1, s32[1]{0:T(128)} %bitcast.seq_ref, s32[1,256]{1,0:T(1,128)} %bitcast.30, ...), custom_call_target="tpu_custom_call" | custom-call | tf_op jit(solution)/shard_map/pack/pallas_call | solution.py:107
  2.2 21.0 %all_to_all.15 = s32[128,1,4]{2,1,0:T(1,128)S(1)} all-to-all(s32[128,1,4]{2,1,0:T(1,128)S(1)} %bitcast.21), channel_id=1, replica_groups=mesh['emb'=32,'seq'=4] {'emb','seq'}, dimensions={0} | all-to-all | bytes 4096 | tf_op jit(solution)/shard_map/all_to_all | solution.py:704
  23.2 2.7 %answer.1 = bf16[1024,256]{1,0:T(8,128)(2,1)} custom-call(s32[128,4]{1,0:T(8,128)S(1)} %bitcast.15, bf16[1024,512]{1,0:T(8,128)(2,1)} %table_hbm.1), custom_call_target="tpu_custom_call" | custom-call | tf_op jit(solution)/shard_map/answer/pallas_call | solution.py:234
  25.9 0.0 copy-start
  25.9 0.0 copy-start.1
  25.9 0.0 copy-start.2
  25.9 0.0 copy-start.3
  25.9 4.3 %all-to-all-start.1 = ((bf16[128,8,256]{2,1,0:T(8,128)(2,1)}), bf16[128,8,256]{2,1,0:T(8,128)(2,1)S(1)}, u32[]{:S(2)}, u32[]{:S(2)}) async-start(bf16[128,8,256]{2,1,0:T(8,128)(2,1)} %bitcast.5), calls=%async_computation.1 | async-start | bytes 1048576 | tf_op jit(solution)/shard_map/all_to_all | solution.py:704
  30.2 1.4 %collective-permute-start = (s32[2,384]{1,0:T(2,128)S(1)}, s32[2,384]{1,0:T(2,128)S(1)}, u32[]{:S(2)}, u32[]{:S(2)}) collective-permute-start(s32[2,384]{1,0:T(2,128)S(1)} %get-tuple-element.27), channel_id=1, source_target_pairs={{0,1},{1,2},{2,3},{3,0},{4,5},{5,6},{6,7},{7,4},{8,9},{9,10},{10,1... | collective-permute-start | bytes 9224 | tf_op jit(solution)/shard_map/ppermute | solution.py:728
  31.6 2.4 %collective-permute-start.1 = (s32[2,384]{1,0:T(2,128)S(1)}, s32[2,384]{1,0:T(2,128)S(1)}, u32[]{:S(2)}, u32[]{:S(2)}) collective-permute-start(s32[2,384]{1,0:T(2,128)S(1)} %get-tuple-element.28), channel_id=1, source_target_pairs={{0,2},{1,3},{2,0},{3,1},{4,6},{5,7},{6,4},{7,5},{8,10},{9,11},{10,... | collective-permute-start | bytes 9224 | tf_op jit(solution)/shard_map/ppermute | solution.py:728
  34.1 1.2 %collective-permute-start.2 = (s32[2,384]{1,0:T(2,128)S(1)}, s32[2,384]{1,0:T(2,128)S(1)}, u32[]{:S(2)}, u32[]{:S(2)}) collective-permute-start(s32[2,384]{1,0:T(2,128)S(1)} %get-tuple-element.29), channel_id=1, source_target_pairs={{0,3},{1,0},{2,1},{3,2},{4,7},{5,4},{6,5},{7,6},{8,11},{9,8},{10,9... | collective-permute-start | bytes 9224 | tf_op jit(solution)/shard_map/ppermute | solution.py:728
  35.2 0.0 copy-done.4
  35.2 0.2 rev.3.flipped_ref
  35.4 3.6 %tables.1 = (f32[4,256,128]{2,1,0:T(8,128)S(1)}, s32[256,128]{1,0:T(8,128)S(1)}, bf16[16,512,128]{2,1,0:T(8,128)(2,1)}, bf16[4,512,128]{2,1,0:T(8,128)(2,1)}) custom-call(f32[4,256]{1,0:T(4,128)S(1)} %rev.3.flipped_ref, s32[1,256]{1,0:T(1,128)S(1)} %get-tuple-element.31.pos_ref, bf16[512,2048]{1,0:T(8,128)(2,1)} %win_hbm.1, bf16[512,512]{1,0:T(8,128)(2,1)} %wout_hbm.1), custom_call_target="tpu_custom_call" | custom-call | tf_op jit(solution)/shard_map/tables/pallas_call | solution.py:162
  39.0 0.0 collective-permute-done.refs_1_
  39.0 0.0 collective-permute-done.1.refs_2_
  39.0 0.0 collective-permute-done.2.refs_3_.refs_1_
  39.1 1.3 %scalars.1.refs_0_ = s32[16]{0:T(128)S(1)} custom-call(s32[1]{0:T(128)} %bitcast.seq_ref, s32[2,384]{1,0:T(2,128)S(1)} %get-tuple-element.26.refs_0_.refs_1_, s32[2,384]{1,0:T(2,128)S(1)} %collective-permute-done.refs_1_, s32[2,384]{1,0:T(2,128)S(1)} %collective-permute-done.1.refs_2_, s32[2,384]{1,0:T(2,128)S(1)} %collective-permute-done.2.refs_3_.refs_1_), custom_call_target="tpu_custom_call" | custom-call | tf_op jit(solution)/shard_map/scalars/pallas_call | solution.py:613
  40.4 3.9 %all-to-all-done.1 = bf16[128,8,256]{2,1,0:T(8,128)(2,1)S(1)} async-done(((bf16[128,8,256]{2,1,0:T(8,128)(2,1)}), bf16[128,8,256]{2,1,0:T(8,128)(2,1)S(1)}, u32[]{:S(2)}, u32[]{:S(2)}) %all-to-all-start.1) | async-done | bytes 524320 | tf_op jit(solution)/shard_map/all_to_all | solution.py:704
  44.3 0.5 compact.1.refs_2_
  44.8 0.4 collective-permute-start.5
  45.2 1.8 %collective-permute-start.4 = (bf16[256,512]{1,0:T(8,128)(2,1)S(1)}, bf16[256,512]{1,0:T(8,128)(2,1)S(1)}, u32[]{:S(2)}, u32[]{:S(2)}) collective-permute-start(bf16[256,512]{1,0:T(8,128)(2,1)S(1)} %compact.1.refs_2_), channel_id=1, source_target_pairs={{0,2},{1,3},{2,0},{3,1},{4,6},{5,7},{6,4},{7,5},{8,10},{9,11},{10,... | collective-permute-start | bytes 786440 | tf_op jit(solution)/shard_map/ppermute | solution.py:738
  47.0 0.6 collective-permute-start.3
  47.7 0.0 copy-done
  47.7 0.0 copy-done.1
  47.7 0.0 copy-done.2
  47.7 0.0 copy-done.3
  47.7 2.3 %layer.4 = (bf16[8,256,512]{2,1,0:T(8,128)(2,1)}, bf16[256,512]{1,0:T(8,128)(2,1)S(1)}, bf16[16,512,128]{2,1,0:T(8,128)(2,1)S(1)}, bf16[4,512,128]{2,1,0:T(8,128)(2,1)S(1)}) custom-call(s32[16]{0:T(128)S(1)} %scalars.1.refs_0_, s32[2,384]{1,0:T(2,128)S(1)} %get-tuple-element.26.refs_0_.refs_1_, bf16[256,512]{1,0:T(8,128)(2,1)S(1)} %compact.1.refs_2_, ...), custom_call_target="tpu_custom_call" | custom-call | tf_op jit(solution)/shard_map/layer/pallas_call | solution.py:569
  50.0 4.4 %collective-permute-done.5.refs_2_ = bf16[256,512]{1,0:T(8,128)(2,1)S(1)} collective-permute-done((bf16[256,512]{1,0:T(8,128)(2,1)S(1)}, bf16[256,512]{1,0:T(8,128)(2,1)S(1)}, u32[]{:S(2)}, u32[]{:S(2)}) %collective-permute-start.5) | collective-permute-done | bytes 262176 | tf_op jit(solution)/shard_map/ppermute | solution.py:738
  54.4 5.7 %layer.5 = (bf16[8,256,512]{2,1,0:T(8,128)(2,1)}, bf16[256,512]{1,0:T(8,128)(2,1)S(1)}) custom-call(s32[16]{0:T(128)S(1)} %scalars.1.refs_0_, s32[2,384]{1,0:T(2,128)S(1)} %collective-permute-done.refs_1_, bf16[256,512]{1,0:T(8,128)(2,1)S(1)} %collective-permute-done.5.refs_2_, bf16[8,256,512]{2,1,0:T(8,128)(2,1)S(1)} %copy-done, ...), custom_call_target="tpu_custom_call", output_to_operand_aliasing={{0}: (10, {})} | custom-call | tf_op jit(solution)/shard_map/layer/pallas_call | solution.py:569
  60.1 0.0 collective-permute-done.4.refs_4_
  60.1 0.0 collective-permute-done.3.refs_3_
  60.1 14.7 %layer.6 = (bf16[8,256,512]{2,1,0:T(8,128)(2,1)}, bf16[256,512]{1,0:T(8,128)(2,1)S(1)}, bf16[256,512]{1,0:T(8,128)(2,1)S(1)}) custom-call(s32[16]{0:T(128)S(1)} %scalars.1.refs_0_, s32[2,384]{1,0:T(2,128)S(1)} %collective-permute-done.2.refs_3_.refs_1_, s32[2,384]{1,0:T(2,128)S(1)} %collective-permute-done.1.refs_2_, ...), custom_call_target="tpu_custom_call", output_to_operand_aliasing={{0}: (12, {})} | custom-call | tf_op jit(solution)/shard_map/layer/pallas_call | solution.py:569
  74.8 0.1 collective-permute-start.7
  74.9 3.5 %collective-permute-start.8 = (bf16[256,512]{1,0:T(8,128)(2,1)S(1)}, bf16[256,512]{1,0:T(8,128)(2,1)S(1)}, u32[]{:S(2)}, u32[]{:S(2)}) collective-permute-start(bf16[256,512]{1,0:T(8,128)(2,1)S(1)} %get-tuple-element.46), channel_id=1, source_target_pairs={{0,2},{1,3},{2,0},{3,1},{4,6},{5,7},{6,4},{7,5},{8,10},{9,11},{10,... | collective-permute-start | bytes 786440 | tf_op jit(solution)/shard_map/ppermute | solution.py:762
  78.4 0.0 collective-permute-start.6
  78.4 5.2 %layer.7 = (bf16[8,256,512]{2,1,0:T(8,128)(2,1)}, bf16[256,512]{1,0:T(8,128)(2,1)S(1)}) custom-call(s32[16]{0:T(128)S(1)} %scalars.1.refs_0_, s32[2,384]{1,0:T(2,128)S(1)} %get-tuple-element.26.refs_0_.refs_1_, bf16[256,512]{1,0:T(8,128)(2,1)S(1)} %compact.1.refs_2_, bf16[8,256,512]{2,1,0:T(8,128)(2,1)S(1)} %copy-done, ...), custom_call_target="tpu_custom_call", output_to_operand_aliasing={{0}: (10, {})} | custom-call | tf_op jit(solution)/shard_map/layer/pallas_call | solution.py:569
  83.6 0.0 collective-permute-done.7.refs_2_
  83.7 3.5 %collective-permute-done.8.refs_3_ = bf16[256,512]{1,0:T(8,128)(2,1)S(1)} collective-permute-done((bf16[256,512]{1,0:T(8,128)(2,1)S(1)}, bf16[256,512]{1,0:T(8,128)(2,1)S(1)}, u32[]{:S(2)}, u32[]{:S(2)}) %collective-permute-start.8) | collective-permute-done | bytes 262176 | tf_op jit(solution)/shard_map/ppermute | solution.py:762
  87.2 0.0 collective-permute-done.6.refs_1_
  87.2 1.4 %expand.1 = bf16[1024,256]{1,0:T(8,128)(2,1)} custom-call(s32[1,256]{1,0:T(1,128)S(1)} %get-tuple-element.31.pos_ref, bf16[256,512]{1,0:T(8,128)(2,1)S(1)} %get-tuple-element.43.refs_0_, bf16[256,512]{1,0:T(8,128)(2,1)S(1)} %collective-permute-done.6.refs_1_, bf16[256,512]{1,0:T(8,128)(2,1)S(1)} %collective-permute-done.7.refs_2_, ...), custom_call_target="tpu_custom_call" | custom-call | tf_op jit(solution)/shard_map/expand/pallas_call | solution.py:637
  88.6 9.7 %all-to-all-start.2 = ((bf16[128,8,256]{2,1,0:T(8,128)(2,1)}), bf16[128,8,256]{2,1,0:T(8,128)(2,1)S(1)}, u32[]{:S(2)}, u32[]{:S(2)}) async-start(bf16[128,8,256]{2,1,0:T(8,128)(2,1)} %bitcast.10), calls=%async_computation.2 | async-start | bytes 1048576 | tf_op jit(solution)/shard_map/all_to_all | solution.py:704
  98.3 0.2 asked_line.1.line_ref
  98.5 13.7 %all-to-all-done.2 = bf16[128,8,256]{2,1,0:T(8,128)(2,1)S(1)} async-done(((bf16[128,8,256]{2,1,0:T(8,128)(2,1)}), bf16[128,8,256]{2,1,0:T(8,128)(2,1)S(1)}, u32[]{:S(2)}, u32[]{:S(2)}) %all-to-all-start.2) | async-done | bytes 524320 | tf_op jit(solution)/shard_map/all_to_all | solution.py:704
  112.2 1.7 %scatter.1 = f32[1024,512]{1,0:T(8,128)} custom-call(s32[1,512]{1,0:T(1,128)S(1)} %asked_line.1.line_ref, bf16[1024,256]{1,0:T(8,128)(2,1)S(1)} %bitcast.14), custom_call_target="tpu_custom_call" | custom-call | tf_op jit(solution)/shard_map/scatter/pallas_call | solution.py:684
Async XLA Ops:
  0.6 34.6 %copy-start.4 = (f32[4,256]{1,0:T(4,128)S(1)}, f32[4,256]{1,0:T(4,128)}, u32[]{:S(2)}) copy-start(f32[4,256]{1,0:T(4,128)} %param.22) | copy-start | bytes 12292
  25.9 21.8 %copy-start = (bf16[8,256,512]{2,1,0:T(8,128)(2,1)S(1)}, bf16[8,256,512]{2,1,0:T(8,128)(2,1)}, u32[]{:S(2)}) copy-start(bf16[8,256,512]{2,1,0:T(8,128)(2,1)} %refs_3_.5) | copy-start | bytes 6291460
  25.9 21.8 %copy-start.1 = (f32[2048]{0:T(1024)S(1)}, f32[2048]{0:T(1024)}, u32[]{:S(2)}) copy-start(f32[2048]{0:T(1024)} %param.18) | copy-start | bytes 24580
  25.9 21.7 %copy-start.2 = (f32[512]{0:T(512)S(1)}, f32[512]{0:T(512)}, u32[]{:S(2)}) copy-start(f32[512]{0:T(512)} %param.19) | copy-start | bytes 6148
  25.9 21.7 %copy-start.3 = (f32[512]{0:T(512)S(1)}, f32[512]{0:T(512)}, u32[]{:S(2)}) copy-start(f32[512]{0:T(512)} %param.20) | copy-start | bytes 6148
  25.9 18.4 %all-to-all-start.1 = ((bf16[128,8,256]{2,1,0:T(8,128)(2,1)}), bf16[128,8,256]{2,1,0:T(8,128)(2,1)S(1)}, u32[]{:S(2)}, u32[]{:S(2)}) async-start(bf16[128,8,256]{2,1,0:T(8,128)(2,1)} %bitcast.5), calls=%async_computation.1 | async-start | bytes 1048576 | tf_op jit(solution)/shard_map/all_to_all | solution.py:704
  30.2 8.8 %collective-permute-start = (s32[2,384]{1,0:T(2,128)S(1)}, s32[2,384]{1,0:T(2,128)S(1)}, u32[]{:S(2)}, u32[]{:S(2)}) collective-permute-start(s32[2,384]{1,0:T(2,128)S(1)} %get-tuple-element.27), channel_id=1, source_target_pairs={{0,1},{1,2},{2,3},{3,0},{4,5},{5,6},{6,7},{7,4},{8,9},{9,10},{10,1... | collective-permute-start | bytes 9224 | tf_op jit(solution)/shard_map/ppermute | solution.py:728
  31.6 7.4 %collective-permute-start.1 = (s32[2,384]{1,0:T(2,128)S(1)}, s32[2,384]{1,0:T(2,128)S(1)}, u32[]{:S(2)}, u32[]{:S(2)}) collective-permute-start(s32[2,384]{1,0:T(2,128)S(1)} %get-tuple-element.28), channel_id=1, source_target_pairs={{0,2},{1,3},{2,0},{3,1},{4,6},{5,7},{6,4},{7,5},{8,10},{9,11},{10,... | collective-permute-start | bytes 9224 | tf_op jit(solution)/shard_map/ppermute | solution.py:728
  34.1 5.0 %collective-permute-start.2 = (s32[2,384]{1,0:T(2,128)S(1)}, s32[2,384]{1,0:T(2,128)S(1)}, u32[]{:S(2)}, u32[]{:S(2)}) collective-permute-start(s32[2,384]{1,0:T(2,128)S(1)} %get-tuple-element.29), channel_id=1, source_target_pairs={{0,3},{1,0},{2,1},{3,2},{4,7},{5,4},{6,5},{7,6},{8,11},{9,8},{10,9... | collective-permute-start | bytes 9224 | tf_op jit(solution)/shard_map/ppermute | solution.py:728
  44.8 9.6 %collective-permute-start.5 = (bf16[256,512]{1,0:T(8,128)(2,1)S(1)}, bf16[256,512]{1,0:T(8,128)(2,1)S(1)}, u32[]{:S(2)}, u32[]{:S(2)}) collective-permute-start(bf16[256,512]{1,0:T(8,128)(2,1)S(1)} %compact.1.refs_2_), channel_id=1, source_target_pairs={{0,1},{1,2},{2,3},{3,0},{4,5},{5,6},{6,7},{7,4},{8,9},{9,10},{10,1... | collective-permute-start | bytes 786440 | tf_op jit(solution)/shard_map/ppermute | solution.py:738
  45.2 14.9 %collective-permute-start.4 = (bf16[256,512]{1,0:T(8,128)(2,1)S(1)}, bf16[256,512]{1,0:T(8,128)(2,1)S(1)}, u32[]{:S(2)}, u32[]{:S(2)}) collective-permute-start(bf16[256,512]{1,0:T(8,128)(2,1)S(1)} %compact.1.refs_2_), channel_id=1, source_target_pairs={{0,2},{1,3},{2,0},{3,1},{4,6},{5,7},{6,4},{7,5},{8,10},{9,11},{10,... | collective-permute-start | bytes 786440 | tf_op jit(solution)/shard_map/ppermute | solution.py:738
  47.0 13.1 %collective-permute-start.3 = (bf16[256,512]{1,0:T(8,128)(2,1)S(1)}, bf16[256,512]{1,0:T(8,128)(2,1)S(1)}, u32[]{:S(2)}, u32[]{:S(2)}) collective-permute-start(bf16[256,512]{1,0:T(8,128)(2,1)S(1)} %compact.1.refs_2_), channel_id=1, source_target_pairs={{0,3},{1,0},{2,1},{3,2},{4,7},{5,4},{6,5},{7,6},{8,11},{9,8},{10,9... | collective-permute-start | bytes 786440 | tf_op jit(solution)/shard_map/ppermute | solution.py:738
  74.8 8.8 %collective-permute-start.7 = (bf16[256,512]{1,0:T(8,128)(2,1)S(1)}, bf16[256,512]{1,0:T(8,128)(2,1)S(1)}, u32[]{:S(2)}, u32[]{:S(2)}) collective-permute-start(bf16[256,512]{1,0:T(8,128)(2,1)S(1)} %get-tuple-element.45), channel_id=1, source_target_pairs={{0,1},{1,2},{2,3},{3,0},{4,5},{5,6},{6,7},{7,4},{8,9},{9,10},{10,1... | collective-permute-start | bytes 786440 | tf_op jit(solution)/shard_map/ppermute | solution.py:762
  74.9 12.3 %collective-permute-start.8 = (bf16[256,512]{1,0:T(8,128)(2,1)S(1)}, bf16[256,512]{1,0:T(8,128)(2,1)S(1)}, u32[]{:S(2)}, u32[]{:S(2)}) collective-permute-start(bf16[256,512]{1,0:T(8,128)(2,1)S(1)} %get-tuple-element.46), channel_id=1, source_target_pairs={{0,2},{1,3},{2,0},{3,1},{4,6},{5,7},{6,4},{7,5},{8,10},{9,11},{10,... | collective-permute-start | bytes 786440 | tf_op jit(solution)/shard_map/ppermute | solution.py:762
  78.4 8.8 %collective-permute-start.6 = (bf16[256,512]{1,0:T(8,128)(2,1)S(1)}, bf16[256,512]{1,0:T(8,128)(2,1)S(1)}, u32[]{:S(2)}, u32[]{:S(2)}) collective-permute-start(bf16[256,512]{1,0:T(8,128)(2,1)S(1)} %get-tuple-element.44), channel_id=1, source_target_pairs={{0,3},{1,0},{2,1},{3,2},{4,7},{5,4},{6,5},{7,6},{8,11},{9,8},{10,9... | collective-permute-start | bytes 786440 | tf_op jit(solution)/shard_map/ppermute | solution.py:762
  88.6 23.6 %all-to-all-start.2 = ((bf16[128,8,256]{2,1,0:T(8,128)(2,1)}), bf16[128,8,256]{2,1,0:T(8,128)(2,1)S(1)}, u32[]{:S(2)}, u32[]{:S(2)}) async-start(bf16[128,8,256]{2,1,0:T(8,128)(2,1)} %bitcast.10), calls=%async_computation.2 | async-start | bytes 1048576 | tf_op jit(solution)/shard_map/all_to_all | solution.py:704

commit v6 on v5

--- a/solution.py
+++ b/solution.py
@@ -209,7 +209,7 @@
     return jnp.concatenate([low.reshape(flat), high.reshape(flat)], axis=1)
 
 
-def answer_kernel(asked_ref, table_hbm, out_ref, table_ref, pick_ref, sem):
+def answer_kernel(asked_ref, table_hbm, out_hbm, table_ref, pick_ref, out_ref, sem):
     loads = []
     for c in range(4):
         part = pl.ds(c * 256, 256)
@@ -225,20 +225,28 @@
     pick_ref[...] = onehot(iota((count, ROWS_DEV), 1) == col)
     for load in loads:
         load.wait()
+    moves = []
     for c in range(2):
         rows = nn(pick_ref[pl.ds(c * 256, 256), :], table_ref[...])
-        out_ref[pl.ds(c * 512, 512), :] = to_halves(rows).astype(BF)
+        part = pl.ds(c * 512, 512)
+        out_ref[part, :] = to_halves(rows).astype(BF)
+        moves.append(pltpu.make_async_copy(out_ref.at[part], out_hbm.at[part], sem.at[4 + c]))
+        moves[-1].start()
+    for move in moves:
+        move.wait()
 
 
 def answer_rows(asked, table):
     return pl.pallas_call(
         answer_kernel,
         in_specs=[pl.BlockSpec(memory_space=pltpu.VMEM), pl.BlockSpec(memory_space=pltpu.HBM)],
+        out_specs=pl.BlockSpec(memory_space=pltpu.HBM),
         out_shape=jax.ShapeDtypeStruct((8 * DEVICES, D // 2), BF),
         scratch_shapes=[
             pltpu.VMEM((ROWS_DEV, D), BF),
             pltpu.VMEM((4 * DEVICES, ROWS_DEV), BF),
-            pltpu.SemaphoreType.DMA((4,)),
+            pltpu.VMEM((8 * DEVICES, D // 2), BF),
+            pltpu.SemaphoreType.DMA((6,)),
         ],
         compiler_params=params(),
         name="answer",
@@ -621,22 +629,37 @@
 
 
 def expand_kernel(pos_ref, *refs):
-    out_ref = refs[-1]
+    out_hbm, out_ref, sems = refs[-3:]
     total = refs[0][...].astype(F32)
-    for r in refs[1:-1]:
+    for r in refs[1:-3]:
         total = total + r[...].astype(F32)
     total = total.astype(BF)
-    row = iota((8 * DEVICES, UNIQ), 0)
     pos = pos_ref[...]
-    upper = nn(onehot(row == pos), total[:, : D // 2])
-    lower = nn(onehot(row == pos + 4), total[:, D // 2 :])
-    out_ref[...] = (upper + lower).astype(BF)
+    size = 256
+    moves = []
+    for c in range(8 * DEVICES // size):
+        row = iota((size, UNIQ), 0) + c * size
+        upper = nn(onehot(row == pos), total[:, : D // 2])
+        lower = nn(onehot(row == pos + 4), total[:, D // 2 :])
+        part = pl.ds(c * size, size)
+        out_ref[part, :] = (upper + lower).astype(BF)
+        moves.append(pltpu.make_async_copy(out_ref.at[part], out_hbm.at[part], sems.at[c]))
+        moves[-1].start()
+    for move in moves:
+        move.wait()
 
 
 def expand(pos, parts):
+    vmem = pl.BlockSpec(memory_space=pltpu.VMEM)
     return pl.pallas_call(
         expand_kernel,
+        in_specs=[vmem] * (1 + len(parts)),
+        out_specs=pl.BlockSpec(memory_space=pltpu.HBM),
         out_shape=jax.ShapeDtypeStruct((8 * DEVICES, D // 2), BF),
+        scratch_shapes=[
+            pltpu.VMEM((8 * DEVICES, D // 2), BF),
+            pltpu.SemaphoreType.DMA((4,)),
+        ],
         compiler_params=params(),
         name="expand",
     )(pos, *parts)

time: 114 us -> 114 us (level)
  no operation moved by 1% of the time
where the time goes in v6:
time: 114 us
  Pallas kernels  40.7 us (36%)
  waiting for transfers between devices  25.5 us (22%)
  starting transfers between devices  25.4 us (22%)
  blocking collectives  21 us (18%)
    pallas_call x4, Pallas kernels, layer(): pl.pallas_call(functools.partial(layer_kernel, plan, prior is not None),...  27.9 us
    all_to_all x1, blocking collectives, exchange(): lax.all_to_all(x.reshape(shape), ('emb', 'seq'), split_axis=0, concat_axi...  21 us
    all_to_all x2, waiting for transfers between devices, exchange(): lax.all_to_all(x.reshape(shape), ('emb', 'seq'), split_axis=0, concat_axi...  17.6 us
    all_to_all x2, starting transfers between devices, exchange(): lax.all_to_all(x.reshape(shape), ('emb', 'seq'), split_axis=0, concat_axi...  14 us
    ppermute x3, starting transfers between devices, program(): lax.ppermute(sent[d], 'seq', ring(d))  5.01 us
    ppermute x3, waiting for transfers between devices, program(): rows.append(lax.ppermute(own, 'seq', ring(d)))  4.4 us
    pallas_call x1, Pallas kernels, tables(): pl.pallas_call(tables_kernel, out_shape=[jax.ShapeDtypeStruct((HEADS, MAX...  3.6 us
    ppermute x3, starting transfers between devices, program(): sums.append(part if d == 0 else lax.ppermute(part, 'seq', ring(-d)))  3.57 us
  transfers between devices with their start and end apart: 11, of which 4 were waited for; matrix products, arithmetic and copies ran while one was open for 0% of the time, Pallas kernels for 16%

profile of v6, /device:TPU:1, one launch (start us, length us, event | category | flops | bytes accessed | tf_op | source)
XLA Modules:
  0.0 113.9 jit_solution(12114192465649424053)
XLA Ops:
  0.6 0.0 copy-start.4
  0.6 1.5 %pack.1 = (s32[128,4]{1,0:T(8,128)S(1)}, s32[1,256]{1,0:T(1,128)S(1)}, s32[2,384]{1,0:T(2,128)S(1)}, s32[2,384]{1,0:T(2,128)S(1)}, s32[2,384]{1,0:T(2,128)S(1)}, /*index=5*/s32[2,384]{1,0:T(2,128)S(1)}) custom-call(s32[8]{0:T(128)} %assign_hbm.1, s32[8]{0:T(128)} %len_hbm.1, s32[1]{0:T(128)} %bitcast.seq_ref, s32[1,256]{1,0:T(1,128)} %bitcast.30, ...), custom_call_target="tpu_custom_call" | custom-call | tf_op jit(solution)/shard_map/pack/pallas_call | solution.py:107
  2.2 21.0 %all_to_all.15 = s32[128,1,4]{2,1,0:T(1,128)S(1)} all-to-all(s32[128,1,4]{2,1,0:T(1,128)S(1)} %bitcast.21), channel_id=1, replica_groups=mesh['emb'=32,'seq'=4] {'emb','seq'}, dimensions={0} | all-to-all | bytes 4096 | tf_op jit(solution)/shard_map/all_to_all | solution.py:727
  23.2 2.7 %answer.1 = bf16[1024,256]{1,0:T(8,128)(2,1)} custom-call(s32[128,4]{1,0:T(8,128)S(1)} %bitcast.15, bf16[1024,512]{1,0:T(8,128)(2,1)} %table_hbm.1), custom_call_target="tpu_custom_call" | custom-call | tf_op jit(solution)/shard_map/answer/pallas_call | solution.py:240
  25.8 0.0 copy-start
  25.8 0.0 copy-start.1
  25.8 0.0 copy-start.2
  25.9 0.0 copy-start.3
  25.9 4.3 %all-to-all-start.1 = ((bf16[128,8,256]{2,1,0:T(8,128)(2,1)}), bf16[128,8,256]{2,1,0:T(8,128)(2,1)S(1)}, u32[]{:S(2)}, u32[]{:S(2)}) async-start(bf16[128,8,256]{2,1,0:T(8,128)(2,1)} %bitcast.5), calls=%async_computation.1 | async-start | bytes 1048576 | tf_op jit(solution)/shard_map/all_to_all | solution.py:727
  30.1 1.4 %collective-permute-start = (s32[2,384]{1,0:T(2,128)S(1)}, s32[2,384]{1,0:T(2,128)S(1)}, u32[]{:S(2)}, u32[]{:S(2)}) collective-permute-start(s32[2,384]{1,0:T(2,128)S(1)} %get-tuple-element.27), channel_id=1, source_target_pairs={{0,1},{1,2},{2,3},{3,0},{4,5},{5,6},{6,7},{7,4},{8,9},{9,10},{10,1... | collective-permute-start | bytes 9224 | tf_op jit(solution)/shard_map/ppermute | solution.py:751
  31.6 2.4 %collective-permute-start.1 = (s32[2,384]{1,0:T(2,128)S(1)}, s32[2,384]{1,0:T(2,128)S(1)}, u32[]{:S(2)}, u32[]{:S(2)}) collective-permute-start(s32[2,384]{1,0:T(2,128)S(1)} %get-tuple-element.28), channel_id=1, source_target_pairs={{0,2},{1,3},{2,0},{3,1},{4,6},{5,7},{6,4},{7,5},{8,10},{9,11},{10,... | collective-permute-start | bytes 9224 | tf_op jit(solution)/shard_map/ppermute | solution.py:751
  34.0 1.2 %collective-permute-start.2 = (s32[2,384]{1,0:T(2,128)S(1)}, s32[2,384]{1,0:T(2,128)S(1)}, u32[]{:S(2)}, u32[]{:S(2)}) collective-permute-start(s32[2,384]{1,0:T(2,128)S(1)} %get-tuple-element.29), channel_id=1, source_target_pairs={{0,3},{1,0},{2,1},{3,2},{4,7},{5,4},{6,5},{7,6},{8,11},{9,8},{10,9... | collective-permute-start | bytes 9224 | tf_op jit(solution)/shard_map/ppermute | solution.py:751
  35.2 0.0 copy-done.4
  35.2 0.2 rev.3.flipped_ref
  35.3 3.6 %tables.1 = (f32[4,256,128]{2,1,0:T(8,128)S(1)}, s32[256,128]{1,0:T(8,128)S(1)}, bf16[16,512,128]{2,1,0:T(8,128)(2,1)}, bf16[4,512,128]{2,1,0:T(8,128)(2,1)}) custom-call(f32[4,256]{1,0:T(4,128)S(1)} %rev.3.flipped_ref, s32[1,256]{1,0:T(1,128)S(1)} %get-tuple-element.31.pos_ref, bf16[512,2048]{1,0:T(8,128)(2,1)} %win_hbm.1, bf16[512,512]{1,0:T(8,128)(2,1)} %wout_hbm.1), custom_call_target="tpu_custom_call" | custom-call | tf_op jit(solution)/shard_map/tables/pallas_call | solution.py:162
  39.0 0.0 collective-permute-done.refs_1_
  39.0 0.0 collective-permute-done.1.refs_2_
  39.0 0.0 collective-permute-done.2.refs_3_.refs_1_
  39.0 1.3 %scalars.1.refs_0_ = s32[16]{0:T(128)S(1)} custom-call(s32[1]{0:T(128)} %bitcast.seq_ref, s32[2,384]{1,0:T(2,128)S(1)} %get-tuple-element.26.refs_0_.refs_1_, s32[2,384]{1,0:T(2,128)S(1)} %collective-permute-done.refs_1_, s32[2,384]{1,0:T(2,128)S(1)} %collective-permute-done.1.refs_2_, s32[2,384]{1,0:T(2,128)S(1)} %collective-permute-done.2.refs_3_.refs_1_), custom_call_target="tpu_custom_call" | custom-call | tf_op jit(solution)/shard_map/scalars/pallas_call | solution.py:621
  40.3 3.9 %all-to-all-done.1 = bf16[128,8,256]{2,1,0:T(8,128)(2,1)S(1)} async-done(((bf16[128,8,256]{2,1,0:T(8,128)(2,1)}), bf16[128,8,256]{2,1,0:T(8,128)(2,1)S(1)}, u32[]{:S(2)}, u32[]{:S(2)}) %all-to-all-start.1) | async-done | bytes 524320 | tf_op jit(solution)/shard_map/all_to_all | solution.py:727
  44.2 0.5 compact.1.refs_2_
  44.7 0.4 collective-permute-start.5
  45.1 1.8 %collective-permute-start.4 = (bf16[256,512]{1,0:T(8,128)(2,1)S(1)}, bf16[256,512]{1,0:T(8,128)(2,1)S(1)}, u32[]{:S(2)}, u32[]{:S(2)}) collective-permute-start(bf16[256,512]{1,0:T(8,128)(2,1)S(1)} %compact.1.refs_2_), channel_id=1, source_target_pairs={{0,2},{1,3},{2,0},{3,1},{4,6},{5,7},{6,4},{7,5},{8,10},{9,11},{10,... | collective-permute-start | bytes 786440 | tf_op jit(solution)/shard_map/ppermute | solution.py:761
  46.9 0.6 collective-permute-start.3
  47.6 0.0 copy-done
  47.6 0.0 copy-done.1
  47.6 0.0 copy-done.2
  47.6 0.0 copy-done.3
  47.6 2.3 %layer.4 = (bf16[8,256,512]{2,1,0:T(8,128)(2,1)}, bf16[256,512]{1,0:T(8,128)(2,1)S(1)}, bf16[16,512,128]{2,1,0:T(8,128)(2,1)S(1)}, bf16[4,512,128]{2,1,0:T(8,128)(2,1)S(1)}) custom-call(s32[16]{0:T(128)S(1)} %scalars.1.refs_0_, s32[2,384]{1,0:T(2,128)S(1)} %get-tuple-element.26.refs_0_.refs_1_, bf16[256,512]{1,0:T(8,128)(2,1)S(1)} %compact.1.refs_2_, ...), custom_call_target="tpu_custom_call" | custom-call | tf_op jit(solution)/shard_map/layer/pallas_call | solution.py:577
  49.9 4.4 %collective-permute-done.5.refs_2_ = bf16[256,512]{1,0:T(8,128)(2,1)S(1)} collective-permute-done((bf16[256,512]{1,0:T(8,128)(2,1)S(1)}, bf16[256,512]{1,0:T(8,128)(2,1)S(1)}, u32[]{:S(2)}, u32[]{:S(2)}) %collective-permute-start.5) | collective-permute-done | bytes 262176 | tf_op jit(solution)/shard_map/ppermute | solution.py:761
  54.3 5.7 %layer.5 = (bf16[8,256,512]{2,1,0:T(8,128)(2,1)}, bf16[256,512]{1,0:T(8,128)(2,1)S(1)}) custom-call(s32[16]{0:T(128)S(1)} %scalars.1.refs_0_, s32[2,384]{1,0:T(2,128)S(1)} %collective-permute-done.refs_1_, bf16[256,512]{1,0:T(8,128)(2,1)S(1)} %collective-permute-done.5.refs_2_, bf16[8,256,512]{2,1,0:T(8,128)(2,1)S(1)} %copy-done, ...), custom_call_target="tpu_custom_call", output_to_operand_aliasing={{0}: (10, {})} | custom-call | tf_op jit(solution)/shard_map/layer/pallas_call | solution.py:577
  60.0 0.0 collective-permute-done.4.refs_4_
  60.0 0.0 collective-permute-done.3.refs_3_
  60.1 14.7 %layer.6 = (bf16[8,256,512]{2,1,0:T(8,128)(2,1)}, bf16[256,512]{1,0:T(8,128)(2,1)S(1)}, bf16[256,512]{1,0:T(8,128)(2,1)S(1)}) custom-call(s32[16]{0:T(128)S(1)} %scalars.1.refs_0_, s32[2,384]{1,0:T(2,128)S(1)} %collective-permute-done.2.refs_3_.refs_1_, s32[2,384]{1,0:T(2,128)S(1)} %collective-permute-done.1.refs_2_, ...), custom_call_target="tpu_custom_call", output_to_operand_aliasing={{0}: (12, {})} | custom-call | tf_op jit(solution)/shard_map/layer/pallas_call | solution.py:577
  74.7 0.1 collective-permute-start.7
  74.8 3.5 %collective-permute-start.8 = (bf16[256,512]{1,0:T(8,128)(2,1)S(1)}, bf16[256,512]{1,0:T(8,128)(2,1)S(1)}, u32[]{:S(2)}, u32[]{:S(2)}) collective-permute-start(bf16[256,512]{1,0:T(8,128)(2,1)S(1)} %get-tuple-element.46), channel_id=1, source_target_pairs={{0,2},{1,3},{2,0},{3,1},{4,6},{5,7},{6,4},{7,5},{8,10},{9,11},{10,... | collective-permute-start | bytes 786440 | tf_op jit(solution)/shard_map/ppermute | solution.py:785
  78.3 0.0 collective-permute-start.6
  78.3 5.2 %layer.7 = (bf16[8,256,512]{2,1,0:T(8,128)(2,1)}, bf16[256,512]{1,0:T(8,128)(2,1)S(1)}) custom-call(s32[16]{0:T(128)S(1)} %scalars.1.refs_0_, s32[2,384]{1,0:T(2,128)S(1)} %get-tuple-element.26.refs_0_.refs_1_, bf16[256,512]{1,0:T(8,128)(2,1)S(1)} %compact.1.refs_2_, bf16[8,256,512]{2,1,0:T(8,128)(2,1)S(1)} %copy-done, ...), custom_call_target="tpu_custom_call", output_to_operand_aliasing={{0}: (10, {})} | custom-call | tf_op jit(solution)/shard_map/layer/pallas_call | solution.py:577
  83.6 0.0 collective-permute-done.7.refs_2_
  83.6 3.5 %collective-permute-done.8.refs_3_ = bf16[256,512]{1,0:T(8,128)(2,1)S(1)} collective-permute-done((bf16[256,512]{1,0:T(8,128)(2,1)S(1)}, bf16[256,512]{1,0:T(8,128)(2,1)S(1)}, u32[]{:S(2)}, u32[]{:S(2)}) %collective-permute-start.8) | collective-permute-done | bytes 262176 | tf_op jit(solution)/shard_map/ppermute | solution.py:785
  87.1 0.0 collective-permute-done.6.refs_1_
  87.1 1.3 %expand.1 = bf16[1024,256]{1,0:T(8,128)(2,1)} custom-call(s32[1,256]{1,0:T(1,128)S(1)} %get-tuple-element.31.pos_ref, bf16[256,512]{1,0:T(8,128)(2,1)S(1)} %get-tuple-element.43.refs_0_, bf16[256,512]{1,0:T(8,128)(2,1)S(1)} %collective-permute-done.6.refs_1_, bf16[256,512]{1,0:T(8,128)(2,1)S(1)} %collective-permute-done.7.refs_2_, ...), custom_call_target="tpu_custom_call" | custom-call | tf_op jit(solution)/shard_map/expand/pallas_call | solution.py:654
  88.4 9.7 %all-to-all-start.2 = ((bf16[128,8,256]{2,1,0:T(8,128)(2,1)}), bf16[128,8,256]{2,1,0:T(8,128)(2,1)S(1)}, u32[]{:S(2)}, u32[]{:S(2)}) async-start(bf16[128,8,256]{2,1,0:T(8,128)(2,1)} %bitcast.10), calls=%async_computation.2 | async-start | bytes 1048576 | tf_op jit(solution)/shard_map/all_to_all | solution.py:727
  98.1 0.2 asked_line.1.line_ref
  98.3 13.7 %all-to-all-done.2 = bf16[128,8,256]{2,1,0:T(8,128)(2,1)S(1)} async-done(((bf16[128,8,256]{2,1,0:T(8,128)(2,1)}), bf16[128,8,256]{2,1,0:T(8,128)(2,1)S(1)}, u32[]{:S(2)}, u32[]{:S(2)}) %all-to-all-start.2) | async-done | bytes 524320 | tf_op jit(solution)/shard_map/all_to_all | solution.py:727
  112.0 1.7 %scatter.1 = f32[1024,512]{1,0:T(8,128)} custom-call(s32[1,512]{1,0:T(1,128)S(1)} %asked_line.1.line_ref, bf16[1024,256]{1,0:T(8,128)(2,1)S(1)} %bitcast.14), custom_call_target="tpu_custom_call" | custom-call | tf_op jit(solution)/shard_map/scatter/pallas_call | solution.py:707
Async XLA Ops:
  0.6 34.5 %copy-start.4 = (f32[4,256]{1,0:T(4,128)S(1)}, f32[4,256]{1,0:T(4,128)}, u32[]{:S(2)}) copy-start(f32[4,256]{1,0:T(4,128)} %param.22) | copy-start | bytes 12292
  25.8 21.8 %copy-start = (bf16[8,256,512]{2,1,0:T(8,128)(2,1)S(1)}, bf16[8,256,512]{2,1,0:T(8,128)(2,1)}, u32[]{:S(2)}) copy-start(bf16[8,256,512]{2,1,0:T(8,128)(2,1)} %refs_3_.5) | copy-start | bytes 6291460
  25.8 21.8 %copy-start.1 = (f32[2048]{0:T(1024)S(1)}, f32[2048]{0:T(1024)}, u32[]{:S(2)}) copy-start(f32[2048]{0:T(1024)} %param.18) | copy-start | bytes 24580
  25.8 21.7 %copy-start.2 = (f32[512]{0:T(512)S(1)}, f32[512]{0:T(512)}, u32[]{:S(2)}) copy-start(f32[512]{0:T(512)} %param.19) | copy-start | bytes 6148
  25.9 21.7 %copy-start.3 = (f32[512]{0:T(512)S(1)}, f32[512]{0:T(512)}, u32[]{:S(2)}) copy-start(f32[512]{0:T(512)} %param.20) | copy-start | bytes 6148
  25.9 18.4 %all-to-all-start.1 = ((bf16[128,8,256]{2,1,0:T(8,128)(2,1)}), bf16[128,8,256]{2,1,0:T(8,128)(2,1)S(1)}, u32[]{:S(2)}, u32[]{:S(2)}) async-start(bf16[128,8,256]{2,1,0:T(8,128)(2,1)} %bitcast.5), calls=%async_computation.1 | async-start | bytes 1048576 | tf_op jit(solution)/shard_map/all_to_all | solution.py:727
  30.1 8.8 %collective-permute-start = (s32[2,384]{1,0:T(2,128)S(1)}, s32[2,384]{1,0:T(2,128)S(1)}, u32[]{:S(2)}, u32[]{:S(2)}) collective-permute-start(s32[2,384]{1,0:T(2,128)S(1)} %get-tuple-element.27), channel_id=1, source_target_pairs={{0,1},{1,2},{2,3},{3,0},{4,5},{5,6},{6,7},{7,4},{8,9},{9,10},{10,1... | collective-permute-start | bytes 9224 | tf_op jit(solution)/shard_map/ppermute | solution.py:751
  31.6 7.4 %collective-permute-start.1 = (s32[2,384]{1,0:T(2,128)S(1)}, s32[2,384]{1,0:T(2,128)S(1)}, u32[]{:S(2)}, u32[]{:S(2)}) collective-permute-start(s32[2,384]{1,0:T(2,128)S(1)} %get-tuple-element.28), channel_id=1, source_target_pairs={{0,2},{1,3},{2,0},{3,1},{4,6},{5,7},{6,4},{7,5},{8,10},{9,11},{10,... | collective-permute-start | bytes 9224 | tf_op jit(solution)/shard_map/ppermute | solution.py:751
  34.0 5.0 %collective-permute-start.2 = (s32[2,384]{1,0:T(2,128)S(1)}, s32[2,384]{1,0:T(2,128)S(1)}, u32[]{:S(2)}, u32[]{:S(2)}) collective-permute-start(s32[2,384]{1,0:T(2,128)S(1)} %get-tuple-element.29), channel_id=1, source_target_pairs={{0,3},{1,0},{2,1},{3,2},{4,7},{5,4},{6,5},{7,6},{8,11},{9,8},{10,9... | collective-permute-start | bytes 9224 | tf_op jit(solution)/shard_map/ppermute | solution.py:751
  44.7 9.6 %collective-permute-start.5 = (bf16[256,512]{1,0:T(8,128)(2,1)S(1)}, bf16[256,512]{1,0:T(8,128)(2,1)S(1)}, u32[]{:S(2)}, u32[]{:S(2)}) collective-permute-start(bf16[256,512]{1,0:T(8,128)(2,1)S(1)} %compact.1.refs_2_), channel_id=1, source_target_pairs={{0,1},{1,2},{2,3},{3,0},{4,5},{5,6},{6,7},{7,4},{8,9},{9,10},{10,1... | collective-permute-start | bytes 786440 | tf_op jit(solution)/shard_map/ppermute | solution.py:761
  45.1 14.9 %collective-permute-start.4 = (bf16[256,512]{1,0:T(8,128)(2,1)S(1)}, bf16[256,512]{1,0:T(8,128)(2,1)S(1)}, u32[]{:S(2)}, u32[]{:S(2)}) collective-permute-start(bf16[256,512]{1,0:T(8,128)(2,1)S(1)} %compact.1.refs_2_), channel_id=1, source_target_pairs={{0,2},{1,3},{2,0},{3,1},{4,6},{5,7},{6,4},{7,5},{8,10},{9,11},{10,... | collective-permute-start | bytes 786440 | tf_op jit(solution)/shard_map/ppermute | solution.py:761
  46.9 13.1 %collective-permute-start.3 = (bf16[256,512]{1,0:T(8,128)(2,1)S(1)}, bf16[256,512]{1,0:T(8,128)(2,1)S(1)}, u32[]{:S(2)}, u32[]{:S(2)}) collective-permute-start(bf16[256,512]{1,0:T(8,128)(2,1)S(1)} %compact.1.refs_2_), channel_id=1, source_target_pairs={{0,3},{1,0},{2,1},{3,2},{4,7},{5,4},{6,5},{7,6},{8,11},{9,8},{10,9... | collective-permute-start | bytes 786440 | tf_op jit(solution)/shard_map/ppermute | solution.py:761
  74.7 8.8 %collective-permute-start.7 = (bf16[256,512]{1,0:T(8,128)(2,1)S(1)}, bf16[256,512]{1,0:T(8,128)(2,1)S(1)}, u32[]{:S(2)}, u32[]{:S(2)}) collective-permute-start(bf16[256,512]{1,0:T(8,128)(2,1)S(1)} %get-tuple-element.45), channel_id=1, source_target_pairs={{0,1},{1,2},{2,3},{3,0},{4,5},{5,6},{6,7},{7,4},{8,9},{9,10},{10,1... | collective-permute-start | bytes 786440 | tf_op jit(solution)/shard_map/ppermute | solution.py:785
  74.8 12.3 %collective-permute-start.8 = (bf16[256,512]{1,0:T(8,128)(2,1)S(1)}, bf16[256,512]{1,0:T(8,128)(2,1)S(1)}, u32[]{:S(2)}, u32[]{:S(2)}) collective-permute-start(bf16[256,512]{1,0:T(8,128)(2,1)S(1)} %get-tuple-element.46), channel_id=1, source_target_pairs={{0,2},{1,3},{2,0},{3,1},{4,6},{5,7},{6,4},{7,5},{8,10},{9,11},{10,... | collective-permute-start | bytes 786440 | tf_op jit(solution)/shard_map/ppermute | solution.py:785
  78.3 8.8 %collective-permute-start.6 = (bf16[256,512]{1,0:T(8,128)(2,1)S(1)}, bf16[256,512]{1,0:T(8,128)(2,1)S(1)}, u32[]{:S(2)}, u32[]{:S(2)}) collective-permute-start(bf16[256,512]{1,0:T(8,128)(2,1)S(1)} %get-tuple-element.44), channel_id=1, source_target_pairs={{0,3},{1,0},{2,1},{3,2},{4,7},{5,4},{6,5},{7,6},{8,11},{9,8},{10,9... | collective-permute-start | bytes 786440 | tf_op jit(solution)/shard_map/ppermute | solution.py:785
  88.4 23.6 %all-to-all-start.2 = ((bf16[128,8,256]{2,1,0:T(8,128)(2,1)}), bf16[128,8,256]{2,1,0:T(8,128)(2,1)S(1)}, u32[]{:S(2)}, u32[]{:S(2)}) async-start(bf16[128,8,256]{2,1,0:T(8,128)(2,1)} %bitcast.10), calls=%async_computation.2 | async-start | bytes 1048576 | tf_op jit(solution)/shard_map/all_to_all | solution.py:727
